TPU v7x, 32 devices: a whole 2x2x4 slice. The times are simulated.
32 devices in a mesh: dp: 2 (over core), row: 4 (over z), col: 4 (over y, x).
Axes of the slice: x: 2, y: 2, z: 4, core: 2. Of those that a mesh axis runs over, the one named last changes fastest.
Arguments:
- tokens: bfloat16 [2, 512, 8192], P(None, 'col', ('dp', 'row')), may hold values from -6 to 6
- cotangent: bfloat16 [2, 512, 8192], P(None, 'col', ('dp', 'row')), may hold values from -6 to 6
- piece_starts: int32 [2, 8, 2], P(None, ('dp', 'col')), may hold values from 0 to 768, as said below
- ln1_gain: bfloat16 [512], P('col'), may hold values from 0.5 to 1.5
- ln1_bias: bfloat16 [512], P('col'), may hold values from -1 to 1
- qkv_weight: bfloat16 [512, 1536], P('col', 'row'), may hold values from -0.25 to 0.25
- content_bias: float32 [8, 64], P('row'), may hold values from -3 to 3
- position_bias: float32 [8, 64], P('row'), may hold values from -3 to 3
- pos_weight: bfloat16 [512, 512], P('col', 'row'), may hold values from -0.25 to 0.25
- out_weight: bfloat16 [512, 512], P('row', 'col'), may hold values from -2 to 2
- ln2_gain: bfloat16 [512], P('col'), may hold values from 0.5 to 1.5
- ln2_bias: bfloat16 [512], P('col'), may hold values from -1 to 1
- up_weight: bfloat16 [512, 2048], P('col', 'row'), may hold values from -0.25 to 0.25
- up_bias: bfloat16 [2048], P('row'), may hold values from -3 to 3
- down_weight: bfloat16 [2048, 512], P('row', 'col'), may hold values from -0.125 to 0.125
- down_bias: bfloat16 [512], P('col'), may hold values from -1 to 1
Outputs:
- output: float32 [2, 512, 8192], P(None, 'col', ('dp', 'row'))
- grad_tokens: float32 [2, 512, 8192], P(None, 'col', ('dp', 'row'))
- grad_ln1_gain: float32 [512], P(('row', 'col', 'dp'))
- grad_ln1_bias: float32 [512], P(('row', 'col', 'dp'))
- grad_qkv_weight: float32 [512, 1536], P('col', ('row', 'dp'))
- grad_content_bias: float32 [8, 64], P('row', ('col', 'dp'))
- grad_position_bias: float32 [8, 64], P('row', ('col', 'dp'))
- grad_pos_weight: float32 [512, 512], P('col', ('row', 'dp'))
- grad_out_weight: float32 [512, 512], P('row', ('col', 'dp'))
- grad_ln2_gain: float32 [512], P(('row', 'col', 'dp'))
- grad_ln2_bias: float32 [512], P(('row', 'col', 'dp'))
- grad_up_weight: float32 [512, 2048], P('col', ('row', 'dp'))
- grad_up_bias: float32 [2048], P(('row', 'col', 'dp'))
- grad_down_weight: float32 [2048, 512], P('row', ('col', 'dp'))
- grad_down_bias: float32 [512], P(('row', 'col', 'dp'))
Inputs may be any that keep to these rules, and one draw needn't show every extreme that they name: `piece_starts`: for every sequence, piece p starts between p * (512) and (p + 1) * 512 - 256, so the 2 pieces of 256 positions lie inside the sequence, in order, without intersection. In every micro-batch some sequence has a piece starting at 0 and one ending at the sequence's end.
All inputs are finite; a program needn't handle non-finite values.
Results may differ from a plain program's by a relative error of at most 0.024.
Values may be sent and summed in bfloat16 or wider, within the bound.
A program may use at most 192 MiB of HBM per device.

v0:
```python
from functools import reduce

import jax
import jax.numpy as jnp
from jax import lax
from jax.sharding import PartitionSpec as P

D = 512
SEQ_LEN = 1024
PIECE = 256


norm_epsilon = 1e-05
big_negative = -1e30
inv_sqrt_two = 0.7071067811865476
inv_sqrt_tau = 0.3989422804014327


def contract(left_op, right_op, flipped):
    if flipped:
        return lax.dot_general(
            left_op, right_op, (((1,), (1,)), ((), ())), preferred_element_type=jnp.float32
        )
    return jnp.dot(left_op, right_op, preferred_element_type=jnp.float32)


def outer_sum(left_op, right_op):
    return lax.dot_general(
        left_op, right_op, (((0,), (0,)), ((), ())), preferred_element_type=jnp.float32
    )


def gather_rows(values):
    return lax.all_gather(values, "row", axis=0, tiled=True)


def gather_cols(values):
    return lax.all_gather(values, "col", axis=0, tiled=True)


def sum_over_cols(gathered, weight, flipped):
    share_rows = gathered.shape[0] // lax.axis_size("col")

    def partial_term(offset, amount):
        return contract(gathered, weight, flipped)

    return lax.psum_scatter(
        partial_term(jnp.int32(0), lax.axis_size("col") * share_rows),
        "col",
        scatter_dimension=0,
        tiled=True,
    )


def sum_over_rows(gathered, weight, flipped):
    share_rows = gathered.shape[0] // lax.axis_size("row")

    def partial_term(offset, amount):
        return contract(gathered, weight, flipped)

    return lax.psum_scatter(
        partial_term(jnp.int32(0), lax.axis_size("row") * share_rows),
        "row",
        scatter_dimension=0,
        tiled=True,
    )


def feature_sums(first_sum, second_sum):
    return lax.psum((first_sum, second_sum), "col")


def normalize(values, gain, bias):
    feature_count = values.shape[1] * lax.axis_size("col")
    total_row, square_row = feature_sums(jnp.sum(values, axis=1), jnp.sum(values * values, axis=1))
    mean_row = total_row / feature_count
    inverse = lax.rsqrt(square_row / feature_count - mean_row * mean_row + norm_epsilon)
    scaled = (values - mean_row[:, None]) * inverse[:, None]
    return (scaled * gain + bias, scaled, inverse)


def normalize_back(grad_in, scaled, inverse, gain):
    feature_count = grad_in.shape[1] * lax.axis_size("col")
    shifted = grad_in * gain
    first_sum, second_sum = feature_sums(
        jnp.sum(shifted, axis=1), jnp.sum(shifted * scaled, axis=1)
    )
    back_rows = inverse[:, None] * (
        shifted - first_sum[:, None] / feature_count - scaled * second_sum[:, None] / feature_count
    )
    return (back_rows, jnp.sum(grad_in * scaled, axis=0), jnp.sum(grad_in, axis=0))


def gelu_exact(values):
    return 0.5 * values * (1.0 + jax.scipy.special.erf(values * inv_sqrt_two))


def gelu_slope(values):
    return (
        0.5 * (1.0 + jax.scipy.special.erf(values * inv_sqrt_two))
        + values * jnp.exp(-0.5 * values * values) * inv_sqrt_tau
    )


def sinusoid_table(seq_len, feature_count):
    offsets = jnp.arange(2 * seq_len - 1, dtype=jnp.float32) - (seq_len - 1)
    frequency = 10000.0 ** (-jnp.arange(0, feature_count, 2, dtype=jnp.float32) / feature_count)
    angles = offsets[:, None] * frequency[None, :]
    return jnp.concatenate([jnp.sin(angles), jnp.cos(angles)], axis=1).astype(jnp.bfloat16)


def piece_labels(positions, starts, piece_len):
    inside = (positions[:, None] >= starts[None, :]) & (
        positions[:, None] < starts[None, :] + piece_len
    )
    numbers = jnp.arange(1, starts.shape[0] + 1, dtype=jnp.int32)
    return jnp.sum(jnp.where(inside, numbers[None, :], 0), axis=1) - 1


def block_mask(offset, block_len, labels):
    positions = jnp.arange(labels.shape[0], dtype=jnp.int32)
    row_pos = offset + jnp.arange(block_len, dtype=jnp.int32)
    row_labels = lax.dynamic_slice_in_dim(labels, offset, block_len, 0)
    same_piece = (row_labels[:, None] == labels[None, :]) & (row_labels[:, None] >= 0)
    return (positions[None, :] <= row_pos[:, None]) | same_piece


def skew_rows(unshifted_reversed_scores, key_total):
    head_total, row_total, rel_span = unshifted_reversed_scores.shape
    flattened = unshifted_reversed_scores.reshape(head_total, row_total * rel_span)
    window = lax.slice_in_dim(
        flattened, row_total - 1, row_total - 1 + row_total * (rel_span - 1), axis=1
    )
    return window.reshape(head_total, row_total, rel_span - 1)[:, :, :key_total]


def unskew_rows(grad_pos, rel_span):
    head_total, row_total, key_total = grad_pos.shape
    padded = jnp.pad(grad_pos, ((0, 0), (0, 0), (0, rel_span - 1 - key_total)))
    flattened = padded.reshape(head_total, row_total * (rel_span - 1))
    flattened = jnp.pad(flattened, ((0, 0), (row_total - 1, 1)))
    return flattened.reshape(head_total, row_total, rel_span)


def block_scores(qu_block, query_position_block, key_rows, relative_block, allowed):
    content = jnp.einsum("ihd,jhd->hij", qu_block, key_rows, preferred_element_type=jnp.float32)
    unshifted_reversed_scores = jnp.einsum(
        "sgw,egw->gse", query_position_block, relative_block, preferred_element_type=jnp.float32
    )
    position = skew_rows(unshifted_reversed_scores, key_rows.shape[0])
    return jnp.where(allowed[None], content + position, big_negative)


def attention_forward(query_u, query_v, key_rows, value_rows, relative_rev, labels):
    seq_len, head_count, head_dim = key_rows.shape
    block_len = min(512, seq_len)
    rel_span = block_len + seq_len - 1
    offsets = jnp.arange(seq_len // block_len, dtype=jnp.int32) * block_len

    def attend(offset):
        qu_block = lax.dynamic_slice_in_dim(query_u, offset, block_len, 0)
        query_position_block = lax.dynamic_slice_in_dim(query_v, offset, block_len, 0)
        relative_block = lax.dynamic_slice_in_dim(
            relative_rev, seq_len - block_len - offset, rel_span, 0
        )
        scores = block_scores(
            qu_block,
            query_position_block,
            key_rows,
            relative_block,
            block_mask(offset, block_len, labels),
        )
        row_max = jnp.max(scores, axis=2, keepdims=True)
        log_total = row_max + jnp.log(jnp.sum(jnp.exp(scores - row_max), axis=2, keepdims=True))
        attn_prob = jnp.exp(scores - log_total).astype(jnp.bfloat16)
        result = jnp.einsum(
            "hij,jhd->ihd", attn_prob, value_rows, preferred_element_type=jnp.float32
        )
        return (result, log_total[:, :, 0])

    results, log_totals = lax.map(attend, offsets)
    return (results.reshape(seq_len, head_count * head_dim), log_totals)


def attention_backward(
    query_u, query_v, key_rows, value_rows, relative_rev, labels, log_totals, grad_att
):
    seq_len, head_count, head_dim = key_rows.shape
    block_len = min(512, seq_len)
    rel_span = block_len + seq_len - 1
    offsets = jnp.arange(seq_len // block_len, dtype=jnp.int32) * block_len

    def back_block(carried, sliced):
        grad_keys, grad_values, grad_rel = carried
        offset, log_total = sliced
        rel_start = seq_len - block_len - offset
        qu_block = lax.dynamic_slice_in_dim(query_u, offset, block_len, 0)
        query_position_block = lax.dynamic_slice_in_dim(query_v, offset, block_len, 0)
        relative_block = lax.dynamic_slice_in_dim(relative_rev, rel_start, rel_span, 0)
        scores = block_scores(
            qu_block,
            query_position_block,
            key_rows,
            relative_block,
            block_mask(offset, block_len, labels),
        )
        attn_prob = jnp.exp(scores - log_total[:, :, None])
        low_prob = attn_prob.astype(jnp.bfloat16)
        grad_block = lax.dynamic_slice_in_dim(grad_att, offset, block_len, 0)
        grad_prob = jnp.einsum(
            "ihd,jhd->hij", grad_block, value_rows, preferred_element_type=jnp.float32
        )
        row_inner = jnp.sum(attn_prob * grad_prob, axis=2, keepdims=True)
        grad_scores = (attn_prob * (grad_prob - row_inner)).astype(jnp.bfloat16)
        grad_values = grad_values + jnp.einsum(
            "hij,ihd->jhd", low_prob, grad_block, preferred_element_type=jnp.float32
        )
        grad_keys = grad_keys + jnp.einsum(
            "hij,ihd->jhd", grad_scores, qu_block, preferred_element_type=jnp.float32
        )
        grad_qu = jnp.einsum(
            "hij,jhd->ihd", grad_scores, key_rows, preferred_element_type=jnp.float32
        )
        gradient_unshifted = unskew_rows(grad_scores, rel_span)
        grad_qv = jnp.einsum(
            "qjp,pqr->jqr", gradient_unshifted, relative_block, preferred_element_type=jnp.float32
        )
        rel_part = jnp.einsum(
            "nfx,fne->xne",
            gradient_unshifted,
            query_position_block,
            preferred_element_type=jnp.float32,
        )
        current = lax.dynamic_slice_in_dim(grad_rel, rel_start, rel_span, 0)
        grad_rel = lax.dynamic_update_slice_in_dim(grad_rel, current + rel_part, rel_start, 0)
        return ((grad_keys, grad_values, grad_rel), (grad_qu, grad_qv))

    zero_rows = jnp.zeros((seq_len, head_count, head_dim), jnp.float32)
    zero_rel = jnp.zeros((2 * seq_len - 1, head_count, head_dim), jnp.float32)
    carried, stacked = lax.scan(back_block, (zero_rows, zero_rows, zero_rel), (offsets, log_totals))
    grad_keys, grad_values, grad_rel = carried
    grad_qu = stacked[0].reshape(seq_len, head_count, head_dim)
    grad_qv = stacked[1].reshape(seq_len, head_count, head_dim)
    return (grad_qu, grad_qv, grad_keys, grad_values, grad_rel)


def heads_pass(packed, content_bias, position_bias, relative_rev, labels):
    seq_len = packed.shape[0]
    head_count, head_dim = content_bias.shape
    scaling = head_dim ** (-0.5)
    packed = packed.reshape(seq_len, head_count, 3, head_dim)
    queries = packed[:, :, 0].astype(jnp.float32)
    key_rows = packed[:, :, 1]
    value_rows = packed[:, :, 2]
    query_u = ((queries + content_bias) * scaling).astype(jnp.bfloat16)
    query_v = ((queries + position_bias) * scaling).astype(jnp.bfloat16)
    attended, log_totals = attention_forward(
        query_u, query_v, key_rows, value_rows, relative_rev, labels
    )
    return (attended.astype(jnp.bfloat16), (query_u, query_v, key_rows, value_rows, log_totals))


def heads_back(kept, relative_rev, labels, grad_att):
    query_u, query_v, key_rows, value_rows, log_totals = kept
    seq_len, head_count, head_dim = key_rows.shape
    scaling = head_dim ** (-0.5)
    grad_att = grad_att.reshape(seq_len, head_count, head_dim)
    grad_qu, grad_qv, grad_keys, grad_values, grad_rel = attention_backward(
        query_u, query_v, key_rows, value_rows, relative_rev, labels, log_totals, grad_att
    )
    cbias_part = jnp.sum(grad_qu, axis=0) * scaling
    pbias_part = jnp.sum(grad_qv, axis=0) * scaling
    grad_query = (grad_qu + grad_qv) * scaling
    grad_packed = jnp.stack([grad_query, grad_keys, grad_values], axis=2)
    grad_packed = grad_packed.reshape(seq_len, head_count * 3 * head_dim).astype(jnp.bfloat16)
    rel_low = grad_rel.reshape(2 * seq_len - 1, head_count * head_dim).astype(jnp.bfloat16)
    return (grad_packed, rel_low, cbias_part, pbias_part)


def grid_micro(seq_feats, cot_feats, params, shared):
    (
        ln1_gain,
        ln1_bias,
        qkv_weight,
        content_bias,
        position_bias,
        out_weight,
        ln2_gain,
        ln2_bias,
        up_weight,
        up_bias,
        down_weight,
        down_bias,
    ) = params
    relative_rev, table_rev, labels = shared
    seq_in = seq_feats.astype(jnp.float32).T
    normed_one, scaled_one, inverse_one = normalize(seq_in, ln1_gain, ln1_bias)
    gathered_one = gather_rows(normed_one.astype(jnp.bfloat16))
    packed = sum_over_cols(gathered_one, qkv_weight, False).astype(jnp.bfloat16)
    attended, kept = heads_pass(packed, content_bias, position_bias, relative_rev, labels)
    att_gathered = gather_cols(attended)
    middle = seq_in + sum_over_rows(att_gathered, out_weight, False)
    normed_two, scaled_two, inverse_two = normalize(middle, ln2_gain, ln2_bias)
    gathered_two = gather_rows(normed_two.astype(jnp.bfloat16))
    pre_act = sum_over_cols(gathered_two, up_weight, False) + up_bias
    activated = gelu_exact(pre_act).astype(jnp.bfloat16)
    act_gathered = gather_cols(activated)
    output = middle + sum_over_rows(act_gathered, down_weight, False) + down_bias
    grad_final = cot_feats.T
    gout = grad_final.astype(jnp.float32)
    final_gathered = gather_rows(grad_final)
    grad_act = sum_over_cols(final_gathered, down_weight, True)
    grad_pre = (grad_act * gelu_slope(pre_act)).astype(jnp.bfloat16)
    pre_gathered = gather_cols(grad_pre)
    grad_two = sum_over_rows(pre_gathered, up_weight, True)
    backward_second, gain_two, bias_two = normalize_back(
        grad_two, scaled_two, inverse_two, ln2_gain
    )
    grad_middle = gout + backward_second
    grad_branch = grad_middle.astype(jnp.bfloat16)
    branch_gathered = gather_rows(grad_branch)
    grad_att = sum_over_cols(branch_gathered, out_weight, True).astype(jnp.bfloat16)
    grad_packed, rel_low, cbias_part, pbias_part = heads_back(kept, relative_rev, labels, grad_att)
    packed_gathered = gather_cols(grad_packed)
    grad_one = sum_over_rows(packed_gathered, qkv_weight, True)
    back_one, gain_one, bias_one = normalize_back(grad_one, scaled_one, inverse_one, ln1_gain)
    grad_in = grad_middle + back_one
    collected = (
        outer_sum(gathered_one, packed_gathered),
        outer_sum(att_gathered, branch_gathered),
        outer_sum(gathered_two, pre_gathered),
        outer_sum(act_gathered, final_gathered),
        outer_sum(table_rev, rel_low),
        cbias_part,
        pbias_part,
        jnp.sum(grad_pre.astype(jnp.float32), axis=0),
        gain_one,
        bias_one,
        gain_two,
        bias_two,
        jnp.sum(gout, axis=0),
    )
    return (output.T, grad_in.T, collected)


def embed_heads(part, row_pick, col_count):
    head_count = part.shape[0]
    spread = jnp.transpose(part.reshape(head_count, col_count, -1), (1, 0, 2))
    placed = jnp.where(row_pick[:, None, None, None], spread[None], 0.0)
    return placed.reshape(row_pick.shape[0] * col_count, head_count, -1)


def shards(
    tokens,
    cotangent,
    piece_starts,
    ln1_gain,
    ln1_bias,
    qkv_weight,
    content_bias,
    position_bias,
    pos_weight,
    out_weight,
    ln2_gain,
    ln2_bias,
    up_weight,
    up_bias,
    down_weight,
    down_bias,
):
    micro_count = tokens.shape[0]
    row_count = lax.axis_size("row")
    col_count = lax.axis_size("col")
    grid_cells = row_count * col_count
    head_count, head_dim = content_bias.shape
    pos_cols = lax.all_gather(pos_weight, "col", axis=0, tiled=True)
    table_rev = sinusoid_table(SEQ_LEN, D)[::-1]
    relative_rev = jnp.dot(table_rev, pos_cols, preferred_element_type=jnp.float32).astype(
        jnp.bfloat16
    )
    relative_rev = relative_rev.reshape(2 * SEQ_LEN - 1, head_count, head_dim)
    positions = jnp.arange(SEQ_LEN, dtype=jnp.int32)
    params = (
        ln1_gain,
        ln1_bias,
        qkv_weight,
        content_bias,
        position_bias,
        out_weight,
        ln2_gain,
        ln2_bias,
        up_weight,
        up_bias,
        down_weight,
        down_bias,
    )
    outputs, grad_inputs, part_lists = ([], [], [])
    for micro_idx in range(micro_count):
        labels = piece_labels(positions, piece_starts[micro_idx, 0], PIECE)
        out_feats, grad_feats, collected = grid_micro(
            tokens[micro_idx], cotangent[micro_idx], params, (relative_rev, table_rev, labels)
        )
        outputs.append(out_feats)
        grad_inputs.append(grad_feats)
        part_lists.append(collected)
    totals = [
        reduce(jnp.add, [collected[member] for collected in part_lists]) for member in range(13)
    ]
    (
        acc_qkv,
        acc_out,
        acc_up,
        acc_down,
        acc_pos,
        acc_cbias,
        acc_pbias,
        acc_ubias,
        acc_g1,
        acc_b1,
        acc_g2,
        acc_b2,
        acc_db,
    ) = totals
    row_pick = jnp.arange(row_count, dtype=jnp.int32) == lax.axis_index("row")
    pos_term = jnp.where(row_pick[:, None, None], acc_pos[None], 0.0).reshape(
        row_count * acc_pos.shape[0], -1
    )
    cbias_term = embed_heads(acc_cbias, row_pick, col_count)
    pbias_term = embed_heads(acc_pbias, row_pick, col_count)
    col_pick = jnp.arange(col_count, dtype=jnp.int32) == lax.axis_index("col")
    ubias_term = jnp.where(row_pick[:, None], acc_ubias[None], 0.0).reshape(grid_cells, -1)
    norm_terms = [
        jnp.where(col_pick[:, None], vector[None], 0.0).reshape(grid_cells, -1)
        for vector in (acc_g1, acc_b1, acc_g2, acc_b2, acc_db)
    ]
    sum_pos, sum_cbias, sum_pbias, sum_ubias, sum_g1, sum_b1, sum_g2, second_bias_total, sum_db = (
        lax.psum_scatter(pos_term, ("row", "col"), scatter_dimension=0, tiled=True),
        lax.psum_scatter(cbias_term, ("row", "col"), scatter_dimension=0, tiled=True),
        lax.psum_scatter(pbias_term, ("row", "col"), scatter_dimension=0, tiled=True),
        lax.psum_scatter(ubias_term, ("row", "col"), scatter_dimension=0, tiled=True),
        lax.psum_scatter(norm_terms[0], ("row", "col"), scatter_dimension=0, tiled=True),
        lax.psum_scatter(norm_terms[1], ("row", "col"), scatter_dimension=0, tiled=True),
        lax.psum_scatter(norm_terms[2], ("row", "col"), scatter_dimension=0, tiled=True),
        lax.psum_scatter(norm_terms[3], ("row", "col"), scatter_dimension=0, tiled=True),
        lax.psum_scatter(norm_terms[4], ("row", "col"), scatter_dimension=0, tiled=True),
    )
    sum_qkv, sum_out, sum_up, sum_down = (acc_qkv, acc_out, acc_up, acc_down)
    summed = (
        lax.psum_scatter(
            sum_qkv.astype(jnp.bfloat16), "dp", scatter_dimension=1, tiled=True
        ).astype(jnp.float32),
        lax.psum_scatter(
            sum_out.astype(jnp.bfloat16), "dp", scatter_dimension=1, tiled=True
        ).astype(jnp.float32),
        lax.psum_scatter(sum_up.astype(jnp.bfloat16), "dp", scatter_dimension=1, tiled=True).astype(
            jnp.float32
        ),
        lax.psum_scatter(
            sum_down.astype(jnp.bfloat16), "dp", scatter_dimension=1, tiled=True
        ).astype(jnp.float32),
        lax.psum_scatter(
            sum_pos.astype(jnp.bfloat16), "dp", scatter_dimension=1, tiled=True
        ).astype(jnp.float32),
        lax.psum_scatter(
            sum_cbias.astype(jnp.bfloat16), "dp", scatter_dimension=2, tiled=True
        ).astype(jnp.float32),
        lax.psum_scatter(
            sum_pbias.astype(jnp.bfloat16), "dp", scatter_dimension=2, tiled=True
        ).astype(jnp.float32),
        lax.psum_scatter(
            sum_ubias.astype(jnp.bfloat16), "dp", scatter_dimension=1, tiled=True
        ).astype(jnp.float32),
        lax.psum_scatter(sum_g1.astype(jnp.bfloat16), "dp", scatter_dimension=1, tiled=True).astype(
            jnp.float32
        ),
        lax.psum_scatter(sum_b1.astype(jnp.bfloat16), "dp", scatter_dimension=1, tiled=True).astype(
            jnp.float32
        ),
        lax.psum_scatter(sum_g2.astype(jnp.bfloat16), "dp", scatter_dimension=1, tiled=True).astype(
            jnp.float32
        ),
        lax.psum_scatter(
            second_bias_total.astype(jnp.bfloat16), "dp", scatter_dimension=1, tiled=True
        ).astype(jnp.float32),
        lax.psum_scatter(sum_db.astype(jnp.bfloat16), "dp", scatter_dimension=1, tiled=True).astype(
            jnp.float32
        ),
    )
    (
        grad_qkv_w,
        grad_out_w,
        grad_up_w,
        grad_down_w,
        grad_pos_w,
        grad_cbias,
        grad_pbias,
        grad_ubias,
        grad_g1,
        grad_b1,
        grad_g2,
        grad_b2,
        grad_dbias,
    ) = summed
    output_rows = jnp.stack(outputs, axis=0)
    grad_rows = jnp.stack(grad_inputs, axis=0)
    return (
        output_rows,
        grad_rows,
        grad_g1.reshape(-1),
        grad_b1.reshape(-1),
        grad_qkv_w,
        grad_cbias.reshape(head_count, -1),
        grad_pbias.reshape(head_count, -1),
        grad_pos_w,
        grad_out_w,
        grad_g2.reshape(-1),
        grad_b2.reshape(-1),
        grad_up_w,
        grad_ubias.reshape(-1),
        grad_down_w,
        grad_dbias.reshape(-1),
    )


def solution(mesh):
    in_specs = (
        P(None, "col", ("dp", "row")),
        P(None, "col", ("dp", "row")),
        P(None, ("dp", "col"), None),
        P("col"),
        P("col"),
        P("col", "row"),
        P("row", None),
        P("row", None),
        P("col", "row"),
        P("row", "col"),
        P("col"),
        P("col"),
        P("col", "row"),
        P("row"),
        P("row", "col"),
        P("col"),
    )
    out_specs = (
        P(None, "col", ("dp", "row")),
        P(None, "col", ("dp", "row")),
        P(("row", "col", "dp")),
        P(("row", "col", "dp")),
        P("col", ("row", "dp")),
        P("row", ("col", "dp")),
        P("row", ("col", "dp")),
        P("col", ("row", "dp")),
        P("row", ("col", "dp")),
        P(("row", "col", "dp")),
        P(("row", "col", "dp")),
        P("col", ("row", "dp")),
        P(("row", "col", "dp")),
        P("row", ("col", "dp")),
        P(("row", "col", "dp")),
    )
    return jax.shard_map(shards, mesh=mesh, in_specs=in_specs, out_specs=out_specs, check_vma=False)
```

profile of v0, /device:TPU:0, one launch (start us, length us, event | category | flops | bytes accessed | tf_op | source)
XLA Modules:
  0.0 2555.0 jit_solution(3032048680456831483)
XLA Ops:
  9.5 17.5 all-reduce.18
  29.8 26.7 %all-gather.17.cloned.1.call-done = bf16[4096,128]{1,0:T(8,128)(2,1)} async-done(((bf16[1024,128]{1,0:T(8,128)(2,1)}), bf16[4096,128]{1,0:T(8,128)(2,1)}) %all-gather.17.cloned.1.call-update) | async-done | bytes 1048592 | tf_op jit(solution)/shard_map/all_gather | solution.py:34
  61.4 24.7 all-gather.25.cloned.1.call-done
  102.4 26.0 %rev.3 = bf16[2047,512]{1,0:T(8,128)(2,1)S(1)} reverse(bf16[2047,512]{1,0:T(8,128)(2,1)} %pad_maximum_fusion), dimensions={0} | reverse | bytes 4192256 | tf_op jit(solution)/shard_map/rev | solution.py:377
  138.4 20.1 reduce-scatter.43.cloned.1.call-done
  162.3 69.1 %reduce-scatter.51.cloned.1.call-done = f32[1024,384]{1,0:T(8,128)} async-done(((f32[4096,384]{1,0:T(8,128)}), f32[1024,384]{1,0:T(8,128)}) %reduce-scatter.51.cloned.1.call-update) | async-done | bytes 1572880 | tf_op jit(solution)/shard_map/reduce_scatter | solution.py:47
  235.5 136.4 %while.71 = (s32[]{:T(128)}, bf16[2,512,2,64]{1,3,2,0:T(8,128)(2,1)}, f32[2,2,512]{2,1,0:T(2,128)S(1)}, s32[2]{0:T(128)}, s32[1024]{0:T(1024)S(1)}, /*index=5*/b...) while((s32[]{:T(128)}, ...), condition=%wide.region_26.27_spmd, body=%wide.region_23.26_spmd.sunk | while | flops 479068160 | bytes 65408316 | solution.py:181
  258.5 13.8 reshape.845
  272.2 10.2 slice.163
  282.4 13.9 reshape.846
  312.0 13.8 reshape.845
  325.7 10.2 slice.163
  335.9 13.9 reshape.846
  374.5 105.8 %while.70 = (s32[]{:T(128)}, bf16[2,512,2,64]{1,3,2,0:T(8,128)(2,1)S(1)}, f32[2,2,512]{2,1,0:T(2,128)}, s32[2]{0:T(128)}, s32[1024]{0:T(1024)S(1)}, /*index=5*/b...) while((s32[]{:T(128)}, ...), condition=%wide.region_9.10_spmd, body=%wide.region_6.9_spmd.sunk | while | flops 479068160 | bytes 63376700 | solution.py:181
  382.7 13.7 reshape.843
  396.5 10.2 slice.162
  406.6 13.8 reshape.844
  435.4 13.7 reshape.843
  449.2 10.2 slice.162
  459.3 13.8 reshape.844
  484.7 23.5 all-gather.19.cloned.1.call-done
  514.4 39.7 %reduce-scatter.53.cloned.1.call-done = f32[1024,128]{1,0:T(8,128)} async-done(((f32[4096,128]{1,0:T(8,128)}), f32[1024,128]{1,0:T(8,128)}) %reduce-scatter.53.cloned.1.call-update) | async-done | bytes 524304 | tf_op jit(solution)/shard_map/reduce_scatter | solution.py:61
  555.5 43.7 %reduce-scatter.45.cloned.1.call-done = f32[1024,128]{1,0:T(8,128)} async-done(((f32[4096,128]{1,0:T(8,128)}), f32[1024,128]{1,0:T(8,128)}) %reduce-scatter.45.cloned.1.call-update) | async-done | bytes 524304 | tf_op jit(solution)/shard_map/reduce_scatter | solution.py:61
  601.2 15.9 all-reduce.17
  633.9 22.9 all-gather.41.cloned.1.call-done
  662.6 23.8 all-gather.21.cloned.1.call-done
  692.2 23.6 all-gather.29.cloned.1.call-done
  722.2 82.4 %reduce-scatter.59.cloned.1.call-done = f32[1024,512]{1,0:T(8,128)} async-done(((f32[4096,512]{1,0:T(8,128)}), f32[1024,512]{1,0:T(8,128)}) %reduce-scatter.59.cloned.1.call-update) | async-done | bytes 2097168 | tf_op jit(solution)/shard_map/reduce_scatter | solution.py:47
  804.6 89.3 %reduce-scatter.67.cloned.1.call-done = f32[1024,512]{1,0:T(8,128)} async-done(((f32[4096,512]{1,0:T(8,128)}), f32[1024,512]{1,0:T(8,128)}) %reduce-scatter.67.cloned.1.call-update) | async-done | bytes 2097168 | tf_op jit(solution)/shard_map/reduce_scatter | solution.py:47
  893.8 89.3 %reduce-scatter.47.cloned.1.call-done = f32[1024,512]{1,0:T(8,128)} async-done(((f32[4096,512]{1,0:T(8,128)}), f32[1024,512]{1,0:T(8,128)}) %reduce-scatter.47.cloned.1.call-update) | async-done | bytes 2097168 | tf_op jit(solution)/shard_map/reduce_scatter | solution.py:47
  983.1 89.3 %reduce-scatter.55.cloned.1.call-done = f32[1024,512]{1,0:T(8,128)} async-done(((f32[4096,512]{1,0:T(8,128)}), f32[1024,512]{1,0:T(8,128)}) %reduce-scatter.55.cloned.1.call-update) | async-done | bytes 2097168 | tf_op jit(solution)/shard_map/reduce_scatter | solution.py:47
  1080.9 50.8 %all-gather.35.cloned.1.call-done = bf16[4096,512]{1,0:T(8,128)(2,1)} async-done(((bf16[1024,512]{1,0:T(8,128)(2,1)}), bf16[4096,512]{1,0:T(8,128)(2,1)}) %all-gather.35.cloned.1.call-update) | async-done | bytes 4194320 | tf_op jit(solution)/shard_map/all_gather | solution.py:38
  1136.7 49.3 %all-gather.43.cloned.1.call-done = bf16[4096,512]{1,0:T(8,128)(2,1)} async-done(((bf16[1024,512]{1,0:T(8,128)(2,1)}), bf16[4096,512]{1,0:T(8,128)(2,1)}) %all-gather.43.cloned.1.call-update) | async-done | bytes 4194320 | tf_op jit(solution)/shard_map/all_gather | solution.py:38
  1190.8 50.1 %all-gather.23.cloned.1.call-done = bf16[4096,512]{1,0:T(8,128)(2,1)} async-done(((bf16[1024,512]{1,0:T(8,128)(2,1)}), bf16[4096,512]{1,0:T(8,128)(2,1)}) %all-gather.23.cloned.1.call-update) | async-done | bytes 4194320 | tf_op jit(solution)/shard_map/all_gather | solution.py:38
  1245.8 49.4 %all-gather.31.cloned.1.call-done = bf16[4096,512]{1,0:T(8,128)(2,1)} async-done(((bf16[1024,512]{1,0:T(8,128)(2,1)}), bf16[4096,512]{1,0:T(8,128)(2,1)}) %all-gather.31.cloned.1.call-update) | async-done | bytes 4194320 | tf_op jit(solution)/shard_map/all_gather | solution.py:38
  1300.2 41.1 %reduce-scatter.61.cloned.1.call-done = f32[1024,128]{1,0:T(8,128)} async-done(((f32[4096,128]{1,0:T(8,128)}), f32[1024,128]{1,0:T(8,128)}) %reduce-scatter.61.cloned.1.call-update) | async-done | bytes 524304 | tf_op jit(solution)/shard_map/reduce_scatter | solution.py:61
  1341.2 45.1 %reduce-scatter.69.cloned.1.call-done = f32[1024,128]{1,0:T(8,128)} async-done(((f32[4096,128]{1,0:T(8,128)}), f32[1024,128]{1,0:T(8,128)}) %reduce-scatter.69.cloned.1.call-update) | async-done | bytes 524304 | tf_op jit(solution)/shard_map/reduce_scatter | solution.py:61
  1389.4 15.9 all-reduce.16
  1405.4 26.2 %reduce-scatter.49.cloned.1.call-done = f32[1024,128]{1,0:T(8,128)} async-done(((f32[4096,128]{1,0:T(8,128)}), f32[1024,128]{1,0:T(8,128)}) %reduce-scatter.49.cloned.1.call-update) | async-done | bytes 524304 | tf_op jit(solution)/shard_map/reduce_scatter | solution.py:61
  1431.5 45.0 %reduce-scatter.57.cloned.1.call-done = f32[1024,128]{1,0:T(8,128)} async-done(((f32[4096,128]{1,0:T(8,128)}), f32[1024,128]{1,0:T(8,128)}) %reduce-scatter.57.cloned.1.call-update) | async-done | bytes 524304 | tf_op jit(solution)/shard_map/reduce_scatter | solution.py:61
  1482.7 26.7 %all-gather.45.cloned.1.call-done = bf16[4096,128]{1,0:T(8,128)(2,1)} async-done(((bf16[1024,128]{1,0:T(8,128)(2,1)}), bf16[4096,128]{1,0:T(8,128)(2,1)}) %all-gather.45.cloned.1.call-update) | async-done | bytes 1048592 | tf_op jit(solution)/shard_map/all_gather | solution.py:34
  1513.2 25.6 %all-gather.37.cloned.1.call-done = bf16[4096,128]{1,0:T(8,128)(2,1)} async-done(((bf16[1024,128]{1,0:T(8,128)(2,1)}), bf16[4096,128]{1,0:T(8,128)(2,1)}) %all-gather.37.cloned.1.call-update) | async-done | bytes 1048592 | tf_op jit(solution)/shard_map/all_gather | solution.py:34
  1541.9 34.3 %reduce-scatter.71.cloned.1.call-done = f32[1024,128]{1,0:T(8,128)} async-done(((f32[4096,128]{1,0:T(8,128)}), f32[1024,128]{1,0:T(8,128)}) %reduce-scatter.71.cloned.1.call-update) | async-done | bytes 524304 | tf_op jit(solution)/shard_map/reduce_scatter | solution.py:47
  1580.3 238.4 %while.73 = (s32[]{:T(128)}, f32[1024,2,64]{0,2,1:T(8,128)}, f32[1024,2,64]{0,2,1:T(8,128)}, f32[2047,2,64]{0,2,1:T(8,128)}, f32[2,512,2,64]{1,3,2,0:T(8,128)}, ...) while((s32[]{:T(128)}, f32[1024,2,64]{0,2,1:T(8,128)}, ...), condition=%wide.region_58.59_spmd.clone, body=%wide.region_56.58_spmd.clone.sunk | while | flops 1286930304 | bytes 180049136 | solution.py:240
  1610.8 13.8 reshape.853
  1624.5 10.2 slice.165
  1634.7 13.8 reshape.854
  1718.3 13.7 reshape.853
  1732.0 10.2 slice.165
  1742.2 13.8 reshape.854
  1825.0 248.1 %while.72 = (s32[]{:T(128)}, f32[1024,2,64]{0,2,1:T(8,128)}, f32[1024,2,64]{0,2,1:T(8,128)}, f32[2047,2,64]{0,2,1:T(8,128)}, f32[2,512,2,64]{1,3,2,0:T(8,128)}, ...) while((s32[]{:T(128)}, f32[1024,2,64]{0,2,1:T(8,128)}, ...), condition=%wide.region_43.44_spmd.clone, body=%wide.region_41.43_spmd.clone.sunk | while | flops 1286930304 | bytes 174806128 | solution.py:240
  1856.6 13.7 reshape.847
  1870.2 10.2 slice.164
  1880.4 13.7 reshape.848
  1964.2 13.7 reshape.847
  1977.8 10.2 slice.164
  1988.0 13.7 reshape.848
  2099.6 58.8 %reduce-scatter.77.cloned.1.call-done = f32[128,128]{0,1:T(8,128)} async-done(((f32[2048,128]{0,1:T(8,128)}), f32[128,128]{0,1:T(8,128)}) %reduce-scatter.77.cloned.1.call-update) | async-done | bytes 65552 | tf_op jit(solution)/shard_map/reduce_scatter | solution.py:437
  2159.9 41.0 %all-gather.39.cloned.1.call-done = bf16[4096,384]{0,1:T(8,128)(2,1)} async-done(((bf16[1024,384]{0,1:T(8,128)(2,1)}), bf16[4096,384]{0,1:T(8,128)(2,1)}) %all-gather.39.cloned.1.call-update) | async-done | bytes 3145744 | tf_op jit(solution)/shard_map/all_gather | solution.py:38
  2203.8 42.8 %all-gather.47.cloned.1.call-done = bf16[4096,384]{0,1:T(8,128)(2,1)} async-done(((bf16[1024,384]{0,1:T(8,128)(2,1)}), bf16[4096,384]{0,1:T(8,128)(2,1)}) %all-gather.47.cloned.1.call-update) | async-done | bytes 3145744 | tf_op jit(solution)/shard_map/all_gather | solution.py:38
  2304.0 45.5 %reduce-scatter.73.cloned.1.call-done = f32[1024,128]{1,0:T(8,128)} async-done(((f32[4096,128]{1,0:T(8,128)}), f32[1024,128]{1,0:T(8,128)}) %reduce-scatter.73.cloned.1.call-update) | async-done | bytes 524304 | tf_op jit(solution)/shard_map/reduce_scatter | solution.py:61
  2349.5 45.1 %reduce-scatter.65.cloned.1.call-done = f32[1024,128]{1,0:T(8,128)} async-done(((f32[4096,128]{1,0:T(8,128)}), f32[1024,128]{1,0:T(8,128)}) %reduce-scatter.65.cloned.1.call-update) | async-done | bytes 524304 | tf_op jit(solution)/shard_map/reduce_scatter | solution.py:61
  2397.5 76.0 %all-reduce.14 = (bf16[16,32]{1,0:T(8,128)(2,1)S(1)}, bf16[16,32]{1,0:T(8,128)(2,1)S(1)}, bf16[16,2,16]{2,1,0:T(2,128)(2,1)S(1)}, bf16[16,2,16]{2,1,0:T(2,128)(2...) all-reduce(f32[16,32]{1,0:T(8,128)S(1)} %get-tuple-element.1082, ...), channel_id=18, replica_groups=mesh['dp'=2,'row'=4,'col'=4] {'row','col'}, use_global_device_ids=true, to_apply=%region_66.67.clone | all-reduce | flops 5632 | bytes 33792
  2484.0 13.8 all-reduce.15
  (691 shorter events, 615.5 us)
Async XLA Ops:
  7.2 679.2 %copy-start = (bf16[128,512]{1,0:T(8,128)(2,1)S(1)}, bf16[128,512]{1,0:T(8,128)(2,1)}, u32[]{:S(2)}) copy-start(bf16[128,512]{1,0:T(8,128)(2,1)} %param.36) | copy-start | bytes 393220
  7.2 49.3 %all-gather.17.cloned.1.call-start = ((), (), s32[]{:S(2)}) async-start(), calls=%async_computation.28 | async-start | bytes 1310720 | tf_op jit(solution)/shard_map/all_gather | solution.py:34
  29.0 57.0 %all-gather.25.cloned.1.call-start = ((), (), s32[]{:S(2)}) async-start(), calls=%async_computation.36 | async-start | bytes 1310720 | tf_op jit(solution)/shard_map/all_gather | solution.py:34
  29.8 128.7 %reduce-scatter.43.cloned.1.call-start = ((), (), s32[]{:S(2)}) async-start(), calls=%async_computation.29 | async-start | bytes 7864320 | tf_op jit(solution)/shard_map/reduce_scatter | solution.py:47
  61.4 170.0 %reduce-scatter.51.cloned.1.call-start = ((), (), s32[]{:S(2)}) async-start(), calls=%async_computation.37 | async-start | bytes 7864320 | tf_op jit(solution)/shard_map/reduce_scatter | solution.py:47
  91.0 390.5 %all-gather.27.cloned.1.call-start = ((), (), s32[]{:S(2)}) async-start(), calls=%async_computation.38 | async-start | bytes 1310720 | tf_op jit(solution)/shard_map/all_gather | solution.py:38
  162.3 71.8 %copy-start.49 = (bf16[1024,384]{0,1:T(8,128)(2,1)}, bf16[1024,384]{0,1:T(8,128)(2,1)S(1)}, u32[]{:S(2)}) copy-start(bf16[1024,384]{0,1:T(8,128)(2,1)S(1)} %copy.89) | copy-start | bytes 2359300
  162.3 71.8 %copy-start.92 = (f32[2,64]{1,0:T(2,128)S(1)}, f32[2,64]{1,0:T(2,128)}, u32[]{:S(2)}) copy-start(f32[2,64]{1,0:T(2,128)} %param.31) | copy-start | bytes 1540
  162.3 71.8 %copy-start.93 = (f32[2,64]{1,0:T(2,128)S(1)}, f32[2,64]{1,0:T(2,128)}, u32[]{:S(2)}) copy-start(f32[2,64]{1,0:T(2,128)} %param.30) | copy-start | bytes 1540
  235.5 139.0 %copy-start.56 = (bf16[2,512,2,64]{1,3,2,0:T(8,128)(2,1)S(1)}, bf16[2,512,2,64]{1,3,2,0:T(8,128)(2,1)}, u32[]{:S(2)}) copy-start(bf16[2,512,2,64]{1,3,2,0:T(8,128)(2,1)} %copy-done.55) | copy-start | bytes 786436
  373.9 134.3 %all-gather.19.cloned.1.call-start = ((), (), s32[]{:S(2)}) async-start(), calls=%async_computation.30 | async-start | bytes 1310720 | tf_op jit(solution)/shard_map/all_gather | solution.py:38
  481.5 72.7 %reduce-scatter.53.cloned.1.call-start = ((), (), s32[]{:S(2)}) async-start(), calls=%async_computation.39 | async-start | bytes 2621440 | tf_op jit(solution)/shard_map/reduce_scatter | solution.py:61
  484.6 114.6 %reduce-scatter.45.cloned.1.call-start = ((), (), s32[]{:S(2)}) async-start(), calls=%async_computation.31 | async-start | bytes 2621440 | tf_op jit(solution)/shard_map/reduce_scatter | solution.py:61
  511.3 88.0 %copy-start.35 = (bf16[1,128,1024]{1,2,0:T(8,128)(2,1)S(1)}, bf16[1,128,1024]{1,2,0:T(8,128)(2,1)}, u32[]{:S(2)}) copy-start(bf16[1,128,1024]{1,2,0:T(8,128)(2,1)} %copy-done.34) | copy-start | bytes 786436
  511.3 116.8 %all-gather.33.cloned.1.call-start = ((), (), s32[]{:S(2)}) async-start(), calls=%async_computation.44 | async-start | bytes 1310720 | tf_op jit(solution)/shard_map/all_gather | solution.py:34
  512.5 115.6 %copy-start.57 = (bf16[512,128]{1,0:T(8,128)(2,1)S(1)}, bf16[512,128]{1,0:T(8,128)(2,1)}, u32[]{:S(2)}) copy-start(bf16[512,128]{1,0:T(8,128)(2,1)} %param.38) | copy-start | bytes 393220
  513.3 143.5 %all-gather.41.cloned.1.call-start = ((), (), s32[]{:S(2)}) async-start(), calls=%async_computation.52 | async-start | bytes 1310720 | tf_op jit(solution)/shard_map/all_gather | solution.py:34
  514.3 172.1 %all-gather.21.cloned.1.call-start = ((), (), s32[]{:S(2)}) async-start(), calls=%async_computation.32 | async-start | bytes 1310720 | tf_op jit(solution)/shard_map/all_gather | solution.py:34
  619.6 96.2 %all-gather.29.cloned.1.call-start = ((), (), s32[]{:S(2)}) async-start(), calls=%async_computation.40 | async-start | bytes 1310720 | tf_op jit(solution)/shard_map/all_gather | solution.py:34
  620.2 184.4 %reduce-scatter.59.cloned.1.call-start = ((), (), s32[]{:S(2)}) async-start(), calls=%async_computation.45 | async-start | bytes 10485760 | tf_op jit(solution)/shard_map/reduce_scatter | solution.py:47
  633.9 260.0 %reduce-scatter.67.cloned.1.call-start = ((), (), s32[]{:S(2)}) async-start(), calls=%async_computation.53 | async-start | bytes 10485760 | tf_op jit(solution)/shard_map/reduce_scatter | solution.py:47
  662.6 320.5 %reduce-scatter.47.cloned.1.call-start = ((), (), s32[]{:S(2)}) async-start(), calls=%async_computation.33 | async-start | bytes 10485760 | tf_op jit(solution)/shard_map/reduce_scatter | solution.py:47
  692.2 380.2 %reduce-scatter.55.cloned.1.call-start = ((), (), s32[]{:S(2)}) async-start(), calls=%async_computation.41 | async-start | bytes 10485760 | tf_op jit(solution)/shard_map/reduce_scatter | solution.py:47
  721.5 410.2 %all-gather.35.cloned.1.call-start = ((), (), s32[]{:S(2)}) async-start(), calls=%async_computation.46 | async-start | bytes 5242880 | tf_op jit(solution)/shard_map/all_gather | solution.py:38
  1078.9 107.0 %all-gather.43.cloned.1.call-start = ((), (), s32[]{:S(2)}) async-start(), calls=%async_computation.54 | async-start | bytes 5242880 | tf_op jit(solution)/shard_map/all_gather | solution.py:38
  1079.5 161.5 %all-gather.23.cloned.1.call-start = ((), (), s32[]{:S(2)}) async-start(), calls=%async_computation.34 | async-start | bytes 5242880 | tf_op jit(solution)/shard_map/all_gather | solution.py:38
  1080.3 215.0 %all-gather.31.cloned.1.call-start = ((), (), s32[]{:S(2)}) async-start(), calls=%async_computation.42 | async-start | bytes 5242880 | tf_op jit(solution)/shard_map/all_gather | solution.py:38
  1080.9 260.4 %reduce-scatter.61.cloned.1.call-start = ((), (), s32[]{:S(2)}) async-start(), calls=%async_computation.47 | async-start | bytes 2621440 | tf_op jit(solution)/shard_map/reduce_scatter | solution.py:61
  1136.4 249.9 %reduce-scatter.69.cloned.1.call-start = ((), (), s32[]{:S(2)}) async-start(), calls=%async_computation.55 | async-start | bytes 2621440 | tf_op jit(solution)/shard_map/reduce_scatter | solution.py:61
  1190.8 240.8 %reduce-scatter.49.cloned.1.call-start = ((), (), s32[]{:S(2)}) async-start(), calls=%async_computation.35 | async-start | bytes 2621440 | tf_op jit(solution)/shard_map/reduce_scatter | solution.py:61
  1245.8 230.8 %reduce-scatter.57.cloned.1.call-start = ((), (), s32[]{:S(2)}) async-start(), calls=%async_computation.43 | async-start | bytes 2621440 | tf_op jit(solution)/shard_map/reduce_scatter | solution.py:61
  1300.1 176.5 %copy-start.53 = (bf16[1,128,1024]{1,2,0:T(8,128)(2,1)S(1)}, bf16[1,128,1024]{1,2,0:T(8,128)(2,1)}, u32[]{:S(2)}) copy-start(bf16[1,128,1024]{1,2,0:T(8,128)(2,1)} %copy.127) | copy-start | bytes 786436
  1300.1 176.5 %copy-start.54 = (bf16[1,128,1024]{1,2,0:T(8,128)(2,1)S(1)}, bf16[1,128,1024]{1,2,0:T(8,128)(2,1)}, u32[]{:S(2)}) copy-start(bf16[1,128,1024]{1,2,0:T(8,128)(2,1)} %copy.128) | copy-start | bytes 786436
  1300.1 209.4 %all-gather.45.cloned.1.call-start = ((), (), s32[]{:S(2)}) async-start(), calls=%async_computation.56 | async-start | bytes 1310720 | tf_op jit(solution)/shard_map/all_gather | solution.py:34
  1482.1 56.7 %all-gather.37.cloned.1.call-start = ((), (), s32[]{:S(2)}) async-start(), calls=%async_computation.48 | async-start | bytes 1310720 | tf_op jit(solution)/shard_map/all_gather | solution.py:34
  1482.7 93.6 %reduce-scatter.71.cloned.1.call-start = ((), (), s32[]{:S(2)}) async-start(), calls=%async_computation.57 | async-start | bytes 2621440 | tf_op jit(solution)/shard_map/reduce_scatter | solution.py:47
  1512.4 308.5 %reduce-scatter.63.cloned.1.call-start = ((), (), s32[]{:S(2)}) async-start(), calls=%async_computation.49 | async-start | bytes 2621440 | tf_op jit(solution)/shard_map/reduce_scatter | solution.py:47
  1512.5 65.0 %copy-start.97 = (pred[4]{0:T(512)(128)(4,1)}, pred[4]{0:T(512)(128)(4,1)S(1)}, u32[]{:S(2)}) copy-start(pred[4]{0:T(512)(128)(4,1)S(1)} %iota_compare_fusion.4) | copy-start | bytes 16
  1541.9 616.5 %reduce-scatter.77.cloned.1.call-start = ((), (), s32[]{:S(2)}) async-start(), calls=%async_computation.61 | async-start | bytes 1114112 | tf_op jit(solution)/shard_map/reduce_scatter | solution.py:437
  2079.5 121.3 %all-gather.39.cloned.1.call-start = ((), (), s32[]{:S(2)}) async-start(), calls=%async_computation.50 | async-start | bytes 3932160 | tf_op jit(solution)/shard_map/all_gather | solution.py:38
  2081.5 165.1 %all-gather.47.cloned.1.call-start = ((), (), s32[]{:S(2)}) async-start(), calls=%async_computation.58 | async-start | bytes 3932160 | tf_op jit(solution)/shard_map/all_gather | solution.py:38
  2084.3 175.8 %reduce-scatter.85.cloned.1.call-start = ((), (), s32[]{:S(2)}) async-start(), calls=%async_computation.65 | async-start | bytes 196608 | tf_op jit(solution)/shard_map/reduce_scatter | solution.py:458
  2089.7 178.7 %reduce-scatter.83.cloned.1.call-start = ((), (), s32[]{:S(2)}) async-start(), calls=%async_computation.64 | async-start | bytes 196608 | tf_op jit(solution)/shard_map/reduce_scatter | solution.py:455
  2094.9 106.0 %copy-start.44 = (bf16[4096,128]{1,0:T(8,128)(2,1)S(1)}, bf16[4096,128]{1,0:T(8,128)(2,1)}, u32[]{:S(2)}) copy-start(bf16[4096,128]{1,0:T(8,128)(2,1)} %all-gather.17.cloned.1.call-done) | copy-start | bytes 3145732
  2095.0 184.9 %reduce-scatter.81.cloned.1.call-start = ((), (), s32[]{:S(2)}) async-start(), calls=%async_computation.63 | async-start | bytes 49152 | tf_op jit(solution)/shard_map/reduce_scatter | solution.py:452
  2099.5 191.7 %reduce-scatter.79.cloned.1.call-start = ((), (), s32[]{:S(2)}) async-start(), calls=%async_computation.62 | async-start | bytes 49152 | tf_op jit(solution)/shard_map/reduce_scatter | solution.py:461
  2159.9 142.7 %reduce-scatter.75.cloned.1.call-start = ((), (), s32[]{:S(2)}) async-start(), calls=%async_computation.60 | async-start | bytes 147456 | tf_op jit(solution)/shard_map/reduce_scatter | solution.py:449
  2250.6 98.9 %reduce-scatter.73.cloned.1.call-start = ((), (), s32[]{:S(2)}) async-start(), calls=%async_computation.59 | async-start | bytes 2621440 | tf_op jit(solution)/shard_map/reduce_scatter | solution.py:61
  2253.2 141.5 %reduce-scatter.65.cloned.1.call-start = ((), (), s32[]{:S(2)}) async-start(), calls=%async_computation.51 | async-start | bytes 2621440 | tf_op jit(solution)/shard_map/reduce_scatter | solution.py:61
  2257.5 137.1 %copy-start.36 = (bf16[1,128,1024]{1,2,0:T(8,128)(2,1)S(1)}, bf16[1,128,1024]{1,2,0:T(8,128)(2,1)}, u32[]{:S(2)}) copy-start(bf16[1,128,1024]{1,2,0:T(8,128)(2,1)} %copy-done.34) | copy-start | bytes 786436
  2257.5 137.2 %copy-start.39 = (bf16[1,128,1024]{1,2,0:T(8,128)(2,1)S(1)}, bf16[1,128,1024]{1,2,0:T(8,128)(2,1)}, u32[]{:S(2)}) copy-start(bf16[1,128,1024]{1,2,0:T(8,128)(2,1)} %copy-done.37) | copy-start | bytes 786436
  2257.5 137.2 %copy-start.78 = (f32[1024]{0:T(1024)S(1)}, f32[1024]{0:T(1024)}, u32[]{:S(2)}) copy-start(f32[1024]{0:T(1024)} %copy-done.77) | copy-start | bytes 12292
  2257.5 137.2 %copy-start.80 = (f32[1024]{0:T(1024)S(1)}, f32[1024]{0:T(1024)}, u32[]{:S(2)}) copy-start(f32[1024]{0:T(1024)} %copy-done.79) | copy-start | bytes 12292
  2257.5 137.2 %copy-start.82 = (f32[1024]{0:T(1024)S(1)}, f32[1024]{0:T(1024)}, u32[]{:S(2)}) copy-start(f32[1024]{0:T(1024)} %copy-done.81) | copy-start | bytes 12292
  2257.5 137.2 %copy-start.84 = (f32[1024]{0:T(1024)S(1)}, f32[1024]{0:T(1024)}, u32[]{:S(2)}) copy-start(f32[1024]{0:T(1024)} %copy-done.83) | copy-start | bytes 12292
  2257.5 137.2 %copy-start.90 = (f32[128]{0:T(128)S(1)}, f32[128]{0:T(128)}, u32[]{:S(2)}) copy-start(f32[128]{0:T(128)} %copy-done.89) | copy-start | bytes 1540
  2257.6 247.7 %reduce-scatter.97.cloned.1.call-start = ((), (), s32[]{:S(2)}) async-start(), calls=%async_computation.71 | async-start | bytes 12288
  2270.2 230.7 %copy-start.62 = (f32[1024,128]{1,0:T(8,128)S(1)}, f32[1024,128]{1,0:T(8,128)}, u32[]{:S(2)}) copy-start(f32[1024,128]{1,0:T(8,128)} %get-tuple-element.1012) | copy-start | bytes 1572868
  2270.2 230.7 %copy-start.63 = (f32[1024,128]{1,0:T(8,128)S(1)}, f32[1024,128]{1,0:T(8,128)}, u32[]{:S(2)}) copy-start(f32[1024,128]{1,0:T(8,128)} %get-tuple-element.1069) | copy-start | bytes 1572868
  2481.3 25.3 reduce-scatter.93.cloned.1.call-start
  2498.5 16.0 reduce-scatter.91.cloned.1.call-start
  2499.3 26.1 %reduce-scatter.89.cloned.1.call-start = ((), (), s32[]{:S(2)}) async-start(), calls=%async_computation.67 | async-start | bytes 12288
  2500.0 36.0 %reduce-scatter.87.cloned.1.call-start = ((), (), s32[]{:S(2)}) async-start(), calls=%async_computation.66 | async-start | bytes 12288
  2500.8 46.1 %reduce-scatter.95.cloned.1.call-start = ((), (), s32[]{:S(2)}) async-start(), calls=%async_computation.70 | async-start | bytes 49152
  (118 other events, 1442.2 us)
Sparse Core Ops, SparseCore 0:
  29.2 27.3 all-gather.16
  58.7 27.3 all-gather.24
  89.1 69.3 reduce-scatter.42
  161.3 70.0 reduce-scatter.50
  374.0 26.4 all-gather.26
  481.6 26.5 all-gather.18
  510.5 43.6 reduce-scatter.52
  556.4 42.8 reduce-scatter.44
  600.8 27.1 all-gather.32
  629.5 27.3 all-gather.40
  659.0 27.3 all-gather.20
  688.4 27.3 all-gather.28
  718.9 85.6 reduce-scatter.58
  807.5 86.3 reduce-scatter.66
  896.8 86.3 reduce-scatter.46
  986.0 86.3 reduce-scatter.54
  1079.1 52.5 all-gather.34
  1133.4 52.5 all-gather.42
  1188.4 52.5 all-gather.22
  1242.7 52.5 all-gather.30
  1297.6 43.6 reduce-scatter.60
  1343.5 42.8 reduce-scatter.68
  1388.7 42.8 reduce-scatter.48
  1433.7 42.8 reduce-scatter.56
  1482.2 27.1 all-gather.44
  1511.5 27.3 all-gather.36
  1541.7 34.5 reduce-scatter.70
  1579.2 35.1 reduce-scatter.62
  2079.7 78.6 reduce-scatter.76
  2160.7 40.1 all-gather.38
  2202.7 43.8 all-gather.46
  2249.4 7.5 reduce-scatter.84
  2259.6 8.6 reduce-scatter.82
  2271.1 8.6 reduce-scatter.80
  2282.6 8.6 reduce-scatter.78
  2293.9 8.6 reduce-scatter.74
  2304.7 44.7 reduce-scatter.72
  2351.8 42.8 reduce-scatter.64
  2481.4 3.8 reduce-scatter.96
  2498.6 5.0 reduce-scatter.92
  2505.9 8.6 reduce-scatter.90
  2516.7 8.6 reduce-scatter.88
  2527.4 8.6 reduce-scatter.86
  2538.3 8.6 reduce-scatter.94
where the time goes:
time: 2570 us; the launch traced here: 2560 us
  waiting for transfers between devices  1430 us (56%)
  local copies, waits for them, and re-layouts  550 us (21%)
  matrix products  215 us (8%)
  blocking collectives  150 us (6%)
  loops' own time  111 us (4%)
  other arithmetic  84.4 us (3%)
    reduce_scatter x8, waiting for transfers between devices, sum_over_cols(): lax.psum_scatter(partial_term(jnp.int32(0), lax.axis_size('col') * share_...  474 us
    reduce_scatter x8, waiting for transfers between devices, sum_over_rows(): lax.psum_scatter(partial_term(jnp.int32(0), lax.axis_size('row') * share_...  332 us
    all_gather x8, waiting for transfers between devices, gather_cols(): return lax.all_gather(values, 'col', axis=0, tiled=True)  307 us
    all_gather x8, waiting for transfers between devices, gather_rows(): return lax.all_gather(values, 'row', axis=0, tiled=True)  182 us
    reshape x8, local copies, waits for them, and re-layouts, skew_rows(): return window.reshape(head_total, row_total, rel_span - 1)[:, :, :key_total]  111 us
    reshape x8, local copies, waits for them, and re-layouts, skew_rows(): unshifted_reversed_scores.reshape(head_total, row_total * rel_span)  110 us
    slice x8, local copies, waits for them, and re-layouts, skew_rows(): lax.slice_in_dim(flattened, row_total - 1, row_total - 1 + row_total * (r...  81.4 us
    unnamed x2, blocking collectives  78.5 us
  transfers between devices with their start and end apart: 44, of which 39 were waited for; matrix products, arithmetic and copies ran while one was open for 19% of the time, Pallas kernels for 0%

commit v1 on v0

--- a/solution.py
+++ b/solution.py
@@ -2,7 +2,10 @@
 
 import jax
 import jax.numpy as jnp
+import numpy as np
 from jax import lax
+from jax.experimental import pallas as pl
+from jax.experimental.pallas import tpu as pltpu
 from jax.sharding import PartitionSpec as P
 
 D = 512
@@ -522,6 +525,1060 @@
     )
 
 
+MESH = pl.DeviceIdType.MESH
+F32 = jnp.float32
+BF16 = jnp.bfloat16
+
+
+def aligned(index, size):
+    return index if isinstance(index, int) else pl.multiple_of(index, size)
+
+
+def nt(a, b):
+    return lax.dot_general(a, b, (((1,), (1,)), ((), ())), preferred_element_type=F32)
+
+
+def nn(a, b):
+    return lax.dot_general(a, b, (((1,), (0,)), ((), ())), preferred_element_type=F32)
+
+
+def tn(a, b):
+    return lax.dot_general(a, b, (((0,), (0,)), ((), ())), preferred_element_type=F32)
+
+
+def place():
+    k, z, c = lax.axis_index("dp"), lax.axis_index("row"), lax.axis_index("col")
+    cx = c + 1 - 2 * lax.rem(c, 2)
+    cy = lax.rem(c + 2, 4)
+    near = (1 - k) * cx + k * cy
+    far = k * cx + (1 - k) * cy
+    return k, z, c, near, far
+
+
+def enter(rows):
+    k, z, c, _, _ = place()
+    barrier = pltpu.get_barrier_semaphore()
+    peers = [(1 - k, z, c)]
+    for step in range(1, rows):
+        peers.append((k, lax.rem(z + step, rows), c))
+    for step in range(1, 4):
+        for core in range(2):
+            peers.append((0 * k + core, z, lax.rem(c + step, 4)))
+    for peer in peers:
+        pl.semaphore_signal(barrier, inc=1, device_id=peer, device_id_type=MESH)
+    pl.semaphore_wait(barrier, len(peers))
+
+
+class Sems:
+    def __init__(self, send, recv):
+        self.send, self.recv, self.next = send, recv, 0
+        self.pending = []
+
+    def take(self, count=1):
+        first = self.next
+        self.next += count
+        return first
+
+
+def remote(sems, src, dst, slot, peer, when=None):
+    copy = pltpu.make_async_remote_copy(
+        src, dst, sems.send.at[slot], sems.recv.at[slot], device_id=peer, device_id_type=MESH
+    )
+
+    def start():
+        copy.start()
+
+    def finish():
+        copy.wait_send()
+
+    if when is None:
+        copy.start()
+        sems.pending.append(finish)
+    else:
+        pl.when(when)(start)
+        sems.pending.append(lambda: pl.when(when)(finish))
+
+
+def arrived(sems, dst, slot):
+    pltpu.make_async_copy(dst, dst, sems.recv.at[slot]).wait()
+
+
+def drain(sems):
+    for finish in sems.pending:
+        finish()
+    sems.pending = []
+
+
+def tall(row):
+    padded = jnp.concatenate([row, jnp.zeros((120, 128), F32)], axis=0)
+    return jnp.transpose(padded)
+
+
+def forward_kernel(
+    tok, cot, starts, small_col, small_row, table, wq, wp, wo, wu, wd,
+    att, wo_all, wu_all, wd_all, wq_half, wp_half, xt, ct, normed_t, qcat, keys, vals, qv, probs, heads_out, params_col, params_row,
+    kcat, own_att, starts_got, send, recv,
+):
+    rows = wu_all.shape[0]
+    cols = wo_all.shape[0]
+    half = rows // 2
+    k, z, c, near, far = place()
+    sems = Sems(send, recv)
+    mine = lax.div(z, half) == k
+    enter(rows)
+
+    def q_block(cc):
+        return wq_half.at[:, pl.ds(aligned(cc * 128, 128), 128), :]
+
+    def p_block(cc):
+        return wp_half.at[:, pl.ds(aligned(cc * 128, 128), 128), :]
+
+    def u_block(cc, core=k):
+        return wu_all.at[pl.ds(core * half, half), pl.ds(aligned(cc * 128, 128), 128), :]
+
+    def o_block(cc, core=k):
+        size = wo_all.shape[1] // 2
+        return wo_all.at[cc, pl.ds(aligned(core * size, 128), size), :]
+
+    def d_block(cc, core=k):
+        size = wd_all.shape[1] // 2
+        return wd_all.at[cc, pl.ds(aligned(core * size, 128), size), :]
+
+    def q_one(i):
+        return wq_half.at[i, pl.ds(aligned(c * 128, 128), 128), :]
+
+    def p_one(i):
+        return wp_half.at[i, pl.ds(aligned(c * 128, 128), 128), :]
+
+    def u_one(i):
+        return wu_all.at[k * half + i, pl.ds(aligned(c * 128, 128), 128), :]
+
+    def o_one(i):
+        size = wo_all.shape[1] // rows
+        return wo_all.at[c, pl.ds(aligned((k * half + i) * size, 128), size), :]
+
+    def d_one(i):
+        size = wd_all.shape[1] // rows
+        return wd_all.at[c, pl.ds(aligned((k * half + i) * size, 128), size), :]
+
+    weights = {
+        "q": (wq, q_one, q_block), "p": (wp, p_one, p_block), "o": (wo, o_one, o_block),
+        "u": (wu, u_one, u_block), "d": (wd, d_one, d_block),
+    }
+    z_slot = {name: sems.take(2 * half * rows) for name in weights}
+    near_slot = {name: sems.take(1) for name in weights}
+    far_slot = {name: sems.take(2) for name in weights}
+    sib_slot = {name: sems.take(4) for name in weights}
+
+    def z_start(name):
+        ref, one, _ = weights[name]
+        for i in range(half):
+            here = z == k * half + i
+            slot = z_slot[name] + i * 2
+
+            @pl.when(here)
+            def _(ref=ref, dst=one(i), slot=slot):
+                pltpu.make_async_copy(ref, dst, recv.at[slot]).start()
+
+            for step in range(1, rows):
+                peer = (k, lax.rem(z + step, rows), c)
+                copy = pltpu.make_async_remote_copy(
+                    ref, one(i), send.at[z_slot[name] + half * 2 + i * rows + step], recv.at[slot],
+                    device_id=peer, device_id_type=MESH,
+                )
+                pl.when(here)(copy.start)
+                sems.pending.append(lambda copy=copy, here=here: pl.when(here)(copy.wait_send))
+
+    def z_done(name):
+        _, one, _ = weights[name]
+        for i in range(half):
+            arrived(sems, one(i), z_slot[name] + i * 2)
+
+    def near_start(name):
+        block = weights[name][2]
+        remote(sems, block(c), block(c), near_slot[name], (k, z, near))
+
+    def near_done(name):
+        arrived(sems, weights[name][2](near), near_slot[name])
+
+    def far_start(name):
+        block = weights[name][2]
+        remote(sems, block(c), block(c), far_slot[name], (k, z, far))
+        remote(sems, block(near), block(near), far_slot[name] + 1, (k, z, far))
+
+    def far_done(name):
+        block = weights[name][2]
+        arrived(sems, block(far), far_slot[name])
+        arrived(sems, block(3 - c), far_slot[name] + 1)
+
+    def sib_start(name):
+        block = weights[name][2]
+        for cc in range(4):
+            remote(sems, block(cc), block(cc), sib_slot[name] + cc, (1 - k, z, c))
+
+    def sib_done(name):
+        block = weights[name][2]
+        for cc in range(4):
+            arrived(sems, block(cc, 1 - k), sib_slot[name] + cc)
+
+    feat = tok.shape[1]
+    x_slot = sems.take(4)
+    x_send = sems.take(4)
+    xf_slot = sems.take(4)
+
+    def x_part(cc, core):
+        return xt.at[pl.ds(aligned(cc * feat + core * (feat // 2), 64), feat // 2), :]
+
+    z_start("q")
+    for b in range(2):
+        target = 2 * b + k
+        for core in range(2):
+            src = tok.at[b, pl.ds(core * (feat // 2), feat // 2), :]
+            dst = x_part(c, core)
+            local = jnp.logical_and(target == c, core == k)
+
+            @pl.when(local)
+            def _(src=src, dst=dst):
+                pltpu.make_async_copy(src, dst, recv.at[x_slot + c]).start()
+
+            copy = pltpu.make_async_remote_copy(
+                src, dst, send.at[x_send + 2 * b + core], recv.at[x_slot + c],
+                device_id=(0 * k + core, z, target), device_id_type=MESH,
+            )
+            far_away = jnp.logical_not(local)
+            pl.when(far_away)(copy.start)
+            sems.pending.append(lambda copy=copy, far_away=far_away: pl.when(far_away)(copy.wait_send))
+
+    g_col = sems.take(4)
+    g_row = sems.take(rows)
+    for step in range(1, 4):
+        peer = (k, z, lax.rem(c + step, 4))
+        copy = pltpu.make_async_remote_copy(
+            small_col, params_col.at[c], send.at[g_col + step], recv.at[g_col],
+            device_id=peer, device_id_type=MESH,
+        )
+        copy.start()
+        sems.pending.append(copy.wait_send)
+    pltpu.make_async_copy(small_col, params_col.at[c], recv.at[g_col]).start()
+    for step in range(1, rows):
+        peer = (k, lax.rem(z + step, rows), c)
+        copy = pltpu.make_async_remote_copy(
+            small_row, params_row.at[z], send.at[g_row + step], recv.at[g_row],
+            device_id=peer, device_id_type=MESH,
+        )
+        copy.start()
+        sems.pending.append(copy.wait_send)
+    pltpu.make_async_copy(small_row, params_row.at[z], recv.at[g_row]).start()
+    s_slot = sems.take(1)
+    s_send = sems.take(4)
+    for b in range(2):
+        for core in range(2):
+            target = 2 * b + k
+            owner = c == z
+            local = jnp.logical_and(owner, jnp.logical_and(target == c, core == k))
+            away = jnp.logical_and(owner, jnp.logical_not(jnp.logical_and(target == c, core == k)))
+
+            @pl.when(local)
+            def _():
+                pltpu.make_async_copy(starts, starts_got, recv.at[s_slot]).start()
+
+            copy = pltpu.make_async_remote_copy(
+                starts, starts_got, send.at[s_send + 2 * b + core], recv.at[s_slot],
+                device_id=(0 * k + core, z, target), device_id_type=MESH,
+            )
+            pl.when(away)(copy.start)
+            sems.pending.append(lambda copy=copy, away=away: pl.when(away)(copy.wait_send))
+
+    for name in ("p", "o", "u", "d"):
+        z_start(name)
+
+    c_slot = sems.take(4)
+    c_send = sems.take(4)
+    tok_half = ct.shape[1]
+    for b in range(2):
+        target = 2 * b + k
+        for core in range(2):
+            src = cot.at[b, :, pl.ds(core * tok_half, tok_half)]
+            dst = ct.at[pl.ds(aligned(c * feat, 128), feat), :]
+            local = jnp.logical_and(target == c, core == k)
+
+            @pl.when(local)
+            def _(src=src, dst=dst):
+                pltpu.make_async_copy(src, dst, recv.at[c_slot + c]).start()
+
+            copy = pltpu.make_async_remote_copy(
+                src, dst, send.at[c_send + 2 * b + core], recv.at[c_slot + c],
+                device_id=(0 * k + core, z, target), device_id_type=MESH,
+            )
+            away = jnp.logical_not(local)
+            pl.when(away)(copy.start)
+            sems.pending.append(lambda copy=copy, away=away: pl.when(away)(copy.wait_send))
+
+    for cc in range(4):
+        arrived(sems, x_part(cc, k), x_slot + cc)
+        remote(sems, x_part(cc, k), x_part(cc, k), xf_slot + cc, (1 - k, z, c))
+    z_done("q")
+    near_start("q")
+    z_done("p")
+    near_start("p")
+    arrived(sems, params_col, g_col)
+    arrived(sems, params_row, g_row)
+    arrived(sems, starts_got, s_slot)
+    for cc in range(4):
+        arrived(sems, x_part(cc, 1 - k), xf_slot + cc)
+
+    columns = [tall(params_col[cc]) for cc in range(4)]
+    gain = jnp.concatenate([col[:, 0:1] for col in columns], axis=0)
+    bias = jnp.concatenate([col[:, 1:2] for col in columns], axis=0)
+    width = xt.shape[0]
+    seq = xt.shape[1]
+    piece = PIECE
+
+    @pl.loop(0, seq // 256)
+    def _(t):
+        here = pl.ds(aligned(t * 256, 256), 256)
+        x = xt[:, here].astype(F32)
+        mean = jnp.sum(x, axis=0, keepdims=True) * (1.0 / width)
+        square = jnp.sum(x * x, axis=0, keepdims=True) * (1.0 / width)
+        inverse = lax.rsqrt(square - mean * mean + norm_epsilon)
+        normed_t[:, here] = ((x - mean) * inverse * gain + bias).astype(BF16)
+
+    near_done("q")
+    far_start("q")
+    near_done("p")
+    far_start("p")
+    for name in ("o", "u", "d"):
+        z_done(name)
+        near_start(name)
+
+    kcat[:, 0:512] = table[...]
+    far_done("q")
+    scale = 0.125
+    zeros = jnp.zeros((256, 64), F32)
+    for i in range(half):
+        small = params_row[k * half + i]
+
+        @pl.loop(0, seq // 256)
+        def _(t, i=i, small=small):
+            here = pl.ds(aligned(t * 256, 256), 256)
+            got = tn(normed_t[:, here], wq_half[i])
+            for hb in range(2):
+                h = 2 * i + hb
+                low = got[:, hb * 192 : hb * 192 + 192].astype(BF16).astype(F32)
+                query, key, value = low[:, 0:64], low[:, 64:128], low[:, 128:192]
+                content = small[4:5, hb * 64 : hb * 64 + 64]
+                position = small[5:6, hb * 64 : hb * 64 + 64]
+                qcat[h, here, 512:640] = jnp.concatenate(
+                    [(query + content) * scale, zeros], axis=1
+                ).astype(BF16)
+                qv[h, here, :] = ((query + position) * scale).astype(BF16)
+                keys[h, here, :] = jnp.concatenate([key, zeros], axis=1).astype(BF16)
+                vals[h, here, :] = value.astype(BF16)
+
+    far_done("p")
+    for i in range(half):
+        for hb in range(2):
+            h = 2 * i + hb
+
+            @pl.loop(0, seq // 256)
+            def _(t, i=i, hb=hb, h=h):
+                here = pl.ds(aligned(t * 256, 256), 256)
+                angle = nt(qv[h, here, :], wp_half[i, :, hb * 64 : hb * 64 + 64])
+                cosine = table[here, 0:256].astype(F32)
+                sine = table[here, 256:512].astype(F32)
+                first, second = angle[:, 0:256], angle[:, 256:512]
+                qcat[h, here, 0:256] = (first * sine + second * cosine).astype(BF16)
+                qcat[h, here, 256:512] = (second * sine - first * cosine).astype(BF16)
+
+    slot_len = seq // 2
+    block = 256
+    batch = lax.div(c, 2)
+
+    def attend(h, low_row, keys_seen, slot):
+        start = starts_got[pl.ds(2 * batch + slot, 1), :][:, 0:1]
+        row = low_row + lax.broadcasted_iota(jnp.int32, (block, 1), 0)
+        inside = jnp.logical_and(row >= start, row < start + piece)
+        limit = jnp.where(inside, start + (piece - 1), row)
+        here = pl.ds(aligned(low_row, block), block)
+        scores = nt(qcat[h, here, :], kcat[0:keys_seen, :])
+        column = slot * slot_len + lax.broadcasted_iota(jnp.int32, (block, slot_len), 1)
+        last = jnp.where(column <= limit, scores[:, keys_seen - slot_len :], big_negative)
+        top = jnp.max(last, axis=1, keepdims=True)
+        if slot == 1:
+            top = jnp.maximum(top, jnp.max(scores[:, :slot_len], axis=1, keepdims=True))
+        last = jnp.exp(last - top)
+        total = jnp.sum(last, axis=1, keepdims=True)
+        if slot == 1:
+            first = jnp.exp(scores[:, :slot_len] - top)
+            total = total + jnp.sum(first, axis=1, keepdims=True)
+            whole = jnp.concatenate([first, last], axis=1)
+        else:
+            whole = last
+        low = (whole * (1.0 / total)).astype(BF16)
+        probs[h, here, 0:keys_seen] = low
+        heads_out[h, here, :] = nn(low, vals[h, 0:keys_seen, :])
+
+    for i in range(half):
+
+        @pl.loop(0, 2)
+        def _(hb, i=i):
+            h = 2 * i + hb
+            kcat[:, 512:640] = keys[h]
+
+            @pl.loop(0, slot_len // block)
+            def _(t):
+                attend(h, t * block, slot_len, 0)
+
+            @pl.loop(0, slot_len // block)
+            def _(t):
+                attend(h, slot_len + t * block, seq, 1)
+
+        if i == 0:
+            for name in ("o", "u", "d"):
+                near_done(name)
+                far_start(name)
+
+    for name in ("o", "u"):
+        far_done(name)
+        sib_start(name)
+    mine_cols = jnp.concatenate([heads_out[h] for h in range(2 * half)], axis=1).astype(BF16)
+    own_att[...] = mine_cols
+    a_slot = sems.take(2)
+    span = own_att.shape[1]
+    other = pl.ds(aligned((1 - k) * tok_half, tok_half), tok_half)
+    own = pl.ds(aligned(k * tok_half, tok_half), tok_half)
+    remote(sems, own_att.at[other, :], att.at[:, pl.ds(aligned(k * span, 128), span)], a_slot, (1 - k, z, c))
+    pltpu.make_async_copy(
+        own_att.at[own, :], att.at[:, pl.ds(aligned(k * span, 128), span)], recv.at[a_slot + 1]
+    ).start()
+    far_done("d")
+    sib_start("d")
+    arrived(sems, own_att.at[own, :], a_slot + 1)
+    arrived(sems, own_att.at[own, :], a_slot)
+    for cc in range(4):
+        arrived(sems, ct.at[pl.ds(cc * feat, feat), :], c_slot + cc)
+    for name in ("o", "u", "d"):
+        sib_done(name)
+    drain(sems)
+
+
+def erf_parts(values):
+    erf = lax.erf(values * inv_sqrt_two)
+    return 0.5 * (1.0 + erf)
+
+
+def middle_kernel(
+    att, wo_all, wu_all, wd_all, xt, ct, params_col, params_row,
+    out_t, grad_mid_t, grad_att, g_up, g_down, g_out, small,
+    mid, norm, hat, inv, gout, acc_out, acc_two, tall_norm,
+):
+    rows, cols = wu_all.shape[0], wo_all.shape[0]
+    count = att.shape[0]
+    k = lax.axis_index("dp")
+    own = pl.ds(aligned(k * count, count), count)
+
+    def line(index):
+        return jnp.concatenate([params_col[cc, index : index + 1, :] for cc in range(cols)], axis=1)
+
+    def out_weight():
+        return jnp.concatenate([wo_all[cc] for cc in range(cols)], axis=1)
+
+    width = att.shape[1]
+    x = jnp.transpose(xt[:, own].astype(F32))
+    middle = x + nn(att[...], out_weight())
+    mid[...] = middle
+    mean = jnp.sum(middle, axis=1, keepdims=True) * (1.0 / width)
+    square = jnp.sum(middle * middle, axis=1, keepdims=True) * (1.0 / width)
+    inverse = lax.rsqrt(square - mean * mean + norm_epsilon)
+    scaled = (middle - mean) * inverse
+    hat[...] = scaled
+    inv[...] = inverse
+    low = (scaled * line(2) + line(3)).astype(BF16)
+    norm[...] = low
+    tall_norm[...] = jnp.transpose(low)
+    gout[...] = jnp.transpose(ct[...])
+    acc_out[...] = jnp.zeros_like(acc_out)
+    acc_two[...] = jnp.zeros_like(acc_two)
+    small[...] = jnp.zeros_like(small)
+    hidden = wu_all.shape[2]
+
+    @pl.loop(0, rows)
+    def _(r):
+        here = pl.ds(aligned(r * hidden, hidden), hidden)
+        bias = jnp.concatenate([params_row[r, j : j + 1, :] for j in range(hidden // 128)], axis=1)
+        down = jnp.concatenate([wd_all[cc, here, :] for cc in range(cols)], axis=1)
+        pre = nn(norm[...], wu_all[r]) + bias
+        grad_act = nt(gout[...], down)
+        half = erf_parts(pre)
+        act = (pre * half).astype(BF16)
+        slope = half + pre * jnp.exp(-0.5 * pre * pre) * inv_sqrt_tau
+        grad = grad_act * slope
+        low_grad = grad.astype(BF16)
+        small[pl.ds(5 + r, 1), :] = jnp.sum(low_grad.astype(F32), axis=0, keepdims=True)
+        acc_out[...] += nn(act, down)
+        acc_two[...] += nt(low_grad, wu_all[r])
+        g_up[r] = nn(tall_norm[...], low_grad).astype(BF16)
+        found = tn(act, gout[...]).astype(BF16)
+        for cc in range(cols):
+            g_down[cc, here, :] = found[:, cc * 128 : cc * 128 + 128]
+
+    cotangent = gout[...].astype(F32)
+    out_t[...] = jnp.transpose(mid[...] + acc_out[...] + line(4)).astype(BF16)
+    two = acc_two[...]
+    small[2:3, :] = jnp.sum(two * hat[...], axis=0, keepdims=True)
+    small[3:4, :] = jnp.sum(two, axis=0, keepdims=True)
+    small[4:5, :] = jnp.sum(cotangent, axis=0, keepdims=True)
+    shifted = two * line(2)
+    first = jnp.sum(shifted, axis=1, keepdims=True) * (1.0 / width)
+    second = jnp.sum(shifted * hat[...], axis=1, keepdims=True) * (1.0 / width)
+    grad_mid = cotangent + inv[...] * (shifted - first - hat[...] * second)
+    grad_mid_t[...] = jnp.transpose(grad_mid)
+    branch = grad_mid.astype(BF16)
+    grad_att[...] = nt(branch, out_weight()).astype(BF16)
+    found = tn(att[...], branch).astype(BF16)
+    for cc in range(cols):
+        g_out[cc] = found[:, cc * 128 : cc * 128 + 128]
+
+
+def backward_kernel(
+    out_t, grad_mid_t, grad_att, g_up, g_down, g_out, small, params_col, table, wq_half, wp_half, xt, normed_t,
+    qcat, keys, vals, qv, probs, heads_out,
+    outs, grads, f_q, f_p, f_o, f_u, f_d, f_small,
+    kcat, grad_o, head_grad, turned, turned_k, turned_v, turned_p, one_t, one_low, one_got, grad_x, sum_a, sum_b,
+    hs_q, hs_p, hs_o, hs_u, hs_d, r0_o, r0_u, r0_d,
+    r1_q, r1_p, r1_o, r1_u, r1_d, r2_q, r2_p, r2_o, r2_u, r2_d, r3_q, r3_p, r3_o, r3_u, r3_d,
+    all_small, got_small, got_z, send, recv,
+):
+    rows, cols = g_up.shape[0], g_out.shape[0]
+    half = rows // 2
+    k, z, c, near, far = place()
+    sems = Sems(send, recv)
+    mine = lax.div(z, half) == k
+    enter(rows)
+    sibling = (1 - k, z, c)
+
+    hs = {
+        "q": lambda i, cc: hs_q.at[i, cc], "p": lambda i, cc: hs_p.at[i, cc], "u": lambda i, cc: hs_u.at[i, cc],
+        "o": lambda i, cc: hs_o.at[cc, i], "d": lambda i, cc: hs_d.at[cc, i],
+    }
+    r1 = {"q": r1_q, "p": r1_p, "o": r1_o, "u": r1_u, "d": r1_d}
+    r2 = {"q": r2_q, "p": r2_p, "o": r2_o, "u": r2_u, "d": r2_d}
+    r3 = {"q": r3_q, "p": r3_p, "o": r3_o, "u": r3_u, "d": r3_d}
+    final = {"q": f_q, "p": f_p, "o": f_o, "u": f_u, "d": f_d}
+    slots = {}
+    for name in ("o", "u", "d", "q", "p"):
+        slots[name, "sib"] = sems.take(4)
+        slots[name, "one"] = sems.take(2 * half)
+        slots[name, "two"] = sems.take(half)
+        slots[name, "z"] = sems.take(rows * half)
+        slots[name, "last"] = sems.take(1)
+
+    def grad_half(name, core):
+        if name == "u":
+            return g_up.at[pl.ds(core * half, half)]
+        full = g_out if name == "o" else g_down
+        size = full.shape[1] // 2
+        return full.at[:, pl.ds(aligned(core * size, 128), size), :]
+
+    got0 = {"u": r0_u, "o": r0_o, "d": r0_d}
+
+    def sib_start(name):
+        remote(sems, grad_half(name, 1 - k), got0[name], slots[name, "sib"], sibling)
+
+    def sib_done(name):
+        arrived(sems, got0[name], slots[name, "sib"])
+        if name == "u":
+            for i in range(half):
+                total = g_up[k * half + i].astype(F32) + r0_u[i].astype(F32)
+                hs_u[i] = total.astype(BF16).reshape(hs_u.shape[1:])
+        else:
+            full = g_out if name == "o" else g_down
+            size = full.shape[1] // 2
+            to = hs_o if name == "o" else hs_d
+            for cc in range(cols):
+                part = full[cc, pl.ds(aligned(k * size, 128), size), :]
+                total = part.astype(F32) + got0[name][cc].astype(F32)
+                to[cc] = total.astype(BF16).reshape(to.shape[1:])
+
+    def one_start(name, i):
+        block = hs[name]
+        remote(sems, block(i, far), r1[name].at[i, 0], slots[name, "one"] + 2 * i, (k, z, far))
+        remote(sems, block(i, 3 - c), r1[name].at[i, 1], slots[name, "one"] + 2 * i + 1, (k, z, far))
+
+    def load(ref):
+        return ref[...].astype(F32)
+
+    def one_done(name, i):
+        block = hs[name]
+        arrived(sems, r1[name].at[i, 1], slots[name, "one"] + 2 * i + 1)
+        r1[name][i, 1] = (r1[name][i, 1].astype(F32) + load(block(i, near))).astype(BF16)
+        remote(sems, r1[name].at[i, 1], r2[name].at[i], slots[name, "two"] + i, (k, z, near))
+        arrived(sems, r1[name].at[i, 0], slots[name, "one"] + 2 * i)
+        r1[name][i, 0] = (r1[name][i, 0].astype(F32) + load(block(i, c))).astype(BF16)
+
+    def two_done(name, i):
+        arrived(sems, r2[name].at[i], slots[name, "two"] + i)
+        r2[name][i] = (r2[name][i].astype(F32) + r1[name][i, 0].astype(F32)).astype(BF16)
+        target = k * half + i
+        base = slots[name, "z"]
+        away = z != target
+        copy = pltpu.make_async_remote_copy(
+            r2[name].at[i], r3[name].at[z], send.at[base + i], recv.at[base + z],
+            device_id=(k, target, c), device_id_type=MESH,
+        )
+        pl.when(away)(copy.start)
+        sems.pending.append(lambda: pl.when(away)(copy.wait_send))
+
+    def z_done(name):
+        base = slots[name, "z"]
+        to = final[name]
+
+        @pl.when(mine)
+        def _():
+            total = r2[name][z - k * half].astype(F32)
+            for step in range(1, rows):
+                source = lax.rem(z + step, rows)
+                arrived(sems, r3[name].at[source], base + source)
+                total = total + r3[name][source].astype(F32)
+            to[...] = total
+
+        copy = pltpu.make_async_remote_copy(
+            to, to, send.at[slots[name, "last"]], recv.at[slots[name, "last"]],
+            device_id=sibling, device_id_type=MESH,
+        )
+        pl.when(mine)(copy.start)
+        sems.pending.append(lambda: pl.when(mine)(copy.wait_send))
+
+    def last_done(name):
+        @pl.when(jnp.logical_not(mine))
+        def _():
+            arrived(sems, final[name], slots[name, "last"])
+
+    batch, origin = lax.div(c, 2), lax.rem(c, 2)
+    feat = outs.shape[2]
+
+    def back_start(src, dst, base):
+        for step in range(4):
+            cc = lax.rem(c + step, 4)
+            part = src.at[pl.ds(aligned(cc * feat, 128), feat), :]
+            if step == 0:
+                local = origin == k
+
+                @pl.when(local)
+                def _():
+                    pltpu.make_async_copy(part, dst.at[batch, k], recv.at[base + 2 * batch + k]).start()
+
+                copy = pltpu.make_async_remote_copy(
+                    part, dst.at[batch, k], send.at[base + step], recv.at[base + 2 * batch + k],
+                    device_id=sibling, device_id_type=MESH,
+                )
+                away = jnp.logical_not(local)
+                pl.when(away)(copy.start)
+                sems.pending.append(lambda copy=copy, away=away: pl.when(away)(copy.wait_send))
+            else:
+                remote(
+                    FarSems(sems, base + step, base + 2 * batch + k), part, dst.at[batch, k], None, (origin, z, cc)
+                )
+
+    def back_done(dst, base):
+        for b in range(2):
+            for core in range(2):
+                arrived(sems, dst.at[b, core], base + 2 * b + core)
+
+    count = grad_att.shape[0]
+    span = grad_o.shape[1]
+    own = pl.ds(aligned(k * count, count), count)
+    d_slot = sems.take(2)
+    remote(sems, grad_att.at[:, pl.ds(aligned((1 - k) * span, 128), span)], grad_o.at[own, :], d_slot, sibling)
+    pltpu.make_async_copy(
+        grad_att.at[:, pl.ds(aligned(k * span, 128), span)], grad_o.at[own, :], recv.at[d_slot + 1]
+    ).start()
+    for name in ("u", "d", "o"):
+        sib_start(name)
+    b_slot = sems.take(4)
+    back_start(out_t, outs, b_slot)
+    kcat[:, 0:512] = table[...]
+    sum_a[...] = jnp.zeros_like(sum_a)
+    sum_b[...] = jnp.zeros_like(sum_b)
+    arrived(sems, grad_o.at[own, :], d_slot + 1)
+    arrived(sems, grad_o.at[own, :], d_slot)
+    for h in range(2 * half):
+        head_grad[h] = grad_o[:, h * 64 : h * 64 + 64]
+
+    seq = xt.shape[1]
+    slot_len = seq // 2
+    block = 256
+
+    def attend_back(h, hb, low_row, keys_seen):
+        here = pl.ds(aligned(low_row, block), block)
+        grad = head_grad[h, here, :]
+        low = probs[h, here, 0:keys_seen]
+        inner = jnp.sum(grad.astype(F32) * heads_out[h, here, :], axis=1, keepdims=True)
+        grad_prob = nt(grad, vals[h, 0:keys_seen, :])
+        grad_score = (low.astype(F32) * (grad_prob - inner)).astype(BF16)
+        turned_v[:, 0:keys_seen] += tn(grad, low)
+        turned_k[:, 0:keys_seen] += tn(qcat[h, here, 512:576], grad_score)
+        got = nn(grad_score, kcat[0:keys_seen, :])
+        cosine = table[here, 0:256].astype(F32)
+        sine = table[here, 256:512].astype(F32)
+        first, second = got[:, 0:256], got[:, 256:512]
+        angle = jnp.concatenate([first * sine - second * cosine, first * cosine + second * sine], axis=1).astype(BF16)
+        return here, got[:, 512:640], angle
+
+    def one_head(i, hb):
+        h = 2 * i + hb
+        kcat[:, 512:640] = keys[h]
+        turned_k[...] = jnp.zeros_like(turned_k)
+        turned_v[...] = jnp.zeros_like(turned_v)
+        turned_p[...] = jnp.zeros_like(turned_p)
+        weight = wp_half[i, :, hb * 64 : hb * 64 + 64]
+
+        def step(low_row, keys_seen):
+            here, grad_u, angle = attend_back(h, hb, low_row, keys_seen)
+            grad_v = nn(angle, weight)
+            turned_p[...] += tn(qv[h, here, :], angle)
+            grad_u = grad_u[:, 0:64]
+            sum_a[h : h + 1, 0:64] += jnp.sum(grad_u, axis=0, keepdims=True) * 0.125
+            sum_b[h : h + 1, 0:64] += jnp.sum(grad_v, axis=0, keepdims=True) * 0.125
+            both = jnp.concatenate([(grad_u + grad_v) * 0.125, jnp.zeros((block, 64), F32)], axis=1)
+            turned[i, hb * 192 : hb * 192 + 64, here] = jnp.transpose(both)[0:64].astype(BF16)
+
+        @pl.loop(0, slot_len // block)
+        def _(t):
+            step(t * block, slot_len)
+
+        @pl.loop(0, slot_len // block)
+        def _(t):
+            step(slot_len + t * block, seq)
+
+        turned[i, hb * 192 + 64 : hb * 192 + 128, :] = turned_k[...].astype(BF16)
+        turned[i, hb * 192 + 128 : hb * 192 + 192, :] = turned_v[...].astype(BF16)
+        return turned_p[...]
+
+    for i in range(half):
+        first = one_head(i, 0)
+        if i == 0:
+            for name in ("u", "d", "o"):
+                sib_done(name)
+                for j in range(half):
+                    one_start(name, j)
+        else:
+            for name in ("u", "d", "o"):
+                for j in range(half):
+                    two_done(name, j)
+        second = one_head(i, 1)
+        hs_p[i] = jnp.transpose(jnp.concatenate([first, second], axis=0)).astype(BF16).reshape(hs_p.shape[1:])
+        hs_q[i] = nt(normed_t[...], turned[i]).astype(BF16).reshape(hs_q.shape[1:])
+        if i == 0:
+            for name in ("u", "d", "o"):
+                for j in range(half):
+                    one_done(name, j)
+        one_start("q", i)
+        one_start("p", i)
+        part = nn(wq_half[i], turned[i])
+        if i == 0:
+            one_t[...] = part
+        else:
+            one_t[...] += part
+
+    other = pl.ds(aligned((1 - k) * count, count), count)
+    one_low[...] = one_t[:, other].astype(BF16)
+    e_slot = sems.take(1)
+    remote(sems, one_low, one_got, e_slot, sibling)
+    for i in range(half):
+        one_done("q", i)
+        one_done("p", i)
+    arrived(sems, one_got, e_slot)
+    columns = [tall(params_col[cc]) for cc in range(cols)]
+    gain = jnp.concatenate([col[:, 0:1] for col in columns], axis=0)
+    width = xt.shape[0]
+    one = one_t[:, own] + one_got[...].astype(F32)
+    x = xt[:, own].astype(F32)
+    mean = jnp.sum(x, axis=0, keepdims=True) * (1.0 / width)
+    square = jnp.sum(x * x, axis=0, keepdims=True) * (1.0 / width)
+    inverse = lax.rsqrt(square - mean * mean + norm_epsilon)
+    scaled = (x - mean) * inverse
+    shifted = one * gain
+    first = jnp.sum(shifted, axis=0, keepdims=True) * (1.0 / width)
+    second = jnp.sum(shifted * scaled, axis=0, keepdims=True) * (1.0 / width)
+    grad_x[...] = (grad_mid_t[...] + inverse * (shifted - first - scaled * second)).astype(BF16)
+    x_slot = sems.take(4)
+    back_start(grad_x, grads, x_slot)
+    gain_sum = jnp.sum(one * scaled, axis=1, keepdims=True)
+    bias_sum = jnp.sum(one, axis=1, keepdims=True)
+    lane = lax.broadcasted_iota(jnp.int32, (width, 128), 1)
+    pair = jnp.where(lane == 0, gain_sum, jnp.where(lane == 1, bias_sum, 0.0))
+    pair = jnp.transpose(pair)[0:8]
+    all_small[0] = small[...]
+    all_small[0, 0:2, :] = pair[0:2]
+
+    def spread(sums):
+        row = jnp.concatenate([sums[h : h + 1, 0:64] for h in range(2 * half)], axis=1)
+        none = jnp.zeros_like(row)
+        first_half = jnp.concatenate([row, none], axis=1)
+        second_half = jnp.concatenate([none, row], axis=1)
+        return jnp.where(k == 0, first_half, second_half)
+
+    all_small[0, 9:10, :] = spread(sum_a[...])
+    all_small[0, 10:11, :] = spread(sum_b[...])
+    t_slot = sems.take(3)
+    v_slot = sems.take(2 * rows)
+    remote(sems, all_small.at[0], got_small.at[0], t_slot, sibling)
+    for i in range(half):
+        two_done("q", i)
+        two_done("p", i)
+    arrived(sems, got_small.at[0], t_slot)
+    all_small[1] = all_small[0] + got_small[0]
+    remote(sems, all_small.at[1], got_small.at[1], t_slot + 1, (k, z, near))
+    for name in ("u", "d", "o"):
+        z_done(name)
+    arrived(sems, got_small.at[1], t_slot + 1)
+    all_small[2] = all_small[1] + got_small[1]
+    remote(sems, all_small.at[2], got_small.at[2], t_slot + 2, (k, z, far))
+    arrived(sems, got_small.at[2], t_slot + 2)
+    all_small[3] = all_small[2] + got_small[2]
+    for step in range(1, rows):
+        peer = lax.rem(z + step, rows)
+        remote(FarSems(sems, v_slot + rows + step, v_slot + z), all_small.at[3], got_z.at[z], None, (k, peer, c))
+    z_done("q")
+    z_done("p")
+    total = all_small[3]
+    for step in range(1, rows):
+        source = lax.rem(z + step, rows)
+        arrived(sems, got_z.at[source], v_slot + source)
+        total = total + got_z[source]
+    f_small[...] = total
+    back_done(outs, b_slot)
+    back_done(grads, x_slot)
+    for name in ("u", "d", "o", "q", "p"):
+        last_done(name)
+    drain(sems)
+
+
+class FarSems:
+    def __init__(self, sems, send_slot, recv_slot):
+        self.send = OneSem(sems.send, send_slot)
+        self.recv = OneSem(sems.recv, recv_slot)
+        self.pending = sems.pending
+
+
+class OneSem:
+    def __init__(self, ref, slot):
+        self.ref, self.slot = ref, slot
+
+    @property
+    def at(self):
+        return self
+
+    def __getitem__(self, _):
+        return self.ref.at[self.slot]
+
+
+def final_kernel(
+    outs, grads, f_q, f_p, f_o, f_u, f_d, f_small,
+    output, grad_tokens, g1, b1, q_w, c_b, p_b, p_w, o_w, g2, b2, u_w, u_b, d_w, d_b,
+):
+    k, z, c, _, _ = place()
+    for b in range(2):
+        for core in range(2):
+            size = outs.shape[3]
+            output[b, :, core * size : core * size + size] = outs[b, core].astype(F32)
+            grad_tokens[b, :, core * size : core * size + size] = grads[b, core].astype(F32)
+    for ref, source in ((q_w, f_q), (p_w, f_p), (o_w, f_o), (u_w, f_u), (d_w, f_d)):
+        size = ref.shape[1]
+
+        @pl.when(k == 0)
+        def _(ref=ref, source=source, size=size):
+            ref[...] = source[:, 0:size]
+
+        @pl.when(k == 1)
+        def _(ref=ref, source=source, size=size):
+            ref[...] = source[:, size : 2 * size]
+
+    width = f_small.shape[1]
+    chip = z * 4 + c
+    share = g1.shape[1]
+    first = pltpu.roll(f_small[0:8, :], lax.rem(width - (chip * 2 + k) * share, width), 1)
+    for row, ref in ((0, g1), (1, b1), (2, g2), (3, b2), (4, d_b)):
+        ref[...] = first[row : row + 1, 0:share]
+    share = u_b.shape[1]
+    line = f_small[pl.ds(5 + z, 1), :]
+    line = jnp.broadcast_to(line, (8, width))
+    u_b[...] = pltpu.roll(line, lax.rem(width - (c * 2 + k) * share, width), 1)[0:1, 0:share]
+    heads, share = c_b.shape
+    third = pltpu.roll(f_small[8:16, :], lax.rem(2 * width - heads * 64 * z - (c * 2 + k) * share, width), 1)
+    for h in range(heads):
+        c_b[h : h + 1, :] = third[1:2, h * 64 : h * 64 + share]
+        p_b[h : h + 1, :] = third[2:3, h * 64 : h * 64 + share]
+
+
+def position_table(seq_len, feature_count):
+    positions = np.arange(seq_len, dtype=np.float64)
+    exponent = -np.arange(0, feature_count, 2, dtype=np.float64) / feature_count
+    angles = positions[:, None] * (10000.0**exponent)[None, :]
+    return np.concatenate([np.cos(angles), np.sin(angles)], axis=1).astype(jnp.bfloat16)
+
+
+def fast_shards(
+    tokens, cotangent, piece_starts, ln1_gain, ln1_bias, qkv_weight, content_bias, position_bias, pos_weight,
+    out_weight, ln2_gain, ln2_bias, up_weight, up_bias, down_weight, down_bias,
+):
+    rows, cols = lax.axis_size("row"), lax.axis_size("col")
+    half = rows // 2
+    micro, feat, seq = tokens.shape
+    width = feat * cols
+    count = seq // 2
+    hidden = up_weight.shape[1]
+    heads = content_bias.shape[0] * half
+    table = jnp.asarray(position_table(seq, width))
+    lines = [v.astype(F32)[None] for v in (ln1_gain, ln1_bias, ln2_gain, ln2_bias, down_bias)]
+    small_col = jnp.concatenate(lines + [jnp.zeros((3, feat), F32)], axis=0)
+    small_row = jnp.concatenate(
+        [up_bias.astype(F32).reshape(-1, 128), content_bias.reshape(1, 128), position_bias.reshape(1, 128), jnp.zeros((2, 128), F32)],
+        axis=0,
+    )
+    flat = jnp.pad(piece_starts.reshape(-1), (0, 4))
+    starts = jnp.broadcast_to(flat[:, None], (8, 128))
+    vm = pl.BlockSpec(memory_space=pltpu.VMEM)
+    anywhere = pl.BlockSpec(memory_space=pl.ANY)
+    limit = 64 * 1024 * 1024 - 128 * 1024
+
+    def shape(dims, kind=BF16):
+        return jax.ShapeDtypeStruct(dims, kind)
+
+    made = pl.pallas_call(
+        forward_kernel,
+        name="forward",
+        out_shape=(
+            shape((count, width)),
+            shape((cols, width, 128)),
+            shape((rows, width, hidden)),
+            shape((cols, rows * hidden, 128)),
+            shape((half, width, qkv_weight.shape[1])),
+            shape((half, width, pos_weight.shape[1])),
+            shape((width, seq)),
+            shape((width, count)),
+            shape((width, seq)),
+            shape((heads, seq, width + 128)),
+            shape((heads, seq, 128)),
+            shape((heads, seq, 64)),
+            shape((heads, seq, 64)),
+            shape((heads, seq, seq)),
+            shape((heads, seq, 64), F32),
+            shape((cols, 8, 128), F32),
+            shape((rows, 8, 128), F32),
+        ),
+        in_specs=[anywhere, anywhere, vm, vm, vm, vm] + [anywhere] * 5,
+        out_specs=(vm,) * 17,
+        scratch_shapes=[
+            pltpu.VMEM((seq, width + 128), BF16),
+            pltpu.VMEM((seq, heads * 64), BF16),
+            pltpu.VMEM((8, 128), jnp.int32),
+            pltpu.SemaphoreType.DMA((200,)),
+            pltpu.SemaphoreType.DMA((200,)),
+        ],
+        compiler_params=pltpu.CompilerParams(collective_id=0, has_side_effects=True, vmem_limit_bytes=limit),
+    )(tokens, cotangent, starts, small_col, small_row, table, qkv_weight, pos_weight, out_weight, up_weight, down_weight)
+    (att, wo_all, wu_all, wd_all, wq_half, wp_half, xt, ct, normed_t, qcat, keys, vals, qv, probs, heads_out, params_col, params_row) = made
+    out_t, grad_mid_t, grad_att, g_up, g_down, g_out, small = pl.pallas_call(
+        middle_kernel,
+        name="middle",
+        out_shape=(
+            shape((width, count)),
+            shape((width, count), F32),
+            shape((count, width)),
+            shape(wu_all.shape),
+            shape(wd_all.shape),
+            shape(wo_all.shape),
+            shape((16, width), F32),
+        ),
+        in_specs=[vm] * 8,
+        out_specs=(vm,) * 7,
+        scratch_shapes=[
+            pltpu.VMEM((count, width), F32),
+            pltpu.VMEM((count, width), BF16),
+            pltpu.VMEM((count, width), F32),
+            pltpu.VMEM((count, 1), F32),
+            pltpu.VMEM((count, width), BF16),
+            pltpu.VMEM((count, width), F32),
+            pltpu.VMEM((count, width), F32),
+            pltpu.VMEM((width, count), BF16),
+        ],
+        compiler_params=pltpu.CompilerParams(vmem_limit_bytes=limit),
+    )(att, wo_all, wu_all, wd_all, xt, ct, params_col, params_row)
+    q_cols, p_cols = qkv_weight.shape[1], pos_weight.shape[1]
+    o_rows, d_rows = out_weight.shape[0], down_weight.shape[0]
+    blocks = {
+        "q": (feat, q_cols), "p": (feat, p_cols), "o": (o_rows, 128), "u": (feat, hidden), "d": (d_rows, 128),
+    }
+    names = ("q", "p", "o", "u", "d")
+    results = pl.pallas_call(
+        backward_kernel,
+        name="backward",
+        out_shape=(
+            shape((micro, 2, feat, count)),
+            shape((micro, 2, feat, count)),
+        )
+        + tuple(shape(blocks[name], F32) for name in names)
+        + (shape((16, width), F32),),
+        in_specs=[vm] * 19,
+        out_specs=(vm,) * 8,
+        scratch_shapes=[
+            pltpu.VMEM((seq, width + 128), BF16),
+            pltpu.VMEM((seq, heads * 64), BF16),
+            pltpu.VMEM((heads, seq, 64), BF16),
+            pltpu.VMEM((half, q_cols, seq), BF16),
+            pltpu.VMEM((64, seq), F32),
+            pltpu.VMEM((64, seq), F32),
+            pltpu.VMEM((64, width), F32),
+            pltpu.VMEM((width, seq), F32),
+            pltpu.VMEM((width, count), BF16),
+            pltpu.VMEM((width, count), BF16),
+            pltpu.VMEM((width, count), BF16),
+            pltpu.VMEM((8, 128), F32),
+            pltpu.VMEM((8, 128), F32),
+            pltpu.VMEM((half, cols) + blocks["q"], BF16),
+            pltpu.VMEM((half, cols) + blocks["p"], BF16),
+            pltpu.VMEM((cols, half) + blocks["o"], BF16),
+            pltpu.VMEM((half, cols) + blocks["u"], BF16),
+            pltpu.VMEM((cols, half) + blocks["d"], BF16),
+            pltpu.VMEM((cols, half * o_rows, 128), BF16),
+            pltpu.VMEM((half, width, hidden), BF16),
+            pltpu.VMEM((cols, half * d_rows, 128), BF16),
+        ]
+        + [pltpu.VMEM((half, 2) + blocks[name], BF16) for name in names]
+        + [pltpu.VMEM((half,) + blocks[name], BF16) for name in names]
+        + [pltpu.VMEM((rows,) + blocks[name], BF16) for name in names]
+        + [
+            pltpu.VMEM((4, 16, width), F32),
+            pltpu.VMEM((3, 16, width), F32),
+            pltpu.VMEM((rows, 16, width), F32),
+            pltpu.SemaphoreType.DMA((160,)),
+            pltpu.SemaphoreType.DMA((160,)),
+        ],
+        compiler_params=pltpu.CompilerParams(collective_id=1, has_side_effects=True, vmem_limit_bytes=limit),
+    )(
+        out_t, grad_mid_t, grad_att, g_up, g_down, g_out, small, params_col, table, wq_half, wp_half, xt, normed_t,
+        qcat, keys, vals, qv, probs, heads_out,
+    )
+    devices = 2 * rows * cols
+    vec = shape((1, width // devices), F32)
+    bias = shape((content_bias.shape[0], 64 // (2 * cols)), F32)
+    done = pl.pallas_call(
+        final_kernel,
+        name="final",
+        out_shape=(
+            shape(tokens.shape, F32), shape(tokens.shape, F32), vec, vec,
+            shape((feat, q_cols // 2), F32), bias, bias, shape((feat, p_cols // 2), F32), shape((o_rows, 64), F32), vec, vec,
+            shape((feat, hidden // 2), F32), shape((1, rows * hidden // devices), F32), shape((d_rows, 64), F32), vec,
+        ),
+        in_specs=[vm] * 8,
+        out_specs=(vm,) * 15,
+        compiler_params=pltpu.CompilerParams(vmem_limit_bytes=limit),
+    )(*results)
+    return tuple(v.reshape(-1) if v.shape[0] == 1 else v for v in done)
+
+
 def solution(mesh):
     in_specs = (
         P(None, "col", ("dp", "row")),
@@ -558,4 +1615,12 @@
         P("row", ("col", "dp")),
         P(("row", "col", "dp")),
     )
-    return jax.shard_map(shards, mesh=mesh, in_specs=in_specs, out_specs=out_specs, check_vma=False)
+
+    def layer(tokens, *others):
+        dp, row, col = mesh.shape["dp"], mesh.shape["row"], mesh.shape["col"]
+        one_each = tokens.shape[2] == dp * row * SEQ_LEN and tokens.shape[0] * dp == col
+        body = fast_shards if one_each and dp == 2 and row == col == 4 else shards
+        part = jax.shard_map(body, mesh=mesh, in_specs=in_specs, out_specs=out_specs, check_vma=False)
+        return part(tokens, *others)
+
+    return layer

time: 2570 us -> 188 us (0.07)
  waiting for transfers between devices: 1430 us -> 0 us
  local copies, waits for them, and re-layouts: 550 us -> 9.91 us
  matrix products: 215 us -> 0 us
  Pallas kernels: 0 us -> 172 us
  blocking collectives: 150 us -> 0 us
  loops' own time: 111 us -> 0 us
  other arithmetic: 84.4 us -> 4.69 us
    reduce_scatter x22 -> x0, waiting for transfers between devices: 898 us -> none  [the longest x8 474 us: sum_over_cols(): lax.psum_scatter(partial_term(jnp.int32(0), lax.axis_size('col') * share_...]
    all_gather x16 -> x0, waiting for transfers between devices: 489 us -> none  [the longest x8 307 us: gather_cols(): return lax.all_gather(values, 'col', axis=0, tiled=True)]
    reshape x24 -> x3, local copies, waits for them, and re-layouts: 272 us -> 1.6 us  [the longest x1 0.76 us: fast_shards(): content_bias.reshape(1, 128)]
    dot_general x71 -> x0, matrix products: 215 us -> none  [the longest x8 36.7 us: contract(): return jnp.dot(left_op, right_op, preferred_element_type=jnp.float32)]
    pallas_call x0 -> x4, Pallas kernels: none -> 172 us  [the longest x1 79.7 us: fast_shards(): pl.pallas_call(forward_kernel, name='forward', out_shape=(shape((count, w...]
    another operation x4 -> x0, loops' own time: 111 us -> none  [the longest x2 67.9 us: attention_backward(): lax.scan(back_block, (zero_rows, zero_rows, zero_rel), (offsets, log_tota...]
    slice x10 -> x0, local copies, waits for them, and re-layouts: 83.6 us -> none  [the longest x8 81.4 us: skew_rows(): lax.slice_in_dim(flattened, row_total - 1, row_total - 1 + row_total * (r...]
    unnamed x2 -> x0, blocking collectives: 78.5 us -> none
  transfers between devices with their start and end apart: 44 -> 0, of which waited for: 39 -> 0; matrix products, arithmetic and copies ran while one was open for 19% -> 0% of each run, Pallas kernels for 0% -> 0%
where the time goes in v1:
time: 188 us; the launch traced here: 187 us
  Pallas kernels  172 us (91%)
  local copies, waits for them, and re-layouts  9.91 us (5%)
  other arithmetic  4.69 us (2%)
    pallas_call x1, Pallas kernels, fast_shards(): pl.pallas_call(forward_kernel, name='forward', out_shape=(shape((count, w...  79.7 us
    pallas_call x1, Pallas kernels, fast_shards(): pl.pallas_call(backward_kernel, name='backward', out_shape=(shape((micro,...  74.5 us
    pallas_call x1, Pallas kernels, fast_shards(): pl.pallas_call(middle_kernel, name='middle', out_shape=(shape((width, cou...  14.5 us
    unnamed x5, local copies, waits for them, and re-layouts  6.95 us

profile of v1, /device:TPU:0, one launch (start us, length us, event | category | flops | bytes accessed | tf_op | source)
XLA Modules:
  0.0 187.1 jit_solution(5519505042232730069)
XLA Ops:
  0.6 0.5 broadcast.8
  1.2 1.3 reduce.3
  2.5 0.1 reshape.64
  2.6 0.7 bitcast_convert_fusion.5
  3.2 0.8 reshape.67
  4.0 0.8 reshape.68
  4.8 0.1 pad.8.clone
  4.8 0.7 bitcast_convert_fusion.3
  5.5 0.7 bitcast_convert_fusion.1
  6.2 0.7 bitcast_convert_fusion
  6.9 0.7 maximum_maximum_fusion.small_row
  7.5 0.6 concatenate.6.small_col
  8.2 0.7 broadcast_in_dim.42.starts
  8.8 79.7 %forward.1 = (bf16[512,512]{1,0:T(8,128)(2,1)}, bf16[4,512,128]{2,1,0:T(8,128)(2,1)}, bf16[4,512,512]{2,1,0:T(8,128)(2,1)}, bf16[4,2048,128]{2,1,0:T(8,128)(2,1)...) custom-call(bf16[2,128,1024]{2,1,0:T(8,128)(2,1)} %tok.1, ...), custom_call_target="tpu_custom_call" | custom-call | tf_op jit(solution)/shard_map/forward/pallas_call | solution.py:1449
  88.5 14.5 %middle.1 = (bf16[512,512]{1,0:T(8,128)(2,1)}, f32[512,512]{1,0:T(8,128)}, bf16[512,512]{1,0:T(8,128)(2,1)}, bf16[4,512,512]{2,1,0:T(8,128)(2,1)}, bf16[4,2048,1...) custom-call(bf16[512,512]{1,0:T(8,128)(2,1)} %get-tuple-element.62.att, ...), custom_call_target="tpu_custom_call" | custom-call | tf_op jit(solution)/shard_map/middle/pallas_call | solution.py:1483
  103.0 74.5 %backward.1 = (bf16[2,2,128,512]{3,2,1,0:T(8,128)(2,1)}, bf16[2,2,128,512]{3,2,1,0:T(8,128)(2,1)}, f32[128,384]{1,0:T(8,128)}, f32[128,128]{1,0:T(8,128)}, f32[1...) custom-call(bf16[512,512]{1,0:T(8,128)(2,1)} %get-tuple-element.70.out_t, ...), custom_call_target="tpu_custom_call" | custom-call | tf_op jit(solution)/shard_map/backward/pallas_call | solution.py:1515
  177.5 3.2 %final.1 = (f32[2,128,1024]{2,1,0:T(8,128)}, f32[2,128,1024]{2,1,0:T(8,128)}, f32[1,16]{1,0:T(1,128)}, f32[1,16]{1,0:T(1,128)}, f32[128,192]{1,0:T(8,128)}, /*in...) custom-call(bf16[2,2,128,512]{3,2,1,0:T(8,128)(2,1)} %get-tuple-elem, ...), custom_call_target="tpu_custom_call" | custom-call | tf_op jit(solution)/shard_map/final/pallas_call | solution.py:1567
  180.7 1.5 copy.33
  182.2 1.5 copy.34
  183.8 1.6 copy.32
  185.4 1.7 copy.35
  (3 shorter events, 0.0 us)

commit v2 on v0

--- a/solution.py
+++ b/solution.py
@@ -2,7 +2,10 @@
 
 import jax
 import jax.numpy as jnp
+import numpy as np
 from jax import lax
+from jax.experimental import pallas as pl
+from jax.experimental.pallas import tpu as pltpu
 from jax.sharding import PartitionSpec as P
 
 D = 512
@@ -522,6 +525,1011 @@
     )
 
 
+MESH = pl.DeviceIdType.MESH
+F32 = jnp.float32
+BF16 = jnp.bfloat16
+
+
+def aligned(index, size):
+    return index if isinstance(index, int) else pl.multiple_of(index, size)
+
+
+def nt(a, b):
+    return lax.dot_general(a, b, (((1,), (1,)), ((), ())), preferred_element_type=F32)
+
+
+def nn(a, b):
+    return lax.dot_general(a, b, (((1,), (0,)), ((), ())), preferred_element_type=F32)
+
+
+def tn(a, b):
+    return lax.dot_general(a, b, (((0,), (0,)), ((), ())), preferred_element_type=F32)
+
+
+def place():
+    k, z, c = lax.axis_index("dp"), lax.axis_index("row"), lax.axis_index("col")
+    cx = c + 1 - 2 * lax.rem(c, 2)
+    cy = lax.rem(c + 2, 4)
+    near = (1 - k) * cx + k * cy
+    far = k * cx + (1 - k) * cy
+    return k, z, c, near, far
+
+
+def enter(rows):
+    k, z, c, _, _ = place()
+    barrier = pltpu.get_barrier_semaphore()
+    peers = [(1 - k, z, c)]
+    for step in range(1, rows):
+        peers.append((k, lax.rem(z + step, rows), c))
+    for step in range(1, 4):
+        for core in range(2):
+            peers.append((0 * k + core, z, lax.rem(c + step, 4)))
+    for peer in peers:
+        pl.semaphore_signal(barrier, inc=1, device_id=peer, device_id_type=MESH)
+    pl.semaphore_wait(barrier, len(peers))
+
+
+class Copies:
+    def __init__(self, send, recv):
+        self.send, self.recv, self.next = send, recv, 0
+        self.pending = {}
+
+    def take(self, count=1):
+        first = self.next
+        self.next += count
+        return first
+
+    def push(self, send_slot, build, when=None):
+        def copy():
+            src, dst, recv_slot, peer = build()
+            return pltpu.make_async_remote_copy(
+                src, dst, self.send.at[send_slot], self.recv.at[recv_slot], device_id=peer, device_id_type=MESH
+            )
+
+        if when is None:
+            copy().start()
+        else:
+            pl.when(when())(lambda: copy().start())
+        self.pending[send_slot] = (copy, when)
+
+    def keep(self, src, dst, slot, when=None):
+        def go():
+            pltpu.make_async_copy(src(), dst(), self.recv.at[slot]).start()
+
+        if when is None:
+            go()
+        else:
+            pl.when(when())(go)
+
+    def arrived(self, dst, slot):
+        pltpu.make_async_copy(dst, dst, self.recv.at[slot]).wait()
+
+    def drain(self):
+        for copy, when in self.pending.values():
+            if when is None:
+                copy().wait_send()
+            else:
+                pl.when(when())(lambda copy=copy: copy().wait_send())
+
+
+def tall(row):
+    padded = jnp.concatenate([row, jnp.zeros((120, 128), F32)], axis=0)
+    return jnp.transpose(padded)
+
+
+def erf_parts(values):
+    erf = lax.erf(values * inv_sqrt_two)
+    return 0.5 * (1.0 + erf)
+
+
+def layer_kernel(
+    tok, cot, starts, packed, cbias, pbias, table, wq, wp, wo, wu, wd,
+    outs, grads, f_q, f_p, f_o, f_u, f_d, f_small,
+    att, wo_all, wu_all, wd_all, wq_half, wp_half, wp_head, xt, ct, normed_t, qcat, keys, vals, probs_a, probs_b, heads_out,
+    params_col, params_row, cb_all, pb_all, kcat, own_att, starts_got,
+    mid, norm, hat, inv, gout, acc_out, acc_two, tall_norm, out_t, grad_mid_t, grad_att, g_up, g_down, g_out, small,
+    grad_o, head_grad, turned, turned_k, turned_v, turned_p, one_t, one_low, one_got, grad_x, sums,
+    hs_q, hs_p, hs_o, hs_u, hs_d, r0_o, r0_u, r0_d,
+    r1_q, r1_p, r1_o, r1_u, r1_d, r2_q, r2_p, r2_o, r2_u, r2_d, r3_q, r3_p, r3_o, r3_u, r3_d,
+    all_small, got_small, got_z, send, recv,
+):
+    rows = wu_all.shape[0]
+    cols = wo_all.shape[0]
+    half = rows // 2
+    heads = 2 * half
+    k, z, c, near, far = place()
+    opposite = 3 - c
+    sibling = (1 - k, z, c)
+    io = Copies(send, recv)
+    mine = lax.div(z, half) == k
+    arrived = io.arrived
+    enter(rows)
+
+    def q_block(cc):
+        return wq_half.at[:, pl.ds(aligned(cc * 128, 128), 128), :]
+
+    def p_block(cc):
+        return wp_half.at[:, pl.ds(aligned(cc * 128, 128), 128), :]
+
+    def u_block(cc, core=k):
+        return wu_all.at[pl.ds(core * half, half), pl.ds(aligned(cc * 128, 128), 128), :]
+
+    def o_block(cc, core=k):
+        size = wo_all.shape[1] // 2
+        return wo_all.at[cc, pl.ds(aligned(core * size, 128), size), :]
+
+    def d_block(cc, core=k):
+        size = wd_all.shape[1] // 2
+        return wd_all.at[cc, pl.ds(aligned(core * size, 128), size), :]
+
+    def q_one(i):
+        return wq_half.at[i, pl.ds(aligned(c * 128, 128), 128), :]
+
+    def p_one(i):
+        return wp_half.at[i, pl.ds(aligned(c * 128, 128), 128), :]
+
+    def u_one(i):
+        return wu_all.at[k * half + i, pl.ds(aligned(c * 128, 128), 128), :]
+
+    def o_one(i):
+        size = wo_all.shape[1] // rows
+        return wo_all.at[c, pl.ds(aligned((k * half + i) * size, 128), size), :]
+
+    def d_one(i):
+        size = wd_all.shape[1] // rows
+        return wd_all.at[c, pl.ds(aligned((k * half + i) * size, 128), size), :]
+
+    weights = {
+        "q": (wq, q_one, q_block), "p": (wp, p_one, p_block), "o": (wo, o_one, o_block),
+        "u": (wu, u_one, u_block), "d": (wd, d_one, d_block),
+    }
+    z_slot = {name: io.take(half) for name in weights}
+    z_send = {name: io.take(half * rows) for name in weights}
+    near_slot = {name: io.take(1) for name in weights}
+    far_slot = {name: io.take(2) for name in weights}
+    sib_slot = {name: io.take(4) for name in weights}
+
+    def z_start(name):
+        ref, one, _ = weights[name]
+        for i in range(half):
+            slot = z_slot[name] + i
+
+            def here(i=i):
+                return z == k * half + i
+
+            io.keep(lambda: ref, lambda i=i: one(i), slot, here)
+            for step in range(1, rows):
+                io.push(
+                    z_send[name] + i * rows + step,
+                    lambda i=i, step=step, slot=slot: (ref, one(i), slot, (k, lax.rem(z + step, rows), c)),
+                    here,
+                )
+
+    def z_done(name):
+        _, one, _ = weights[name]
+        for i in range(half):
+            arrived(one(i), z_slot[name] + i)
+
+    def near_start(name):
+        block = weights[name][2]
+        io.push(near_slot[name], lambda: (block(c), block(c), near_slot[name], (k, z, near)))
+
+    def near_done(name):
+        arrived(weights[name][2](near), near_slot[name])
+
+    def far_start(name):
+        block = weights[name][2]
+        io.push(far_slot[name], lambda: (block(c), block(c), far_slot[name], (k, z, far)))
+        io.push(far_slot[name] + 1, lambda: (block(near), block(near), far_slot[name] + 1, (k, z, far)))
+
+    def far_done(name):
+        block = weights[name][2]
+        arrived(block(far), far_slot[name])
+        arrived(block(3 - c), far_slot[name] + 1)
+
+    def sib_start(name):
+        block = weights[name][2]
+        for cc in range(4):
+            slot = sib_slot[name] + cc
+            io.push(slot, lambda cc=cc, slot=slot: (block(cc), block(cc), slot, (1 - k, z, c)))
+
+    def sib_done(name):
+        block = weights[name][2]
+        for cc in range(4):
+            arrived(block(cc, 1 - k), sib_slot[name] + cc)
+
+    feat = tok.shape[1]
+    x_slot = io.take(4)
+    x_send = io.take(4)
+    xf_slot = io.take(4)
+
+    def x_part(cc, core):
+        return xt.at[pl.ds(aligned(cc * feat + core * (feat // 2), 64), feat // 2), :]
+
+    def is_local(b, core):
+        return jnp.logical_and(2 * b + k == c, core == k)
+
+    z_start("q")
+    for b in range(2):
+        for core in range(2):
+
+            def src(b=b, core=core):
+                return tok.at[b, pl.ds(core * (feat // 2), feat // 2), :]
+
+            def dst(core=core):
+                return x_part(c, core)
+
+            io.keep(src, dst, x_slot + c, lambda b=b, core=core: is_local(b, core))
+            io.push(
+                x_send + 2 * b + core,
+                lambda src=src, dst=dst, b=b, core=core: (src(), dst(), x_slot + c, (0 * k + core, z, 2 * b + k)),
+                lambda b=b, core=core: jnp.logical_not(is_local(b, core)),
+            )
+    z_start("p")
+
+    t_slot = io.take(1)
+    io.keep(lambda: table, lambda: kcat.at[:, pl.ds(0, table.shape[1])], t_slot)
+    g_col = io.take(4)
+    g_row = io.take(rows)
+    g_cb = io.take(rows)
+    g_pb = io.take(rows)
+    for step in range(1, 4):
+        io.push(
+            g_col + step,
+            lambda step=step: (packed.at[pl.ds(0, 8)], params_col.at[c], g_col, (k, z, lax.rem(c + step, 4))),
+        )
+    io.keep(lambda: packed.at[pl.ds(0, 8)], lambda: params_col.at[c], g_col)
+    for source, target, slot in ((packed.at[pl.ds(8, 8)], params_row, g_row), (cbias, cb_all, g_cb), (pbias, pb_all, g_pb)):
+        for step in range(1, rows):
+            io.push(
+                slot + step,
+                lambda step=step, source=source, target=target, slot=slot: (
+                    source, target.at[z], slot, (k, lax.rem(z + step, rows), c)
+                ),
+            )
+        io.keep(lambda source=source: source, lambda target=target: target.at[z], slot)
+    s_slot = io.take(1)
+    s_send = io.take(4)
+    for b in range(2):
+        for core in range(2):
+            io.keep(
+                lambda: starts, lambda: starts_got, s_slot,
+                lambda b=b, core=core: jnp.logical_and(c == z, is_local(b, core)),
+            )
+            io.push(
+                s_send + 2 * b + core,
+                lambda b=b, core=core: (starts, starts_got, s_slot, (0 * k + core, z, 2 * b + k)),
+                lambda b=b, core=core: jnp.logical_and(c == z, jnp.logical_not(is_local(b, core))),
+            )
+    for name in ("o", "u", "d"):
+        z_start(name)
+
+    c_slot = io.take(4)
+    c_send = io.take(4)
+    count = ct.shape[1]
+
+    def cot_start():
+        for b in range(2):
+            for core in range(2):
+
+                def src(b=b, core=core):
+                    return cot.at[b, :, pl.ds(core * count, count)]
+
+                def dst():
+                    return ct.at[pl.ds(aligned(c * feat, 128), feat), :]
+
+                io.keep(src, dst, c_slot + c, lambda b=b, core=core: is_local(b, core))
+                io.push(
+                    c_send + 2 * b + core,
+                    lambda src=src, dst=dst, b=b, core=core: (src(), dst(), c_slot + c, (0 * k + core, z, 2 * b + k)),
+                    lambda b=b, core=core: jnp.logical_not(is_local(b, core)),
+                )
+
+    for cc in range(4):
+        arrived(x_part(cc, k), x_slot + cc)
+        io.push(xf_slot + cc, lambda cc=cc: (x_part(cc, k), x_part(cc, k), xf_slot + cc, sibling))
+    z_done("q")
+    near_start("q")
+    z_done("p")
+    near_start("p")
+    arrived(params_col, g_col)
+    arrived(params_row, g_row)
+    arrived(cb_all, g_cb)
+    arrived(pb_all, g_pb)
+    arrived(starts_got, s_slot)
+    for cc in range(4):
+        arrived(x_part(cc, 1 - k), xf_slot + cc)
+
+    columns = [tall(params_col[cc]) for cc in range(4)]
+    gain = jnp.concatenate([col[:, 0:1] for col in columns], axis=0)
+    bias = jnp.concatenate([col[:, 1:2] for col in columns], axis=0)
+    width = xt.shape[0]
+    seq = xt.shape[1]
+    piece = PIECE
+    blocks = seq // 256
+
+    @pl.loop(0, blocks)
+    def _(t):
+        here = pl.ds(aligned(t * 256, 256), 256)
+        x = xt[:, here].astype(F32)
+        mean = jnp.sum(x, axis=0, keepdims=True) * (1.0 / width)
+        square = jnp.sum(x * x, axis=0, keepdims=True) * (1.0 / width)
+        inverse = lax.rsqrt(square - mean * mean + norm_epsilon)
+        normed_t[:, here] = ((x - mean) * inverse * gain + bias).astype(BF16)
+
+    near_done("q")
+    far_start("q")
+    near_done("p")
+    far_start("p")
+    cot_start()
+    z_done("o")
+    near_start("o")
+    z_done("u")
+    near_start("u")
+    far_done("q")
+    scale = 0.125
+    none = jnp.zeros((256, 64), F32)
+
+    @pl.loop(0, half * blocks)
+    def _(n):
+        i, t = lax.div(n, blocks), lax.rem(n, blocks)
+        here = pl.ds(aligned(t * 256, 256), 256)
+        got = tn(normed_t[:, here], wq_half[i])
+        for hb in range(2):
+            h = 2 * i + hb
+            low = got[:, hb * 192 : hb * 192 + 192].astype(BF16).astype(F32)
+            query, key, value = low[:, 0:64], low[:, 64:128], low[:, 128:192]
+            content = cb_all[k * half + i, hb : hb + 1, :]
+            position = pb_all[k * half + i, hb : hb + 1, :]
+            qcat[h, here, 512:640] = jnp.concatenate(
+                [(query + content) * scale, (query + position) * scale], axis=1
+            ).astype(BF16)
+            keys[h, here, :] = jnp.concatenate([key, none], axis=1).astype(BF16)
+            vals[h, here, :] = value.astype(BF16)
+
+    z_done("d")
+    near_start("d")
+    far_done("p")
+    arrived(kcat.at[:, pl.ds(0, 512)], t_slot)
+    for h in range(heads):
+        part = wp_half[h // 2, :, (h % 2) * 64 : (h % 2) * 64 + 64]
+        wp_head[h] = jnp.concatenate([jnp.zeros_like(part), part], axis=1)
+
+    @pl.loop(0, heads * blocks)
+    def _(n):
+        h, t = lax.div(n, blocks), lax.rem(n, blocks)
+        here = pl.ds(aligned(t * 256, 256), 256)
+        angle = nt(qcat[h, here, 512:640], wp_head[h])
+        cosine = kcat[here, 0:256].astype(F32)
+        sine = kcat[here, 256:512].astype(F32)
+        first, second = angle[:, 0:256], angle[:, 256:512]
+        qcat[h, here, 0:256] = (first * sine + second * cosine).astype(BF16)
+        qcat[h, here, 256:512] = (second * sine - first * cosine).astype(BF16)
+
+    slot_len = seq // 2
+    block = 256
+    batch = lax.div(c, 2)
+
+    def attend(h, low_row, keys_seen, slot):
+        start = starts_got[batch, 0:1, slot : slot + 1]
+        row = slot * slot_len + low_row + lax.broadcasted_iota(jnp.int32, (block, 1), 0)
+        inside = jnp.logical_and(row >= start, row < start + piece)
+        limit = jnp.where(inside, start + (piece - 1), row)
+        here = pl.ds(aligned(slot * slot_len + low_row, block), block)
+        scores = nt(qcat[h, here, :], kcat[0:keys_seen, :])
+        column = slot * slot_len + lax.broadcasted_iota(jnp.int32, (block, slot_len), 1)
+        last = jnp.where(column <= limit, scores[:, keys_seen - slot_len :], big_negative)
+        top = jnp.max(last, axis=1, keepdims=True)
+        if slot == 1:
+            top = jnp.maximum(top, jnp.max(scores[:, :slot_len], axis=1, keepdims=True))
+        last = jnp.exp(last - top)
+        total = jnp.sum(last, axis=1, keepdims=True)
+        if slot == 1:
+            first = jnp.exp(scores[:, :slot_len] - top)
+            total = total + jnp.sum(first, axis=1, keepdims=True)
+            whole = jnp.concatenate([first, last], axis=1)
+        else:
+            whole = last
+        low = (whole * (1.0 / total)).astype(BF16)
+        probs = (probs_a, probs_b)[slot]
+        probs[h, pl.ds(aligned(low_row, block), block), :] = low
+        heads_out[h, here, :] = nn(low, vals[h, 0:keys_seen, :]).astype(BF16)
+
+    def stage_zero():
+        near_done("o")
+        far_start("o")
+        near_done("u")
+        far_start("u")
+
+    def stage_one():
+        near_done("d")
+        far_start("d")
+        far_done("o")
+        sib_start("o")
+
+    def stage_two():
+        far_done("u")
+        sib_start("u")
+
+    @pl.loop(0, heads)
+    def _(h):
+        kcat[:, 512:640] = keys[h]
+
+        @pl.loop(0, slot_len // block)
+        def _(t):
+            attend(h, t * block, slot_len, 0)
+
+        @pl.loop(0, slot_len // block)
+        def _(t):
+            attend(h, t * block, seq, 1)
+
+        for number, stage in enumerate((stage_zero, stage_one, stage_two)):
+            pl.when(h == number)(stage)
+
+    own_att[...] = jnp.concatenate([heads_out[h] for h in range(heads)], axis=1)
+    a_slot = io.take(2)
+    span = own_att.shape[1]
+    other = pl.ds(aligned((1 - k) * count, count), count)
+    own = pl.ds(aligned(k * count, count), count)
+    att_part = att.at[:, pl.ds(aligned(k * span, 128), span)]
+    io.push(a_slot, lambda: (own_att.at[other, :], att_part, a_slot, sibling))
+    io.keep(lambda: own_att.at[own, :], lambda: att_part, a_slot + 1)
+    far_done("d")
+    sib_start("d")
+    for cc in range(4):
+        arrived(ct.at[pl.ds(cc * feat, feat), :], c_slot + cc)
+    gout[...] = jnp.transpose(ct[...])
+    sib_done("o")
+    arrived(own_att.at[own, :], a_slot + 1)
+    arrived(own_att.at[own, :], a_slot)
+
+    def line(index):
+        return jnp.concatenate([params_col[cc, index : index + 1, :] for cc in range(cols)], axis=1)
+
+    def out_weight():
+        return jnp.concatenate([wo_all[cc] for cc in range(cols)], axis=1)
+
+    x = jnp.transpose(xt[:, own].astype(F32))
+    middle = x + nn(att[...], out_weight())
+    mid[...] = middle
+    mean = jnp.sum(middle, axis=1, keepdims=True) * (1.0 / width)
+    square = jnp.sum(middle * middle, axis=1, keepdims=True) * (1.0 / width)
+    inverse = lax.rsqrt(square - mean * mean + norm_epsilon)
+    scaled = (middle - mean) * inverse
+    hat[...] = scaled
+    inv[...] = inverse
+    low = (scaled * line(2) + line(3)).astype(BF16)
+    norm[...] = low
+    tall_norm[...] = jnp.transpose(low)
+    acc_out[...] = jnp.zeros_like(acc_out)
+    acc_two[...] = jnp.zeros_like(acc_two)
+    small[...] = jnp.zeros_like(small)
+    hidden = wu_all.shape[2]
+
+    @pl.loop(0, rows)
+    def _(step):
+        r = lax.rem(k * half + step, rows)
+
+        @pl.when(step == half)
+        def _():
+            for name in ("u", "d"):
+                sib_done(name)
+
+        here = pl.ds(aligned(r * hidden, hidden), hidden)
+        bias = jnp.concatenate([params_row[r, j : j + 1, :] for j in range(hidden // 128)], axis=1)
+        down = jnp.concatenate([wd_all[cc, here, :] for cc in range(cols)], axis=1)
+        pre = nn(norm[...], wu_all[r]) + bias
+        grad_act = nt(gout[...], down)
+        lower = erf_parts(pre)
+        act = (pre * lower).astype(BF16)
+        slope = lower + pre * jnp.exp(-0.5 * pre * pre) * inv_sqrt_tau
+        low_grad = (grad_act * slope).astype(BF16)
+        small[pl.ds(5 + r, 1), :] = jnp.sum(low_grad.astype(F32), axis=0, keepdims=True)
+        acc_out[...] += nn(act, down)
+        acc_two[...] += nt(low_grad, wu_all[r])
+        g_up[r] = nn(tall_norm[...], low_grad).astype(BF16)
+        found = tn(act, gout[...]).astype(BF16)
+        for cc in range(cols):
+            g_down[cc, here, :] = found[:, cc * 128 : cc * 128 + 128]
+
+    hs = {
+        "q": lambda i, cc: hs_q.at[i, cc], "p": lambda i, cc: hs_p.at[i, cc], "u": lambda i, cc: hs_u.at[i, cc],
+        "o": lambda i, cc: hs_o.at[cc, i], "d": lambda i, cc: hs_d.at[cc, i],
+    }
+    r1 = {"q": r1_q, "p": r1_p, "o": r1_o, "u": r1_u, "d": r1_d}
+    r2 = {"q": r2_q, "p": r2_p, "o": r2_o, "u": r2_u, "d": r2_d}
+    r3 = {"q": r3_q, "p": r3_p, "o": r3_o, "u": r3_u, "d": r3_d}
+    final = {"q": f_q, "p": f_p, "o": f_o, "u": f_u, "d": f_d}
+    slots = {}
+    for name in ("o", "u", "d", "q", "p"):
+        slots[name, "sib"] = io.take(1)
+        slots[name, "one"] = io.take(2 * half)
+        slots[name, "two"] = io.take(half)
+        slots[name, "z"] = io.take(rows)
+        slots[name, "last"] = io.take(1)
+
+    def grad_half(name, core):
+        if name == "u":
+            return g_up.at[pl.ds(core * half, half)]
+        full = g_out if name == "o" else g_down
+        size = full.shape[1] // 2
+        return full.at[:, pl.ds(aligned(core * size, 128), size), :]
+
+    got0 = {"u": r0_u, "o": r0_o, "d": r0_d}
+
+    def grad_sib_start(name):
+        slot = slots[name, "sib"]
+        io.push(slot, lambda: (grad_half(name, 1 - k), got0[name], slot, sibling))
+
+    def grad_sib_done(name):
+        arrived(got0[name], slots[name, "sib"])
+        if name == "u":
+            for i in range(half):
+                total = g_up[k * half + i].astype(F32) + r0_u[i].astype(F32)
+                hs_u[i] = total.astype(BF16).reshape(hs_u.shape[1:])
+        else:
+            full = g_out if name == "o" else g_down
+            size = full.shape[1] // 2
+            to = hs_o if name == "o" else hs_d
+            for cc in range(cols):
+                part = full[cc, pl.ds(aligned(k * size, 128), size), :]
+                total = part.astype(F32) + got0[name][cc].astype(F32)
+                to[cc] = total.astype(BF16).reshape(to.shape[1:])
+
+    def one_start(name, i):
+        block = hs[name]
+        slot = slots[name, "one"] + 2 * i
+        io.push(slot, lambda: (block(i, far), r1[name].at[i, 0], slot, (k, z, far)))
+        io.push(slot + 1, lambda: (block(i, 3 - c), r1[name].at[i, 1], slot + 1, (k, z, far)))
+
+    def load(ref):
+        return ref[...].astype(F32)
+
+    def one_done(name, i):
+        block = hs[name]
+        slot = slots[name, "one"] + 2 * i
+        arrived(r1[name].at[i, 1], slot + 1)
+        r1[name][i, 1] = (r1[name][i, 1].astype(F32) + load(block(i, near))).astype(BF16)
+        io.push(
+            slots[name, "two"] + i, lambda: (r1[name].at[i, 1], r2[name].at[i], slots[name, "two"] + i, (k, z, near))
+        )
+        arrived(r1[name].at[i, 0], slot)
+        r1[name][i, 0] = (r1[name][i, 0].astype(F32) + load(block(i, c))).astype(BF16)
+
+    def two_done(name, i):
+        arrived(r2[name].at[i], slots[name, "two"] + i)
+        r2[name][i] = (r2[name][i].astype(F32) + r1[name][i, 0].astype(F32)).astype(BF16)
+        base = slots[name, "z"]
+        io.push(
+            base + i,
+            lambda: (r2[name].at[i], r3[name].at[z], base + z, (k, k * half + i, c)),
+            lambda: z != k * half + i,
+        )
+
+    def grad_z_done(name):
+        base = slots[name, "z"]
+        to = final[name]
+
+        @pl.when(mine)
+        def _():
+            total = r2[name][z - k * half].astype(F32)
+            for step in range(1, rows):
+                source = lax.rem(z + step, rows)
+                arrived(r3[name].at[source], base + source)
+                total = total + r3[name][source].astype(F32)
+            to[...] = total
+
+        slot = slots[name, "last"]
+        io.push(slot, lambda: (to, to, slot, sibling), lambda: mine)
+
+    def last_done(name):
+        @pl.when(jnp.logical_not(mine))
+        def _():
+            arrived(final[name], slots[name, "last"])
+
+    origin = lax.rem(c, 2)
+    b_slot = {"out": io.take(4), "grad": io.take(4)}
+
+    def back_start(src, dst, base):
+        for step in range(4):
+
+            def part(step=step):
+                return src.at[pl.ds(aligned(lax.rem(c + step, 4) * feat, 128), feat), :]
+
+            def landing():
+                return dst.at[batch, k]
+
+            if step == 0:
+                io.keep(part, landing, base + 2 * batch + k, lambda: origin == k)
+                io.push(
+                    base + step,
+                    lambda part=part, landing=landing: (part(), landing(), base + 2 * batch + k, sibling),
+                    lambda: origin != k,
+                )
+            else:
+                io.push(
+                    base + step,
+                    lambda part=part, landing=landing, step=step: (
+                        part(), landing(), base + 2 * batch + k, (origin, z, lax.rem(c + step, 4))
+                    ),
+                )
+
+    def back_done(dst, base):
+        for b in range(2):
+            for core in range(2):
+                arrived(dst.at[b, core], base + 2 * b + core)
+
+    for name in ("u", "d"):
+        grad_sib_start(name)
+    cotangent = gout[...].astype(F32)
+    out_t[...] = jnp.transpose(mid[...] + acc_out[...] + line(4)).astype(BF16)
+    back_start(out_t, outs, b_slot["out"])
+    two = acc_two[...]
+    small[2:3, :] = jnp.sum(two * hat[...], axis=0, keepdims=True)
+    small[3:4, :] = jnp.sum(two, axis=0, keepdims=True)
+    small[4:5, :] = jnp.sum(cotangent, axis=0, keepdims=True)
+    shifted = two * line(2)
+    first = jnp.sum(shifted, axis=1, keepdims=True) * (1.0 / width)
+    second = jnp.sum(shifted * hat[...], axis=1, keepdims=True) * (1.0 / width)
+    grad_mid = cotangent + inv[...] * (shifted - first - hat[...] * second)
+    branch = grad_mid.astype(BF16)
+    grad_att[...] = nt(branch, out_weight()).astype(BF16)
+    e_slot = io.take(2)
+    io.push(
+        e_slot,
+        lambda: (grad_att.at[:, pl.ds(aligned((1 - k) * span, 128), span)], grad_o.at[own, :], e_slot, sibling),
+    )
+    io.keep(
+        lambda: grad_att.at[:, pl.ds(aligned(k * span, 128), span)], lambda: grad_o.at[own, :], e_slot + 1
+    )
+    grad_mid_t[...] = jnp.transpose(grad_mid)
+    found = tn(att[...], branch).astype(BF16)
+    for cc in range(cols):
+        g_out[cc] = found[:, cc * 128 : cc * 128 + 128]
+    grad_sib_start("o")
+    sums[...] = jnp.zeros_like(sums)
+    arrived(grad_o.at[own, :], e_slot + 1)
+    arrived(grad_o.at[own, :], e_slot)
+    for h in range(heads):
+        head_grad[h] = grad_o[:, h * 64 : h * 64 + 64]
+    for name in ("u", "d"):
+        grad_sib_done(name)
+        for j in range(half):
+            one_start(name, j)
+
+    def attend_back(h, low_row, keys_seen, slot):
+        at = pl.ds(aligned(low_row, block), block)
+        here = pl.ds(aligned(slot * slot_len + low_row, block), block)
+        grad = head_grad[h, here, :]
+        low = (probs_a, probs_b)[slot][h, at, :]
+        inner = jnp.sum(grad.astype(F32) * heads_out[h, here, :].astype(F32), axis=1, keepdims=True)
+        grad_prob = nt(grad, vals[h, 0:keys_seen, :])
+        grad_score = (low.astype(F32) * (grad_prob - inner)).astype(BF16)
+        turned_v[:, 0:keys_seen] += tn(grad, low)
+        turned_k[:, 0:keys_seen] += tn(qcat[h, here, 512:576], grad_score)
+        got = nn(grad_score, kcat[0:keys_seen, :])
+        cosine = kcat[here, 0:256].astype(F32)
+        sine = kcat[here, 256:512].astype(F32)
+        first, second = got[:, 0:256], got[:, 256:512]
+        angle = jnp.concatenate([first * sine - second * cosine, first * cosine + second * sine], axis=1).astype(BF16)
+        both = got[:, 512:640] + nn(angle, wp_head[h])
+        turned_p[h] += tn(qcat[h, here, 512:640], angle)[64:128]
+        sums[pl.ds(h, 1), :] += jnp.sum(both, axis=0, keepdims=True) * 0.125
+        query = (both + pltpu.roll(both, 64, 1)) * 0.125
+        turned[h, 0:64, here] = jnp.transpose(query)[0:64].astype(BF16)
+
+    def project_back(i):
+        pair = jnp.concatenate([turned[2 * i], turned[2 * i + 1]], axis=0)
+        hs_q[i] = nt(normed_t[...], pair).astype(BF16).reshape(hs_q.shape[1:])
+        one_start("q", i)
+        pos = jnp.concatenate([turned_p[2 * i], turned_p[2 * i + 1]], axis=0)
+        hs_p[i] = jnp.transpose(pos).astype(BF16).reshape(hs_p.shape[1:])
+        one_start("p", i)
+        part = nn(wq_half[i], pair)
+        if i == 0:
+            one_t[...] = part
+        else:
+            one_t[...] += part
+
+    def back_zero():
+        grad_sib_done("o")
+        for j in range(half):
+            one_start("o", j)
+
+    def back_one():
+        project_back(0)
+        for name in ("u", "d"):
+            for j in range(half):
+                one_done(name, j)
+
+    def back_two():
+        for j in range(half):
+            one_done("o", j)
+        for name in ("u", "d"):
+            for j in range(half):
+                two_done(name, j)
+
+    @pl.loop(0, heads)
+    def _(h):
+        kcat[:, 512:640] = keys[h]
+        turned_k[...] = jnp.zeros_like(turned_k)
+        turned_v[...] = jnp.zeros_like(turned_v)
+        turned_p[h] = jnp.zeros(turned_p.shape[1:], F32)
+
+        @pl.loop(0, slot_len // block)
+        def _(t):
+            attend_back(h, t * block, slot_len, 0)
+
+        @pl.loop(0, slot_len // block)
+        def _(t):
+            attend_back(h, t * block, seq, 1)
+
+        turned[h, 64:128, :] = turned_k[...].astype(BF16)
+        turned[h, 128:192, :] = turned_v[...].astype(BF16)
+        for number, stage in enumerate((back_zero, back_one, back_two)):
+            pl.when(h == number)(stage)
+
+    project_back(1)
+
+    one_low[...] = one_t[:, other].astype(BF16)
+    f_slot = io.take(1)
+    io.push(f_slot, lambda: (one_low, one_got, f_slot, sibling))
+    one_done("q", 0)
+    one_done("p", 0)
+    for j in range(half):
+        two_done("o", j)
+    arrived(one_got, f_slot)
+    columns = [tall(params_col[cc]) for cc in range(cols)]
+    gain = jnp.concatenate([col[:, 0:1] for col in columns], axis=0)
+    one = one_t[:, own] + one_got[...].astype(F32)
+    x = xt[:, own].astype(F32)
+    mean = jnp.sum(x, axis=0, keepdims=True) * (1.0 / width)
+    square = jnp.sum(x * x, axis=0, keepdims=True) * (1.0 / width)
+    inverse = lax.rsqrt(square - mean * mean + norm_epsilon)
+    scaled = (x - mean) * inverse
+    shifted = one * gain
+    first = jnp.sum(shifted, axis=0, keepdims=True) * (1.0 / width)
+    second = jnp.sum(shifted * scaled, axis=0, keepdims=True) * (1.0 / width)
+    grad_x[...] = (grad_mid_t[...] + inverse * (shifted - first - scaled * second)).astype(BF16)
+    back_start(grad_x, grads, b_slot["grad"])
+    gain_sum = jnp.sum(one * scaled, axis=1, keepdims=True)
+    bias_sum = jnp.sum(one, axis=1, keepdims=True)
+    lane = lax.broadcasted_iota(jnp.int32, (width, 128), 1)
+    pair = jnp.where(lane == 0, gain_sum, jnp.where(lane == 1, bias_sum, 0.0))
+    pair = jnp.transpose(pair)[0:8]
+    all_small[0] = small[...]
+    all_small[0, 0:2, :] = pair[0:2]
+
+    def spread(first_lane):
+        row = jnp.concatenate([sums[h : h + 1, first_lane : first_lane + 64] for h in range(heads)], axis=1)
+        blank = jnp.zeros_like(row)
+        return jnp.where(k == 0, jnp.concatenate([row, blank], axis=1), jnp.concatenate([blank, row], axis=1))
+
+    all_small[0, 9:10, :] = spread(0)
+    all_small[0, 10:11, :] = spread(64)
+    m_slot = io.take(3)
+    v_send = io.take(rows)
+    v_slot = io.take(rows)
+    io.push(m_slot, lambda: (all_small.at[0], got_small.at[0], m_slot, sibling))
+    for i in range(half):
+        if i > 0:
+            one_done("q", i)
+            one_done("p", i)
+    arrived(got_small.at[0], m_slot)
+    all_small[1] = all_small[0] + got_small[0]
+    io.push(m_slot + 1, lambda: (all_small.at[1], got_small.at[1], m_slot + 1, (k, z, near)))
+    for name in ("u", "d"):
+        grad_z_done(name)
+    for i in range(half):
+        two_done("q", i)
+        two_done("p", i)
+    arrived(got_small.at[1], m_slot + 1)
+    all_small[2] = all_small[1] + got_small[1]
+    io.push(m_slot + 2, lambda: (all_small.at[2], got_small.at[2], m_slot + 2, (k, z, far)))
+    grad_z_done("o")
+    arrived(got_small.at[2], m_slot + 2)
+    all_small[3] = all_small[2] + got_small[2]
+    for step in range(1, rows):
+        io.push(
+            v_send + step,
+            lambda step=step: (all_small.at[3], got_z.at[z], v_slot + z, (k, lax.rem(z + step, rows), c)),
+        )
+    grad_z_done("q")
+    grad_z_done("p")
+    total = all_small[3]
+    for step in range(1, rows):
+        source = lax.rem(z + step, rows)
+        arrived(got_z.at[source], v_slot + source)
+        total = total + got_z[source]
+    f_small[...] = total
+    back_done(outs, b_slot["out"])
+    back_done(grads, b_slot["grad"])
+    for name in ("u", "d", "o", "q", "p"):
+        last_done(name)
+    io.drain()
+
+
+def final_kernel(
+    outs, grads, f_q, f_p, f_o, f_u, f_d, f_small,
+    output, grad_tokens, g1, b1, q_w, c_b, p_b, p_w, o_w, g2, b2, u_w, u_b, d_w, d_b,
+):
+    k, z, c, _, _ = place()
+    for b in range(2):
+        for core in range(2):
+            size = outs.shape[3]
+            output[b, :, core * size : core * size + size] = outs[b, core].astype(F32)
+            grad_tokens[b, :, core * size : core * size + size] = grads[b, core].astype(F32)
+    for core in range(2):
+
+        @pl.when(k == core)
+        def _(core=core):
+            for ref, source in ((q_w, f_q), (p_w, f_p), (o_w, f_o), (d_w, f_d)):
+                size = ref.shape[0]
+                ref[...] = jnp.transpose(source[:, core * size : core * size + size])
+            size = u_w.shape[1]
+            u_w[...] = f_u[:, core * size : core * size + size]
+
+    width = f_small.shape[1]
+    chip = z * 4 + c
+    share = g1.shape[1]
+    first = pltpu.roll(f_small[0:8, :], lax.rem(width - (chip * 2 + k) * share, width), 1)
+    for row, ref in ((0, g1), (1, b1), (2, g2), (3, b2), (4, d_b)):
+        ref[...] = first[row : row + 1, 0:share]
+    share = u_b.shape[1]
+    line = f_small[pl.ds(5 + z, 1), :]
+    line = jnp.broadcast_to(line, (8, width))
+    u_b[...] = pltpu.roll(line, lax.rem(width - (c * 2 + k) * share, width), 1)[0:1, 0:share]
+    heads, share = c_b.shape
+    third = pltpu.roll(f_small[8:16, :], lax.rem(2 * width - heads * 64 * z - (c * 2 + k) * share, width), 1)
+    for h in range(heads):
+        c_b[h : h + 1, :] = third[1:2, h * 64 : h * 64 + share]
+        p_b[h : h + 1, :] = third[2:3, h * 64 : h * 64 + share]
+
+
+def position_table(seq_len, feature_count):
+    positions = np.arange(seq_len, dtype=np.float64)
+    exponent = -np.arange(0, feature_count, 2, dtype=np.float64) / feature_count
+    angles = positions[:, None] * (10000.0**exponent)[None, :]
+    return np.concatenate([np.cos(angles), np.sin(angles)], axis=1).astype(jnp.bfloat16)
+
+
+def fast_shards(
+    tokens, cotangent, piece_starts, ln1_gain, ln1_bias, qkv_weight, content_bias, position_bias, pos_weight,
+    out_weight, ln2_gain, ln2_bias, up_weight, up_bias, down_weight, down_bias,
+):
+    rows, cols = lax.axis_size("row"), lax.axis_size("col")
+    half = rows // 2
+    micro, feat, seq = tokens.shape
+    width = feat * cols
+    count = seq // 2
+    hidden = up_weight.shape[1]
+    heads = content_bias.shape[0] * half
+    table = jnp.asarray(position_table(seq, width))
+    lines = jnp.concatenate(
+        [ln1_gain, ln1_bias, ln2_gain, ln2_bias, down_bias, jnp.zeros((3 * feat,), BF16), up_bias, jnp.zeros((8 * 128 - hidden,), BF16)]
+    )
+    packed = lines.reshape(16, 128).astype(F32)
+    vm = pl.BlockSpec(memory_space=pltpu.VMEM)
+    anywhere = pl.BlockSpec(memory_space=pl.ANY)
+    limit = 64 * 1024 * 1024 - 128 * 1024
+
+    def shape(dims, kind=BF16):
+        return jax.ShapeDtypeStruct(dims, kind)
+
+    def vmem(dims, kind=BF16):
+        return pltpu.VMEM(dims, kind)
+
+    q_cols, p_cols = qkv_weight.shape[1], pos_weight.shape[1]
+    o_rows, d_rows = out_weight.shape[0], down_weight.shape[0]
+    blocks = {
+        "q": (feat, q_cols), "p": (feat, p_cols), "o": (o_rows, 128), "u": (feat, hidden), "d": (d_rows, 128),
+    }
+    names = ("q", "p", "o", "u", "d")
+    results = pl.pallas_call(
+        layer_kernel,
+        name="layer",
+        out_shape=(
+            shape((micro, 2, feat, count)),
+            shape((micro, 2, feat, count)),
+        )
+        + tuple(shape(blocks[name], F32) for name in names)
+        + (shape((16, width), F32),),
+        in_specs=[anywhere, anywhere, vm, vm, vm, vm] + [anywhere] * 6,
+        out_specs=(vm,) * 8,
+        scratch_shapes=[
+            vmem((count, width)),
+            vmem((cols, width, 128)),
+            vmem((rows, width, hidden)),
+            vmem((cols, rows * hidden, 128)),
+            vmem((half, width, q_cols)),
+            vmem((half, width, p_cols)),
+            vmem((heads, width, 128)),
+            vmem((width, seq)),
+            vmem((width, count)),
+            vmem((width, seq)),
+            vmem((heads, seq, width + 128)),
+            vmem((heads, seq, 128)),
+            vmem((heads, seq, 64)),
+            vmem((heads, count, count)),
+            vmem((heads, count, seq)),
+            vmem((heads, seq, 64)),
+            vmem((cols, 8, 128), F32),
+            vmem((rows, 8, 128), F32),
+            vmem((rows,) + content_bias.shape, F32),
+            vmem((rows,) + position_bias.shape, F32),
+            vmem((seq, width + 128)),
+            vmem((seq, heads * 64)),
+            vmem(piece_starts.shape, jnp.int32),
+            vmem((count, width), F32),
+            vmem((count, width)),
+            vmem((count, width), F32),
+            vmem((count, 1), F32),
+            vmem((count, width)),
+            vmem((count, width), F32),
+            vmem((count, width), F32),
+            vmem((width, count)),
+            vmem((width, count)),
+            vmem((width, count), F32),
+            vmem((count, width)),
+            vmem((rows, width, hidden)),
+            vmem((cols, rows * hidden, 128)),
+            vmem((cols, width, 128)),
+            vmem((16, width), F32),
+            vmem((seq, heads * 64)),
+            vmem((heads, seq, 64)),
+            vmem((heads, 192, seq)),
+            vmem((64, seq), F32),
+            vmem((64, seq), F32),
+            vmem((heads, 64, width), F32),
+            vmem((width, seq), F32),
+            vmem((width, count)),
+            vmem((width, count)),
+            vmem((width, count)),
+            vmem((8, 128), F32),
+            vmem((half, cols) + blocks["q"]),
+            vmem((half, cols) + blocks["p"]),
+            vmem((cols, half) + blocks["o"]),
+            vmem((half, cols) + blocks["u"]),
+            vmem((cols, half) + blocks["d"]),
+            vmem((cols, half * o_rows, 128)),
+            vmem((half, width, hidden)),
+            vmem((cols, half * d_rows, 128)),
+        ]
+        + [vmem((half, 2) + blocks[name]) for name in names]
+        + [vmem((half,) + blocks[name]) for name in names]
+        + [vmem((rows,) + blocks[name]) for name in names]
+        + [
+            vmem((4, 16, width), F32),
+            vmem((3, 16, width), F32),
+            vmem((rows, 16, width), F32),
+            pltpu.SemaphoreType.DMA((280,)),
+            pltpu.SemaphoreType.DMA((280,)),
+        ],
+        compiler_params=pltpu.CompilerParams(collective_id=0, has_side_effects=True, vmem_limit_bytes=limit),
+    )(
+        tokens, cotangent, piece_starts, packed, content_bias, position_bias, table,
+        qkv_weight, pos_weight, out_weight, up_weight, down_weight,
+    )
+    devices = 2 * rows * cols
+    vec = shape((1, width // devices), F32)
+    bias = shape((content_bias.shape[0], 64 // (2 * cols)), F32)
+    done = list(pl.pallas_call(
+        final_kernel,
+        name="final",
+        out_shape=(
+            shape(tokens.shape, F32), shape(tokens.shape, F32), vec, vec,
+            shape((q_cols // 2, feat), F32), bias, bias, shape((p_cols // 2, feat), F32), shape((64, o_rows), F32), vec, vec,
+            shape((feat, hidden // 2), F32), shape((1, rows * hidden // devices), F32), shape((64, d_rows), F32), vec,
+        ),
+        in_specs=[vm] * 8,
+        out_specs=(vm,) * 15,
+        compiler_params=pltpu.CompilerParams(vmem_limit_bytes=limit),
+    )(*results))
+    for index in (4, 7, 8, 13):
+        done[index] = done[index].T
+    return tuple(v.reshape(-1) if v.shape[0] == 1 else v for v in done)
+
+
 def solution(mesh):
     in_specs = (
         P(None, "col", ("dp", "row")),
@@ -558,4 +1566,12 @@
         P("row", ("col", "dp")),
         P(("row", "col", "dp")),
     )
-    return jax.shard_map(shards, mesh=mesh, in_specs=in_specs, out_specs=out_specs, check_vma=False)
+
+    def layer(tokens, *others):
+        dp, row, col = mesh.shape["dp"], mesh.shape["row"], mesh.shape["col"]
+        one_each = tokens.shape[2] == dp * row * SEQ_LEN and tokens.shape[0] * dp == col
+        body = fast_shards if one_each and dp == 2 and row == col == 4 else shards
+        part = jax.shard_map(body, mesh=mesh, in_specs=in_specs, out_specs=out_specs, check_vma=False)
+        return part(tokens, *others)
+
+    return layer

time: 2570 us -> 136 us (0.05)
  waiting for transfers between devices: 1430 us -> 0 us
  local copies, waits for them, and re-layouts: 550 us -> 4.5 us
  matrix products: 215 us -> 0 us
  blocking collectives: 150 us -> 0 us
  Pallas kernels: 0 us -> 130 us
  loops' own time: 111 us -> 0 us
  other arithmetic: 84.4 us -> 0.6 us
    reduce_scatter x22 -> x0, waiting for transfers between devices: 898 us -> none  [the longest x8 474 us: sum_over_cols(): lax.psum_scatter(partial_term(jnp.int32(0), lax.axis_size('col') * share_...]
    all_gather x16 -> x0, waiting for transfers between devices: 489 us -> none  [the longest x8 307 us: gather_cols(): return lax.all_gather(values, 'col', axis=0, tiled=True)]
    reshape x24 -> x0, local copies, waits for them, and re-layouts: 272 us -> none  [the longest x8 111 us: skew_rows(): return window.reshape(head_total, row_total, rel_span - 1)[:, :, :key_total]]
    dot_general x71 -> x0, matrix products: 215 us -> none  [the longest x8 36.7 us: contract(): return jnp.dot(left_op, right_op, preferred_element_type=jnp.float32)]
    pallas_call x0 -> x2, Pallas kernels: none -> 130 us  [the longest x1 127 us: fast_shards(): pl.pallas_call(layer_kernel, name='layer', out_shape=(shape((micro, 2, fe...]
    another operation x4 -> x0, loops' own time: 111 us -> none  [the longest x2 67.9 us: attention_backward(): lax.scan(back_block, (zero_rows, zero_rows, zero_rel), (offsets, log_tota...]
    slice x10 -> x0, local copies, waits for them, and re-layouts: 83.6 us -> none  [the longest x8 81.4 us: skew_rows(): lax.slice_in_dim(flattened, row_total - 1, row_total - 1 + row_total * (r...]
    unnamed x2 -> x0, blocking collectives: 78.5 us -> none
  transfers between devices with their start and end apart: 44 -> 0, of which waited for: 39 -> 0; matrix products, arithmetic and copies ran while one was open for 19% -> 0% of each run, Pallas kernels for 0% -> 0%
where the time goes in v2:
time: 136 us
  Pallas kernels  130 us (96%)
  local copies, waits for them, and re-layouts  4.5 us (3%)
    pallas_call x1, Pallas kernels, fast_shards(): pl.pallas_call(layer_kernel, name='layer', out_shape=(shape((micro, 2, fe...  127 us
    unnamed x19, local copies, waits for them, and re-layouts  4.29 us
    pallas_call x1, Pallas kernels, fast_shards(): pl.pallas_call(final_kernel, name='final', out_shape=(shape(tokens.shape,...  3.25 us

profile of v2, /device:TPU:0, one launch (start us, length us, event | category | flops | bytes accessed | tf_op | source)
XLA Modules:
  0.0 136.2 jit_solution(9976571454511652785)
XLA Ops:
  0.6 0.0 copy-start.1
  0.7 0.6 copy-done.1
  1.3 0.0 copy-start.2
  1.3 0.2 dynamic-update-slice
  1.5 0.5 copy-done.2
  2.0 0.0 copy-start.3
  2.0 0.2 dynamic-update-slice.1
  2.1 0.5 copy-done.3
  2.6 0.0 copy-start.4
  2.6 0.2 dynamic-update-slice.2
  2.8 0.5 copy-done.4
  3.3 0.0 copy-start.5
  3.3 0.2 dynamic-update-slice.3
  3.5 0.5 copy-done.5
  3.9 0.2 dynamic-update-slice.4
  4.1 0.0 copy-start
  4.1 0.2 dynamic-update-slice.5
  4.4 0.4 copy-done
  4.8 0.2 dynamic-update-slice.6
  5.0 0.2 dynamic-update-slice.7
  5.2 0.6 bitcast_convert_fusion.packed
  5.8 127.0 %layer.1 = (bf16[2,2,128,512]{3,2,1,0:T(8,128)(2,1)}, bf16[2,2,128,512]{3,2,1,0:T(8,128)(2,1)}, f32[128,384]{1,0:T(8,128)}, f32[128,128]{1,0:T(8,128)}, f32[128,...) custom-call(bf16[2,128,1024]{2,1,0:T(8,128)(2,1)} %tok.1, ...), custom_call_target="tpu_custom_call" | custom-call | tf_op jit(solution)/shard_map/layer/pallas_call | solution.py:1428
  132.8 3.3 %final.1 = (f32[2,128,1024]{2,1,0:T(8,128)}, f32[2,128,1024]{2,1,0:T(8,128)}, f32[1,16]{1,0:T(1,128)}, f32[1,16]{1,0:T(1,128)}, f32[192,128]{1,0:T(8,128)}, /*in...) custom-call(bf16[2,2,128,512]{3,2,1,0:T(8,128)(2,1)} %get-tuple-elem, ...), custom_call_target="tpu_custom_call" | custom-call | tf_op jit(solution)/shard_map/final/pallas_call | solution.py:1516
  (3 shorter events, 0.0 us)
Async XLA Ops:
  0.6 0.7 copy-start.1
  1.3 0.7 copy-start.2
  2.0 0.7 copy-start.3
  2.6 0.7 copy-start.4
  3.3 0.7 copy-start.5
  4.1 0.7 copy-start

commit v3 on v2

--- a/solution.py
+++ b/solution.py
@@ -571,26 +571,35 @@
 
 class Copies:
     def __init__(self, send, recv):
-        self.send, self.recv, self.next = send, recv, 0
+        self.send, self.recv = send, recv
+        self.sends, self.recvs = 0, 0
         self.pending = {}
 
-    def take(self, count=1):
-        first = self.next
-        self.next += count
+    def leave(self, count=1):
+        first = self.sends
+        self.sends += count
         return first
 
+    def land(self, count=1):
+        first = self.recvs
+        self.recvs += count
+        return first
+
+    def copy(self, send_slot, build):
+        src, dst, recv_slot, peer = build()
+        return pltpu.make_async_remote_copy(
+            src, dst, self.send.at[send_slot], self.recv.at[recv_slot], device_id=peer, device_id_type=MESH
+        )
+
     def push(self, send_slot, build, when=None):
-        def copy():
-            src, dst, recv_slot, peer = build()
-            return pltpu.make_async_remote_copy(
-                src, dst, self.send.at[send_slot], self.recv.at[recv_slot], device_id=peer, device_id_type=MESH
-            )
-
         if when is None:
-            copy().start()
+            self.copy(send_slot, build).start()
         else:
-            pl.when(when())(lambda: copy().start())
-        self.pending[send_slot] = (copy, when)
+            pl.when(when())(lambda: self.copy(send_slot, build).start())
+        self.later(send_slot, build, when)
+
+    def later(self, send_slot, build, when=None):
+        self.pending[send_slot] = (lambda: self.copy(send_slot, build), when)
 
     def keep(self, src, dst, slot, when=None):
         def go():
@@ -624,14 +633,14 @@
 
 def layer_kernel(
     tok, cot, starts, packed, cbias, pbias, table, wq, wp, wo, wu, wd,
-    outs, grads, f_q, f_p, f_o, f_u, f_d, f_small,
+    outs, grads, f_qp, f_o, f_u, f_d, f_small,
     att, wo_all, wu_all, wd_all, wq_half, wp_half, wp_head, xt, ct, normed_t, qcat, keys, vals, probs_a, probs_b, heads_out,
     params_col, params_row, cb_all, pb_all, kcat, own_att, starts_got,
     mid, norm, hat, inv, gout, acc_out, acc_two, tall_norm, out_t, grad_mid_t, grad_att, g_up, g_down, g_out, small,
     grad_o, head_grad, turned, turned_k, turned_v, turned_p, one_t, one_low, one_got, grad_x, sums,
-    hs_q, hs_p, hs_o, hs_u, hs_d, r0_o, r0_u, r0_d,
-    r1_q, r1_p, r1_o, r1_u, r1_d, r2_q, r2_p, r2_o, r2_u, r2_d, r3_q, r3_p, r3_o, r3_u, r3_d,
-    all_small, got_small, got_z, send, recv,
+    hs_qp, hs_o, hs_u, hs_d, r0_o, r0_u, r0_d, s_d,
+    r1_qp, r1_o, r1_u, r1_d, r2_qp, r2_o, r2_u, r2_d, r3_qp, r3_o, r3_u, r3_d,
+    all_small, got_sib, got_plane, got_z, send, recv,
 ):
     rows = wu_all.shape[0]
     cols = wo_all.shape[0]
@@ -683,27 +692,22 @@
         "q": (wq, q_one, q_block), "p": (wp, p_one, p_block), "o": (wo, o_one, o_block),
         "u": (wu, u_one, u_block), "d": (wd, d_one, d_block),
     }
-    z_slot = {name: io.take(half) for name in weights}
-    z_send = {name: io.take(half * rows) for name in weights}
-    near_slot = {name: io.take(1) for name in weights}
-    far_slot = {name: io.take(2) for name in weights}
-    sib_slot = {name: io.take(4) for name in weights}
+    z_slot = {name: io.land(half) for name in weights}
+    z_send = {name: io.leave(rows - 1) for name in weights}
+    near_slot = {name: (io.leave(), io.land()) for name in weights}
+    far_slot = {name: (io.leave(2), io.land(2)) for name in weights}
+    sib_slot = {name: (io.leave(), io.land()) for name in ("o", "u", "d")}
+    turn = z - k * half
 
     def z_start(name):
         ref, one, _ = weights[name]
-        for i in range(half):
-            slot = z_slot[name] + i
-
-            def here(i=i):
-                return z == k * half + i
-
-            io.keep(lambda: ref, lambda i=i: one(i), slot, here)
-            for step in range(1, rows):
-                io.push(
-                    z_send[name] + i * rows + step,
-                    lambda i=i, step=step, slot=slot: (ref, one(i), slot, (k, lax.rem(z + step, rows), c)),
-                    here,
-                )
+        io.keep(lambda: ref, lambda: one(turn), z_slot[name] + turn, lambda: mine)
+        for step in range(1, rows):
+            io.push(
+                z_send[name] + step - 1,
+                lambda step=step: (ref, one(turn), z_slot[name] + turn, (k, lax.rem(z + step, rows), c)),
+                lambda: mine,
+            )
 
     def z_done(name):
         _, one, _ = weights[name]
@@ -712,36 +716,42 @@
 
     def near_start(name):
         block = weights[name][2]
-        io.push(near_slot[name], lambda: (block(c), block(c), near_slot[name], (k, z, near)))
+        leave, land = near_slot[name]
+        io.push(leave, lambda: (block(c), block(c), land, (k, z, near)))
 
     def near_done(name):
-        arrived(weights[name][2](near), near_slot[name])
+        arrived(weights[name][2](near), near_slot[name][1])
 
     def far_start(name):
         block = weights[name][2]
-        io.push(far_slot[name], lambda: (block(c), block(c), far_slot[name], (k, z, far)))
-        io.push(far_slot[name] + 1, lambda: (block(near), block(near), far_slot[name] + 1, (k, z, far)))
+        leave, land = far_slot[name]
+        io.push(leave, lambda: (block(c), block(c), land, (k, z, far)))
+        io.push(leave + 1, lambda: (block(near), block(near), land + 1, (k, z, far)))
 
     def far_done(name):
         block = weights[name][2]
-        arrived(block(far), far_slot[name])
-        arrived(block(3 - c), far_slot[name] + 1)
+        arrived(block(far), far_slot[name][1])
+        arrived(block(opposite), far_slot[name][1] + 1)
+
+    def core_half(name, core):
+        if name == "u":
+            return wu_all.at[pl.ds(core * half, half)]
+        full = wo_all if name == "o" else wd_all
+        size = full.shape[1] // 2
+        return full.at[:, pl.ds(aligned(core * size, 128), size), :]
 
     def sib_start(name):
-        block = weights[name][2]
-        for cc in range(4):
-            slot = sib_slot[name] + cc
-            io.push(slot, lambda cc=cc, slot=slot: (block(cc), block(cc), slot, (1 - k, z, c)))
+        leave, land = sib_slot[name]
+        io.push(leave, lambda: (core_half(name, k), core_half(name, k), land, sibling))
 
     def sib_done(name):
-        block = weights[name][2]
-        for cc in range(4):
-            arrived(block(cc, 1 - k), sib_slot[name] + cc)
+        arrived(core_half(name, 1 - k), sib_slot[name][1])
 
     feat = tok.shape[1]
-    x_slot = io.take(4)
-    x_send = io.take(4)
-    xf_slot = io.take(4)
+    x_slot = io.land(4)
+    x_send = io.leave(4)
+    xf_slot = io.land(4)
+    xf_send = io.leave(4)
 
     def x_part(cc, core):
         return xt.at[pl.ds(aligned(cc * feat + core * (feat // 2), 64), feat // 2), :]
@@ -767,29 +777,28 @@
             )
     z_start("p")
 
-    t_slot = io.take(1)
+    t_slot = io.land()
     io.keep(lambda: table, lambda: kcat.at[:, pl.ds(0, table.shape[1])], t_slot)
-    g_col = io.take(4)
-    g_row = io.take(rows)
-    g_cb = io.take(rows)
-    g_pb = io.take(rows)
+    g_col, g_row, g_cb, g_pb = io.land(), io.land(), io.land(), io.land()
+    col_send = io.leave(3)
     for step in range(1, 4):
         io.push(
-            g_col + step,
+            col_send + step - 1,
             lambda step=step: (packed.at[pl.ds(0, 8)], params_col.at[c], g_col, (k, z, lax.rem(c + step, 4))),
         )
     io.keep(lambda: packed.at[pl.ds(0, 8)], lambda: params_col.at[c], g_col)
     for source, target, slot in ((packed.at[pl.ds(8, 8)], params_row, g_row), (cbias, cb_all, g_cb), (pbias, pb_all, g_pb)):
+        row_send = io.leave(rows - 1)
         for step in range(1, rows):
             io.push(
-                slot + step,
+                row_send + step - 1,
                 lambda step=step, source=source, target=target, slot=slot: (
                     source, target.at[z], slot, (k, lax.rem(z + step, rows), c)
                 ),
             )
         io.keep(lambda source=source: source, lambda target=target: target.at[z], slot)
-    s_slot = io.take(1)
-    s_send = io.take(4)
+    s_slot = io.land()
+    s_send = io.leave(4)
     for b in range(2):
         for core in range(2):
             io.keep(
@@ -804,8 +813,8 @@
     for name in ("o", "u", "d"):
         z_start(name)
 
-    c_slot = io.take(4)
-    c_send = io.take(4)
+    c_slot = io.land(4)
+    c_send = io.leave(4)
     count = ct.shape[1]
 
     def cot_start():
@@ -825,11 +834,11 @@
                     lambda b=b, core=core: jnp.logical_not(is_local(b, core)),
                 )
 
+    z_done("q")
+    near_start("q")
     for cc in range(4):
         arrived(x_part(cc, k), x_slot + cc)
-        io.push(xf_slot + cc, lambda cc=cc: (x_part(cc, k), x_part(cc, k), xf_slot + cc, sibling))
-    z_done("q")
-    near_start("q")
+        io.push(xf_send + cc, lambda cc=cc: (x_part(cc, k), x_part(cc, k), xf_slot + cc, sibling))
     z_done("p")
     near_start("p")
     arrived(params_col, g_col)
@@ -839,6 +848,8 @@
     arrived(starts_got, s_slot)
     for cc in range(4):
         arrived(x_part(cc, 1 - k), xf_slot + cc)
+    near_done("q")
+    far_start("q")
 
     columns = [tall(params_col[cc]) for cc in range(4)]
     gain = jnp.concatenate([col[:, 0:1] for col in columns], axis=0)
@@ -857,15 +868,13 @@
         inverse = lax.rsqrt(square - mean * mean + norm_epsilon)
         normed_t[:, here] = ((x - mean) * inverse * gain + bias).astype(BF16)
 
-    near_done("q")
-    far_start("q")
     near_done("p")
     far_start("p")
-    cot_start()
     z_done("o")
     near_start("o")
     z_done("u")
     near_start("u")
+    cot_start()
     far_done("q")
     scale = 0.125
     none = jnp.zeros((256, 64), F32)
@@ -887,6 +896,8 @@
             keys[h, here, :] = jnp.concatenate([key, none], axis=1).astype(BF16)
             vals[h, here, :] = value.astype(BF16)
 
+    near_done("o")
+    far_start("o")
     z_done("d")
     near_start("d")
     far_done("p")
@@ -905,6 +916,9 @@
         first, second = angle[:, 0:256], angle[:, 256:512]
         qcat[h, here, 0:256] = (first * sine + second * cosine).astype(BF16)
         qcat[h, here, 256:512] = (second * sine - first * cosine).astype(BF16)
+
+    near_done("u")
+    far_start("u")
 
     slot_len = seq // 2
     block = 256
@@ -935,21 +949,24 @@
         probs[h, pl.ds(aligned(low_row, block), block), :] = low
         heads_out[h, here, :] = nn(low, vals[h, 0:keys_seen, :]).astype(BF16)
 
-    def stage_zero():
-        near_done("o")
-        far_start("o")
-        near_done("u")
-        far_start("u")
-
-    def stage_one():
+    def far_d():
         near_done("d")
         far_start("d")
+
+    def sib_o():
         far_done("o")
         sib_start("o")
 
-    def stage_two():
+    def sib_u():
         far_done("u")
         sib_start("u")
+
+    def ticks(h, slot, t, actions):
+        for number, action in actions.items():
+            if (number % 4) // 2 == slot:
+                pl.when(4 * h + 2 * slot + t == number)(action)
+
+    ahead = {6: far_d, 7: sib_o, 12: sib_u}
 
     @pl.loop(0, heads)
     def _(h):
@@ -958,30 +975,30 @@
         @pl.loop(0, slot_len // block)
         def _(t):
             attend(h, t * block, slot_len, 0)
+            ticks(h, 0, t, ahead)
 
         @pl.loop(0, slot_len // block)
         def _(t):
             attend(h, t * block, seq, 1)
-
-        for number, stage in enumerate((stage_zero, stage_one, stage_two)):
-            pl.when(h == number)(stage)
+            ticks(h, 1, t, ahead)
 
     own_att[...] = jnp.concatenate([heads_out[h] for h in range(heads)], axis=1)
-    a_slot = io.take(2)
+    a_slot, a_send = io.land(2), io.leave()
     span = own_att.shape[1]
     other = pl.ds(aligned((1 - k) * count, count), count)
     own = pl.ds(aligned(k * count, count), count)
     att_part = att.at[:, pl.ds(aligned(k * span, 128), span)]
-    io.push(a_slot, lambda: (own_att.at[other, :], att_part, a_slot, sibling))
+    io.push(a_send, lambda: (own_att.at[other, :], att_part, a_slot, sibling))
     io.keep(lambda: own_att.at[own, :], lambda: att_part, a_slot + 1)
-    far_done("d")
-    sib_start("d")
     for cc in range(4):
         arrived(ct.at[pl.ds(cc * feat, feat), :], c_slot + cc)
     gout[...] = jnp.transpose(ct[...])
     sib_done("o")
     arrived(own_att.at[own, :], a_slot + 1)
     arrived(own_att.at[own, :], a_slot)
+
+    far_done("d")
+    sib_start("d")
 
     def line(index):
         return jnp.concatenate([params_col[cc, index : index + 1, :] for cc in range(cols)], axis=1)
@@ -1006,11 +1023,262 @@
     small[...] = jnp.zeros_like(small)
     hidden = wu_all.shape[2]
 
+    part_rows = wd_all.shape[1] // rows // 2
+    u0_slot = (io.leave(half), io.land(half))
+    o0_slot = (io.leave(), io.land())
+    d0_slot = (io.leave(rows), io.land(rows))
+    u_slot = {"one": (io.leave(2 * half), io.land(2 * half)), "two": (io.leave(half), io.land(half)), "z": (io.leave(half), io.land(rows))}
+    o_slot = {"one": (io.leave(2), io.land(2)), "two": (io.leave(), io.land()), "z": (io.leave(half), io.land(rows))}
+    d_slot = {"one": (io.leave(2), io.land(2)), "two": (io.leave(), io.land()), "z": (io.leave(rows), io.land(rows))}
+    qp_slot = {
+        "one": (io.leave(2 * heads), io.land(2 * heads)), "two": (io.leave(heads), io.land(heads)),
+        "z": (io.leave(heads), io.land(2 * rows)),
+    }
+    last_slot = {name: (io.leave(), io.land()) for name in ("u", "o", "d", "qp")}
+
+    def load(ref):
+        return ref[...].astype(F32)
+
+    def add(to, term):
+        to[...] = (load(to) + load(term)).astype(BF16)
+
+    def near_on(first, leave, land, target):
+        io.push(leave, lambda: (first(), target(), land, (k, z, near)))
+
+    def u_sib(j):
+        leave, land = u0_slot
+        io.push(leave + j, lambda: (g_up.at[(1 - k) * half + j], r0_u.at[j], land + j, sibling))
+
+    def u_one(j):
+        arrived(r0_u.at[j], u0_slot[1] + j)
+        total = load(g_up.at[k * half + j]) + load(r0_u.at[j])
+        hs_u[j] = total.astype(BF16).reshape(hs_u.shape[1:])
+        leave, land = u_slot["one"]
+        io.push(leave + 2 * j, lambda: (hs_u.at[j, far], r1_u.at[j, 0], land + 2 * j, (k, z, far)))
+        io.push(leave + 2 * j + 1, lambda: (hs_u.at[j, 3 - c], r1_u.at[j, 1], land + 2 * j + 1, (k, z, far)))
+
+    def u_two(j):
+        land = u_slot["one"][1] + 2 * j
+        arrived(r1_u.at[j, 1], land + 1)
+        add(r1_u.at[j, 1], hs_u.at[j, near])
+        near_on(lambda: r1_u.at[j, 1], u_slot["two"][0] + j, u_slot["two"][1] + j, lambda: r2_u.at[j])
+        arrived(r1_u.at[j, 0], land)
+        add(r1_u.at[j, 0], hs_u.at[j, c])
+
+    def u_z(j):
+        arrived(r2_u.at[j], u_slot["two"][1] + j)
+        add(r2_u.at[j], r1_u.at[j, 0])
+        leave, land = u_slot["z"]
+        io.push(
+            leave + j, lambda: (r2_u.at[j], r3_u.at[z], land + z, (k, k * half + j, c)), lambda: z != k * half + j
+        )
+
+    def z_total(total, r3, land, hb=None):
+        for step in range(1, rows):
+            source = lax.rem(z + step, rows)
+            part = r3.at[source] if hb is None else r3.at[hb, source]
+            arrived(part, land + source)
+            total = total + load(part)
+        return total
+
+    def finish(name, to):
+        leave, land = last_slot[name]
+        io.push(leave, lambda: (to, to, land, sibling), lambda: mine)
+
+    def u_last():
+        @pl.when(mine)
+        def _():
+            f_u[...] = z_total(load(r2_u.at[turn]), r3_u, u_slot["z"][1])
+
+        finish("u", f_u)
+
+    def o_sib():
+        leave, land = o0_slot
+        size = g_out.shape[1] // 2
+        io.push(leave, lambda: (g_out.at[:, pl.ds(aligned((1 - k) * size, 128), size), :], r0_o, land, sibling))
+
+    def o_one():
+        arrived(r0_o, o0_slot[1])
+        size = g_out.shape[1] // 2
+        for cc in range(cols):
+            total = load(g_out.at[cc, pl.ds(aligned(k * size, 128), size), :]) + load(r0_o.at[cc])
+            hs_o[cc] = total.astype(BF16).reshape(hs_o.shape[1:])
+        leave, land = o_slot["one"]
+        io.push(leave, lambda: (hs_o.at[far], r1_o.at[0], land, (k, z, far)))
+        io.push(leave + 1, lambda: (hs_o.at[3 - c], r1_o.at[1], land + 1, (k, z, far)))
+
+    def o_two():
+        land = o_slot["one"][1]
+        arrived(r1_o.at[1], land + 1)
+        add(r1_o.at[1], hs_o.at[near])
+        near_on(lambda: r1_o.at[1], o_slot["two"][0], o_slot["two"][1], lambda: r2_o)
+        arrived(r1_o.at[0], land)
+        add(r1_o.at[0], hs_o.at[c])
+
+    def o_z():
+        arrived(r2_o, o_slot["two"][1])
+        add(r2_o, r1_o.at[0])
+        leave, land = o_slot["z"]
+        for j in range(half):
+            io.push(
+                leave + j,
+                lambda j=j: (r2_o.at[j], r3_o.at[z], land + z, (k, k * half + j, c)),
+                lambda j=j: z != k * half + j,
+            )
+
+    def o_last():
+        @pl.when(mine)
+        def _():
+            f_o[...] = z_total(load(r2_o.at[turn]), r3_o, o_slot["z"][1])
+
+        finish("o", f_o)
+
+    def d_part(r, core):
+        return g_down.at[:, pl.ds(aligned((2 * r + core) * part_rows, 128), part_rows), :]
+
+    def d_sib(r, number):
+        leave, land = d0_slot
+        io.push(leave + number, lambda: (d_part(r(), 1 - k), r0_d.at[r()], land + r(), sibling))
+
+    def d_z(r, number):
+        arrived(r0_d.at[r()], d0_slot[1] + r())
+        hs_d[r()] = (load(d_part(r(), k)) + load(r0_d.at[r()])).astype(BF16)
+        leave, land = d_slot["z"]
+        io.push(leave + number, lambda: (hs_d.at[r()], r3_d.at[z], land + z, (k, r(), c)), lambda: z != r())
+
+    def d_one():
+        s_d[...] = z_total(load(hs_d.at[z]), r3_d, d_slot["z"][1]).astype(BF16)
+        leave, land = d_slot["one"]
+        io.push(leave, lambda: (s_d.at[far], r1_d.at[0], land, (k, z, far)))
+        io.push(leave + 1, lambda: (s_d.at[3 - c], r1_d.at[1], land + 1, (k, z, far)))
+
+    def d_two():
+        land = d_slot["one"][1]
+        arrived(r1_d.at[1], land + 1)
+        add(r1_d.at[1], s_d.at[near])
+        near_on(lambda: r1_d.at[1], d_slot["two"][0], d_slot["two"][1], lambda: r2_d)
+        arrived(r1_d.at[0], land)
+        add(r1_d.at[0], s_d.at[c])
+
+    def d_last():
+        arrived(r2_d, d_slot["two"][1])
+        leave, land = last_slot["d"]
+        f_d[pl.ds(aligned(k * part_rows, 128), part_rows), :] = load(r2_d) + load(r1_d.at[0])
+
+        def of_core():
+            return f_d.at[pl.ds(aligned(k * part_rows, 128), part_rows), :]
+
+        io.push(leave, lambda: (of_core(), of_core(), land, sibling))
+
+    def qp_builds(h):
+        leave, land = qp_slot["one"]
+        return (
+            (leave + 2 * h, lambda: (hs_qp.at[h, far], r1_qp.at[h, 0], land + 2 * h, (k, z, far))),
+            (leave + 2 * h + 1, lambda: (hs_qp.at[h, opposite], r1_qp.at[h, 1], land + 2 * h + 1, (k, z, far))),
+        )
+
+    def qp_one(h):
+        found = nt(turned[h], normed_t[...]).astype(BF16)
+        position = turned_p[h].astype(BF16)
+        for cc in range(cols):
+            hs_qp[h, cc, 0:192, :] = found[:, cc * 128 : cc * 128 + 128]
+            hs_qp[h, cc, 192:256, :] = position[:, cc * 128 : cc * 128 + 128]
+        for leave, build in qp_builds(h):
+            io.copy(leave, build).start()
+
+    for h in range(heads):
+        for leave, build in qp_builds(h):
+            io.later(leave, build)
+
+    def qp_two(h):
+        land = qp_slot["one"][1] + 2 * h
+        arrived(r1_qp.at[h, 1], land + 1)
+        add(r1_qp.at[h, 1], hs_qp.at[h, near])
+        near_on(lambda: r1_qp.at[h, 1], qp_slot["two"][0] + h, qp_slot["two"][1] + h, lambda: r2_qp.at[h])
+        arrived(r1_qp.at[h, 0], land)
+        add(r1_qp.at[h, 0], hs_qp.at[h, c])
+
+    def qp_z(h):
+        arrived(r2_qp.at[h], qp_slot["two"][1] + h)
+        add(r2_qp.at[h], r1_qp.at[h, 0])
+        leave, land = qp_slot["z"]
+        io.push(
+            leave + h,
+            lambda: (r2_qp.at[h], r3_qp.at[h % 2, z], land + (h % 2) * rows + z, (k, k * half + h // 2, c)),
+            lambda: z != k * half + h // 2,
+        )
+
+    def qp_last():
+        @pl.when(mine)
+        def _():
+            for hb in range(2):
+                f_qp[hb] = z_total(load(r2_qp.at[2 * turn + hb]), r3_qp, qp_slot["z"][1] + hb * rows, hb)
+
+        finish("qp", f_qp)
+
+    def last_done():
+        @pl.when(jnp.logical_not(mine))
+        def _():
+            for name, to in (("u", f_u), ("o", f_o), ("qp", f_qp)):
+                arrived(to, last_slot[name][1])
+
+        arrived(f_d.at[pl.ds(aligned((1 - k) * part_rows, 128), part_rows), :], last_slot["d"][1])
+
+    origin = lax.rem(c, 2)
+    out_slot, grad_slot = (io.leave(4), io.land(4)), (io.leave(4), io.land(4))
+
+    def back_start(src, dst, pair):
+        leave, base = pair
+        for step in range(4):
+
+            def part(step=step):
+                return src.at[pl.ds(aligned(lax.rem(c + step, 4) * feat, 128), feat), :]
+
+            def landing():
+                return dst.at[batch, k]
+
+            if step == 0:
+                io.keep(part, landing, base + 2 * batch + k, lambda: origin == k)
+                io.push(
+                    leave + step,
+                    lambda part=part, landing=landing: (part(), landing(), base + 2 * batch + k, sibling),
+                    lambda: origin != k,
+                )
+            else:
+                io.push(
+                    leave + step,
+                    lambda part=part, landing=landing, step=step: (
+                        part(), landing(), base + 2 * batch + k, (origin, z, lax.rem(c + step, 4))
+                    ),
+                )
+
+    def back_done(dst, pair):
+        base = pair[1]
+        for b in range(2):
+            for core in range(2):
+                arrived(dst.at[b, core], base + 2 * b + core)
+
+
+    def rows_of(number):
+        core = k if number % 2 == 0 else 1 - k
+        return core * half + number // 2
+
+    def after_one():
+        u_sib(0)
+        for number in range(2):
+            d_sib(lambda number=number: rows_of(number), number)
+
+    def after_two():
+        u_one(0)
+        for number in range(2):
+            d_z(lambda number=number: rows_of(number), number)
+
     @pl.loop(0, rows)
     def _(step):
-        r = lax.rem(k * half + step, rows)
-
-        @pl.when(step == half)
+        turn_of = lax.rem(step, 2)
+        r = ((1 - turn_of) * k + turn_of * (1 - k)) * half + lax.div(step, 2)
+
+        @pl.when(step == 1)
         def _():
             for name in ("u", "d"):
                 sib_done(name)
@@ -1031,139 +1299,15 @@
         found = tn(act, gout[...]).astype(BF16)
         for cc in range(cols):
             g_down[cc, here, :] = found[:, cc * 128 : cc * 128 + 128]
-
-    hs = {
-        "q": lambda i, cc: hs_q.at[i, cc], "p": lambda i, cc: hs_p.at[i, cc], "u": lambda i, cc: hs_u.at[i, cc],
-        "o": lambda i, cc: hs_o.at[cc, i], "d": lambda i, cc: hs_d.at[cc, i],
-    }
-    r1 = {"q": r1_q, "p": r1_p, "o": r1_o, "u": r1_u, "d": r1_d}
-    r2 = {"q": r2_q, "p": r2_p, "o": r2_o, "u": r2_u, "d": r2_d}
-    r3 = {"q": r3_q, "p": r3_p, "o": r3_o, "u": r3_u, "d": r3_d}
-    final = {"q": f_q, "p": f_p, "o": f_o, "u": f_u, "d": f_d}
-    slots = {}
-    for name in ("o", "u", "d", "q", "p"):
-        slots[name, "sib"] = io.take(1)
-        slots[name, "one"] = io.take(2 * half)
-        slots[name, "two"] = io.take(half)
-        slots[name, "z"] = io.take(rows)
-        slots[name, "last"] = io.take(1)
-
-    def grad_half(name, core):
-        if name == "u":
-            return g_up.at[pl.ds(core * half, half)]
-        full = g_out if name == "o" else g_down
-        size = full.shape[1] // 2
-        return full.at[:, pl.ds(aligned(core * size, 128), size), :]
-
-    got0 = {"u": r0_u, "o": r0_o, "d": r0_d}
-
-    def grad_sib_start(name):
-        slot = slots[name, "sib"]
-        io.push(slot, lambda: (grad_half(name, 1 - k), got0[name], slot, sibling))
-
-    def grad_sib_done(name):
-        arrived(got0[name], slots[name, "sib"])
-        if name == "u":
-            for i in range(half):
-                total = g_up[k * half + i].astype(F32) + r0_u[i].astype(F32)
-                hs_u[i] = total.astype(BF16).reshape(hs_u.shape[1:])
-        else:
-            full = g_out if name == "o" else g_down
-            size = full.shape[1] // 2
-            to = hs_o if name == "o" else hs_d
-            for cc in range(cols):
-                part = full[cc, pl.ds(aligned(k * size, 128), size), :]
-                total = part.astype(F32) + got0[name][cc].astype(F32)
-                to[cc] = total.astype(BF16).reshape(to.shape[1:])
-
-    def one_start(name, i):
-        block = hs[name]
-        slot = slots[name, "one"] + 2 * i
-        io.push(slot, lambda: (block(i, far), r1[name].at[i, 0], slot, (k, z, far)))
-        io.push(slot + 1, lambda: (block(i, 3 - c), r1[name].at[i, 1], slot + 1, (k, z, far)))
-
-    def load(ref):
-        return ref[...].astype(F32)
-
-    def one_done(name, i):
-        block = hs[name]
-        slot = slots[name, "one"] + 2 * i
-        arrived(r1[name].at[i, 1], slot + 1)
-        r1[name][i, 1] = (r1[name][i, 1].astype(F32) + load(block(i, near))).astype(BF16)
-        io.push(
-            slots[name, "two"] + i, lambda: (r1[name].at[i, 1], r2[name].at[i], slots[name, "two"] + i, (k, z, near))
-        )
-        arrived(r1[name].at[i, 0], slot)
-        r1[name][i, 0] = (r1[name][i, 0].astype(F32) + load(block(i, c))).astype(BF16)
-
-    def two_done(name, i):
-        arrived(r2[name].at[i], slots[name, "two"] + i)
-        r2[name][i] = (r2[name][i].astype(F32) + r1[name][i, 0].astype(F32)).astype(BF16)
-        base = slots[name, "z"]
-        io.push(
-            base + i,
-            lambda: (r2[name].at[i], r3[name].at[z], base + z, (k, k * half + i, c)),
-            lambda: z != k * half + i,
-        )
-
-    def grad_z_done(name):
-        base = slots[name, "z"]
-        to = final[name]
-
-        @pl.when(mine)
-        def _():
-            total = r2[name][z - k * half].astype(F32)
-            for step in range(1, rows):
-                source = lax.rem(z + step, rows)
-                arrived(r3[name].at[source], base + source)
-                total = total + r3[name][source].astype(F32)
-            to[...] = total
-
-        slot = slots[name, "last"]
-        io.push(slot, lambda: (to, to, slot, sibling), lambda: mine)
-
-    def last_done(name):
-        @pl.when(jnp.logical_not(mine))
-        def _():
-            arrived(final[name], slots[name, "last"])
-
-    origin = lax.rem(c, 2)
-    b_slot = {"out": io.take(4), "grad": io.take(4)}
-
-    def back_start(src, dst, base):
-        for step in range(4):
-
-            def part(step=step):
-                return src.at[pl.ds(aligned(lax.rem(c + step, 4) * feat, 128), feat), :]
-
-            def landing():
-                return dst.at[batch, k]
-
-            if step == 0:
-                io.keep(part, landing, base + 2 * batch + k, lambda: origin == k)
-                io.push(
-                    base + step,
-                    lambda part=part, landing=landing: (part(), landing(), base + 2 * batch + k, sibling),
-                    lambda: origin != k,
-                )
-            else:
-                io.push(
-                    base + step,
-                    lambda part=part, landing=landing, step=step: (
-                        part(), landing(), base + 2 * batch + k, (origin, z, lax.rem(c + step, 4))
-                    ),
-                )
-
-    def back_done(dst, base):
-        for b in range(2):
-            for core in range(2):
-                arrived(dst.at[b, core], base + 2 * b + core)
-
-    for name in ("u", "d"):
-        grad_sib_start(name)
+        pl.when(step == 1)(after_one)
+        pl.when(step == 2)(after_two)
+
+    u_sib(1)
+    for number in range(2, 4):
+        d_sib(lambda number=number: rows_of(number), number)
     cotangent = gout[...].astype(F32)
     out_t[...] = jnp.transpose(mid[...] + acc_out[...] + line(4)).astype(BF16)
-    back_start(out_t, outs, b_slot["out"])
+    back_start(out_t, outs, out_slot)
     two = acc_two[...]
     small[2:3, :] = jnp.sum(two * hat[...], axis=0, keepdims=True)
     small[3:4, :] = jnp.sum(two, axis=0, keepdims=True)
@@ -1174,9 +1318,9 @@
     grad_mid = cotangent + inv[...] * (shifted - first - hat[...] * second)
     branch = grad_mid.astype(BF16)
     grad_att[...] = nt(branch, out_weight()).astype(BF16)
-    e_slot = io.take(2)
+    e_slot, e_send = io.land(2), io.leave()
     io.push(
-        e_slot,
+        e_send,
         lambda: (grad_att.at[:, pl.ds(aligned((1 - k) * span, 128), span)], grad_o.at[own, :], e_slot, sibling),
     )
     io.keep(
@@ -1186,16 +1330,16 @@
     found = tn(att[...], branch).astype(BF16)
     for cc in range(cols):
         g_out[cc] = found[:, cc * 128 : cc * 128 + 128]
-    grad_sib_start("o")
+    o_sib()
+    u_one(1)
+    for number in range(2, 4):
+        d_z(lambda number=number: rows_of(number), number)
+    one_t[...] = jnp.zeros_like(one_t)
     sums[...] = jnp.zeros_like(sums)
     arrived(grad_o.at[own, :], e_slot + 1)
     arrived(grad_o.at[own, :], e_slot)
     for h in range(heads):
         head_grad[h] = grad_o[:, h * 64 : h * 64 + 64]
-    for name in ("u", "d"):
-        grad_sib_done(name)
-        for j in range(half):
-            one_start(name, j)
 
     def attend_back(h, low_row, keys_seen, slot):
         at = pl.ds(aligned(low_row, block), block)
@@ -1218,36 +1362,17 @@
         query = (both + pltpu.roll(both, 64, 1)) * 0.125
         turned[h, 0:64, here] = jnp.transpose(query)[0:64].astype(BF16)
 
-    def project_back(i):
-        pair = jnp.concatenate([turned[2 * i], turned[2 * i + 1]], axis=0)
-        hs_q[i] = nt(normed_t[...], pair).astype(BF16).reshape(hs_q.shape[1:])
-        one_start("q", i)
-        pos = jnp.concatenate([turned_p[2 * i], turned_p[2 * i + 1]], axis=0)
-        hs_p[i] = jnp.transpose(pos).astype(BF16).reshape(hs_p.shape[1:])
-        one_start("p", i)
-        part = nn(wq_half[i], pair)
-        if i == 0:
-            one_t[...] = part
-        else:
-            one_t[...] += part
-
-    def back_zero():
-        grad_sib_done("o")
-        for j in range(half):
-            one_start("o", j)
-
-    def back_one():
-        project_back(0)
-        for name in ("u", "d"):
-            for j in range(half):
-                one_done(name, j)
-
-    def back_two():
-        for j in range(half):
-            one_done("o", j)
-        for name in ("u", "d"):
-            for j in range(half):
-                two_done(name, j)
+    def both(*actions):
+        def run():
+            for action in actions:
+                action()
+
+        return run
+
+    behind = {
+        0: both(o_one, lambda: u_two(0)), 6: lambda: u_two(1), 7: o_two, 9: lambda: u_z(0), 10: lambda: qp_two(0),
+        11: lambda: u_z(1), 12: o_z, 13: lambda: qp_two(1), 14: lambda: qp_z(0),
+    }
 
     @pl.loop(0, heads)
     def _(h):
@@ -1259,25 +1384,28 @@
         @pl.loop(0, slot_len // block)
         def _(t):
             attend_back(h, t * block, slot_len, 0)
+            ticks(h, 0, t, behind)
 
         @pl.loop(0, slot_len // block)
         def _(t):
             attend_back(h, t * block, seq, 1)
+            ticks(h, 1, t, behind)
 
         turned[h, 64:128, :] = turned_k[...].astype(BF16)
         turned[h, 128:192, :] = turned_v[...].astype(BF16)
-        for number, stage in enumerate((back_zero, back_one, back_two)):
-            pl.when(h == number)(stage)
-
-    project_back(1)
+        qp_one(h)
+
+        @pl.when(lax.rem(h, 2) == 1)
+        def _():
+            i = lax.div(h, 2)
+            pair = jnp.concatenate([turned[2 * i], turned[2 * i + 1]], axis=0)
+            one_t[...] += nn(wq_half[i], pair)
 
     one_low[...] = one_t[:, other].astype(BF16)
-    f_slot = io.take(1)
-    io.push(f_slot, lambda: (one_low, one_got, f_slot, sibling))
-    one_done("q", 0)
-    one_done("p", 0)
-    for j in range(half):
-        two_done("o", j)
+    f_slot, f_send = io.land(), io.leave()
+    io.push(f_send, lambda: (one_low, one_got, f_slot, sibling))
+    qp_two(2)
+    qp_z(1)
     arrived(one_got, f_slot)
     columns = [tall(params_col[cc]) for cc in range(cols)]
     gain = jnp.concatenate([col[:, 0:1] for col in columns], axis=0)
@@ -1290,8 +1418,6 @@
     shifted = one * gain
     first = jnp.sum(shifted, axis=0, keepdims=True) * (1.0 / width)
     second = jnp.sum(shifted * scaled, axis=0, keepdims=True) * (1.0 / width)
-    grad_x[...] = (grad_mid_t[...] + inverse * (shifted - first - scaled * second)).astype(BF16)
-    back_start(grad_x, grads, b_slot["grad"])
     gain_sum = jnp.sum(one * scaled, axis=1, keepdims=True)
     bias_sum = jnp.sum(one, axis=1, keepdims=True)
     lane = lax.broadcasted_iota(jnp.int32, (width, 128), 1)
@@ -1307,50 +1433,45 @@
 
     all_small[0, 9:10, :] = spread(0)
     all_small[0, 10:11, :] = spread(64)
-    m_slot = io.take(3)
-    v_send = io.take(rows)
-    v_slot = io.take(rows)
-    io.push(m_slot, lambda: (all_small.at[0], got_small.at[0], m_slot, sibling))
-    for i in range(half):
-        if i > 0:
-            one_done("q", i)
-            one_done("p", i)
-    arrived(got_small.at[0], m_slot)
-    all_small[1] = all_small[0] + got_small[0]
-    io.push(m_slot + 1, lambda: (all_small.at[1], got_small.at[1], m_slot + 1, (k, z, near)))
-    for name in ("u", "d"):
-        grad_z_done(name)
-    for i in range(half):
-        two_done("q", i)
-        two_done("p", i)
-    arrived(got_small.at[1], m_slot + 1)
-    all_small[2] = all_small[1] + got_small[1]
-    io.push(m_slot + 2, lambda: (all_small.at[2], got_small.at[2], m_slot + 2, (k, z, far)))
-    grad_z_done("o")
-    arrived(got_small.at[2], m_slot + 2)
-    all_small[3] = all_small[2] + got_small[2]
+    m_slot, m_send = io.land(), io.leave()
+    p_slot, p_send = io.land(), io.leave(3)
+    v_slot, v_send = io.land(), io.leave(rows - 1)
+    io.push(m_send, lambda: (all_small.at[0], got_sib, m_slot, sibling))
+    grad_x[...] = (grad_mid_t[...] + inverse * (shifted - first - scaled * second)).astype(BF16)
+    arrived(got_sib, m_slot)
+    all_small[1] = all_small[0] + got_sib[...]
+    for step in range(1, 4):
+        io.push(
+            p_send + step - 1, lambda step=step: (all_small.at[1], got_plane.at[c], p_slot, (k, z, lax.rem(c + step, 4)))
+        )
+    io.keep(lambda: all_small.at[1], lambda: got_plane.at[c], p_slot)
+    back_start(grad_x, grads, grad_slot)
+    qp_two(3)
+    d_one()
+    qp_z(2)
+    arrived(got_plane, p_slot)
+    all_small[2] = (got_plane[0] + got_plane[1]) + (got_plane[2] + got_plane[3])
     for step in range(1, rows):
         io.push(
-            v_send + step,
-            lambda step=step: (all_small.at[3], got_z.at[z], v_slot + z, (k, lax.rem(z + step, rows), c)),
-        )
-    grad_z_done("q")
-    grad_z_done("p")
-    total = all_small[3]
-    for step in range(1, rows):
-        source = lax.rem(z + step, rows)
-        arrived(got_z.at[source], v_slot + source)
-        total = total + got_z[source]
-    f_small[...] = total
-    back_done(outs, b_slot["out"])
-    back_done(grads, b_slot["grad"])
-    for name in ("u", "d", "o", "q", "p"):
-        last_done(name)
+            v_send + step - 1, lambda step=step: (all_small.at[2], got_z.at[z], v_slot, (k, lax.rem(z + step, rows), c))
+        )
+    io.keep(lambda: all_small.at[2], lambda: got_z.at[z], v_slot)
+    u_last()
+    o_last()
+    d_two()
+    qp_z(3)
+    d_last()
+    arrived(got_z, v_slot)
+    f_small[...] = (got_z[0] + got_z[1]) + (got_z[2] + got_z[3])
+    qp_last()
+    back_done(outs, out_slot)
+    back_done(grads, grad_slot)
+    last_done()
     io.drain()
 
 
 def final_kernel(
-    outs, grads, f_q, f_p, f_o, f_u, f_d, f_small,
+    outs, grads, f_qp, f_o, f_u, f_d, f_small,
     output, grad_tokens, g1, b1, q_w, c_b, p_b, p_w, o_w, g2, b2, u_w, u_b, d_w, d_b,
 ):
     k, z, c, _, _ = place()
@@ -1363,7 +1484,9 @@
 
         @pl.when(k == core)
         def _(core=core):
-            for ref, source in ((q_w, f_q), (p_w, f_p), (o_w, f_o), (d_w, f_d)):
+            q_w[...] = f_qp[core, 0:192, :]
+            p_w[...] = f_qp[core, 192:256, :]
+            for ref, source in ((o_w, f_o), (d_w, f_d)):
                 size = ref.shape[0]
                 ref[...] = jnp.transpose(source[:, core * size : core * size + size])
             size = u_w.shape[1]
@@ -1405,10 +1528,10 @@
     hidden = up_weight.shape[1]
     heads = content_bias.shape[0] * half
     table = jnp.asarray(position_table(seq, width))
-    lines = jnp.concatenate(
-        [ln1_gain, ln1_bias, ln2_gain, ln2_bias, down_bias, jnp.zeros((3 * feat,), BF16), up_bias, jnp.zeros((8 * 128 - hidden,), BF16)]
-    )
-    packed = lines.reshape(16, 128).astype(F32)
+    lines = [ln1_gain, ln1_bias, ln2_gain, ln2_bias, down_bias]
+    places = [(line, index * feat) for index, line in enumerate(lines)] + [(up_bias, 8 * 128)]
+    packed = sum(jnp.pad(line.astype(F32), (at, 16 * 128 - at - line.shape[0])) for line, at in places)
+    packed = packed.reshape(16, 128)
     vm = pl.BlockSpec(memory_space=pltpu.VMEM)
     anywhere = pl.BlockSpec(memory_space=pl.ANY)
     limit = 64 * 1024 * 1024 - 128 * 1024
@@ -1421,10 +1544,7 @@
 
     q_cols, p_cols = qkv_weight.shape[1], pos_weight.shape[1]
     o_rows, d_rows = out_weight.shape[0], down_weight.shape[0]
-    blocks = {
-        "q": (feat, q_cols), "p": (feat, p_cols), "o": (o_rows, 128), "u": (feat, hidden), "d": (d_rows, 128),
-    }
-    names = ("q", "p", "o", "u", "d")
+    qp, part = (256, feat), (d_rows // 2, 128)
     results = pl.pallas_call(
         layer_kernel,
         name="layer",
@@ -1432,10 +1552,12 @@
             shape((micro, 2, feat, count)),
             shape((micro, 2, feat, count)),
         )
-        + tuple(shape(blocks[name], F32) for name in names)
-        + (shape((16, width), F32),),
+        + (
+            shape((2,) + qp, F32), shape((o_rows, 128), F32), shape((feat, hidden), F32), shape((d_rows, 128), F32),
+            shape((16, width), F32),
+        ),
         in_specs=[anywhere, anywhere, vm, vm, vm, vm] + [anywhere] * 6,
-        out_specs=(vm,) * 8,
+        out_specs=(vm,) * 7,
         scratch_shapes=[
             vmem((count, width)),
             vmem((cols, width, 128)),
@@ -1486,24 +1608,32 @@
             vmem((width, count)),
             vmem((width, count)),
             vmem((8, 128), F32),
-            vmem((half, cols) + blocks["q"]),
-            vmem((half, cols) + blocks["p"]),
-            vmem((cols, half) + blocks["o"]),
-            vmem((half, cols) + blocks["u"]),
-            vmem((cols, half) + blocks["d"]),
+            vmem((heads, cols) + qp),
+            vmem((cols, half, o_rows, 128)),
+            vmem((half, cols, feat, hidden)),
+            vmem((rows, cols) + part),
             vmem((cols, half * o_rows, 128)),
             vmem((half, width, hidden)),
-            vmem((cols, half * d_rows, 128)),
-        ]
-        + [vmem((half, 2) + blocks[name]) for name in names]
-        + [vmem((half,) + blocks[name]) for name in names]
-        + [vmem((rows,) + blocks[name]) for name in names]
-        + [
-            vmem((4, 16, width), F32),
+            vmem((rows, cols) + part),
+            vmem((cols,) + part),
+            vmem((heads, 2) + qp),
+            vmem((2, half, o_rows, 128)),
+            vmem((half, 2, feat, hidden)),
+            vmem((2,) + part),
+            vmem((heads,) + qp),
+            vmem((half, o_rows, 128)),
+            vmem((half, feat, hidden)),
+            vmem(part),
+            vmem((2, rows) + qp),
+            vmem((rows, o_rows, 128)),
+            vmem((rows, feat, hidden)),
+            vmem((rows, cols) + part),
             vmem((3, 16, width), F32),
+            vmem((16, width), F32),
+            vmem((cols, 16, width), F32),
             vmem((rows, 16, width), F32),
-            pltpu.SemaphoreType.DMA((280,)),
-            pltpu.SemaphoreType.DMA((280,)),
+            pltpu.SemaphoreType.DMA((126,)),
+            pltpu.SemaphoreType.DMA((117,)),
         ],
         compiler_params=pltpu.CompilerParams(collective_id=0, has_side_effects=True, vmem_limit_bytes=limit),
     )(
@@ -1521,7 +1651,7 @@
             shape((q_cols // 2, feat), F32), bias, bias, shape((p_cols // 2, feat), F32), shape((64, o_rows), F32), vec, vec,
             shape((feat, hidden // 2), F32), shape((1, rows * hidden // devices), F32), shape((64, d_rows), F32), vec,
         ),
-        in_specs=[vm] * 8,
+        in_specs=[vm] * 7,
         out_specs=(vm,) * 15,
         compiler_params=pltpu.CompilerParams(vmem_limit_bytes=limit),
     )(*results))

time: 136 us -> 121 us (0.89)
  the two profiles are of different devices: /device:TPU:0 before, /device:TPU:9 now
where the time goes in v3:
time: 121 us
  Pallas kernels  119 us (98%)
  other arithmetic  1.35 us (1%)
    pallas_call x1, Pallas kernels, fast_shards(): pl.pallas_call(layer_kernel, name='layer', out_shape=(shape((micro, 2, fe...  115 us
    pallas_call x1, Pallas kernels, fast_shards(): pl.pallas_call(final_kernel, name='final', out_shape=(shape(tokens.shape,...  3.34 us

profile of v3, /device:TPU:9, one launch (start us, length us, event | category | flops | bytes accessed | tf_op | source)
XLA Modules:
  0.0 120.7 jit_solution(15311684313582370790)
XLA Ops:
  0.6 1.3 %add_bitcast_fusion.packed = f32[16,128]{1,0:T(8,128)} fusion(bf16[512]{0:T(512)(128)(2,1)} %param.30, bf16[128]{0:T(256)(128)(2,1)} %param.32, bf16[128]{0:T(256)(128)(2,1)} %param.28, bf16[128]{0:T(256)(128)(2,1)} %param.27, bf16[128]{0:T(256)(128)(2,1)} %param.21, bf16[128]{0:T(256)(128)(2,1)} %param.20), kind=kLoop, calls=%fused_computation | loop fusion | flops 22528 | bytes 10496 | tf_op jit(solution)/shard_map/reshape | solution.py:1534
  2.0 115.2 %layer.1 = (bf16[2,2,128,512]{3,2,1,0:T(8,128)(2,1)}, bf16[2,2,128,512]{3,2,1,0:T(8,128)(2,1)}, f32[2,256,128]{2,1,0:T(8,128)}, f32[128,128]{1,0:T(8,128)}, f32[...) custom-call(bf16[2,128,1024]{2,1,0:T(8,128)(2,1)} %tok.1, bf16[2,128,1024]{2,1,0:T(8,128)(2,1)} %cot.1, ...), custom_call_target="tpu_custom_call" | custom-call | tf_op jit(solution)/shard_map/layer/pallas_call | solution.py:1548
  117.2 3.3 %final.1 = (f32[2,128,1024]{2,1,0:T(8,128)}, f32[2,128,1024]{2,1,0:T(8,128)}, f32[1,16]{1,0:T(1,128)}, f32[1,16]{1,0:T(1,128)}, f32[192,128]{1,0:T(8,128)}, /*in...) custom-call(bf16[2,2,128,512]{3,2,1,0:T(8,128)(2,1)} %get-tuple-elem, ...), custom_call_target="tpu_custom_call" | custom-call | tf_op jit(solution)/shard_map/final/pallas_call | solution.py:1646

commit v4 on v3

--- a/solution.py
+++ b/solution.py
@@ -654,11 +654,11 @@
     arrived = io.arrived
     enter(rows)
 
-    def q_block(cc):
-        return wq_half.at[:, pl.ds(aligned(cc * 128, 128), 128), :]
-
-    def p_block(cc):
-        return wp_half.at[:, pl.ds(aligned(cc * 128, 128), 128), :]
+    def q_block(cc, i):
+        return wq_half.at[i, pl.ds(aligned(cc * 128, 128), 128), :]
+
+    def p_block(cc, i):
+        return wp_half.at[i, pl.ds(aligned(cc * 128, 128), 128), :]
 
     def u_block(cc, core=k):
         return wu_all.at[pl.ds(core * half, half), pl.ds(aligned(cc * 128, 128), 128), :]
@@ -667,16 +667,6 @@
         size = wo_all.shape[1] // 2
         return wo_all.at[cc, pl.ds(aligned(core * size, 128), size), :]
 
-    def d_block(cc, core=k):
-        size = wd_all.shape[1] // 2
-        return wd_all.at[cc, pl.ds(aligned(core * size, 128), size), :]
-
-    def q_one(i):
-        return wq_half.at[i, pl.ds(aligned(c * 128, 128), 128), :]
-
-    def p_one(i):
-        return wp_half.at[i, pl.ds(aligned(c * 128, 128), 128), :]
-
     def u_one(i):
         return wu_all.at[k * half + i, pl.ds(aligned(c * 128, 128), 128), :]
 
@@ -684,19 +674,15 @@
         size = wo_all.shape[1] // rows
         return wo_all.at[c, pl.ds(aligned((k * half + i) * size, 128), size), :]
 
-    def d_one(i):
-        size = wd_all.shape[1] // rows
-        return wd_all.at[c, pl.ds(aligned((k * half + i) * size, 128), size), :]
-
     weights = {
-        "q": (wq, q_one, q_block), "p": (wp, p_one, p_block), "o": (wo, o_one, o_block),
-        "u": (wu, u_one, u_block), "d": (wd, d_one, d_block),
+        "q": (wq, lambda i: q_block(c, i), q_block), "p": (wp, lambda i: p_block(c, i), p_block), "o": (wo, o_one, o_block),
+        "u": (wu, u_one, u_block),
     }
     z_slot = {name: io.land(half) for name in weights}
     z_send = {name: io.leave(rows - 1) for name in weights}
-    near_slot = {name: (io.leave(), io.land()) for name in weights}
-    far_slot = {name: (io.leave(2), io.land(2)) for name in weights}
-    sib_slot = {name: (io.leave(), io.land()) for name in ("o", "u", "d")}
+    near_slot = {name: (io.leave(half), io.land(half)) for name in weights}
+    far_slot = {name: (io.leave(2 * half), io.land(2 * half)) for name in weights}
+    sib_slot = {name: (io.leave(), io.land()) for name in ("o", "u")}
     turn = z - k * half
 
     def z_start(name):
@@ -709,36 +695,37 @@
                 lambda: mine,
             )
 
-    def z_done(name):
+    def z_done(name, i=None):
         _, one, _ = weights[name]
-        for i in range(half):
-            arrived(one(i), z_slot[name] + i)
-
-    def near_start(name):
+        for number in range(half) if i is None else (i,):
+            arrived(one(number), z_slot[name] + number)
+
+    def block_of(name, cc, i):
         block = weights[name][2]
-        leave, land = near_slot[name]
-        io.push(leave, lambda: (block(c), block(c), land, (k, z, near)))
-
-    def near_done(name):
-        arrived(weights[name][2](near), near_slot[name][1])
-
-    def far_start(name):
-        block = weights[name][2]
-        leave, land = far_slot[name]
-        io.push(leave, lambda: (block(c), block(c), land, (k, z, far)))
-        io.push(leave + 1, lambda: (block(near), block(near), land + 1, (k, z, far)))
-
-    def far_done(name):
-        block = weights[name][2]
-        arrived(block(far), far_slot[name][1])
-        arrived(block(opposite), far_slot[name][1] + 1)
+        return block(cc) if i is None else block(cc, i)
+
+    def near_start(name, i=None):
+        leave, land = (slot + (i or 0) for slot in near_slot[name])
+        io.push(leave, lambda: (block_of(name, c, i), block_of(name, c, i), land, (k, z, near)))
+
+    def near_done(name, i=None):
+        arrived(block_of(name, near, i), near_slot[name][1] + (i or 0))
+
+    def far_start(name, i=None):
+        leave, land = (slot + 2 * (i or 0) for slot in far_slot[name])
+        io.push(leave, lambda: (block_of(name, c, i), block_of(name, c, i), land, (k, z, far)))
+        io.push(leave + 1, lambda: (block_of(name, near, i), block_of(name, near, i), land + 1, (k, z, far)))
+
+    def far_done(name, i=None):
+        land = far_slot[name][1] + (0 if i is None else 2 * i)
+        arrived(block_of(name, far, i), land)
+        arrived(block_of(name, opposite, i), land + 1)
 
     def core_half(name, core):
         if name == "u":
             return wu_all.at[pl.ds(core * half, half)]
-        full = wo_all if name == "o" else wd_all
-        size = full.shape[1] // 2
-        return full.at[:, pl.ds(aligned(core * size, 128), size), :]
+        size = wo_all.shape[1] // 2
+        return wo_all.at[:, pl.ds(aligned(core * size, 128), size), :]
 
     def sib_start(name):
         leave, land = sib_slot[name]
@@ -747,34 +734,108 @@
     def sib_done(name):
         arrived(core_half(name, 1 - k), sib_slot[name][1])
 
+    part_rows = wd.shape[0] // 2
+
+    def d_cells(zz, core):
+        return wd_all.at[:, pl.ds(aligned((2 * zz + core) * part_rows, 128), part_rows), :]
+
+    def d_cell(cc, core=k):
+        return wd_all.at[cc, pl.ds(aligned((2 * z + core) * part_rows, 128), part_rows), :]
+
+    def d_own():
+        return wd.at[pl.ds(aligned(k * part_rows, 128), part_rows), :]
+
+    d_plane = (io.leave(3), io.land(4))
+    d_line = (io.leave(5), io.land(rows))
+    d_sibs = (io.leave(rows), io.land(rows))
+    relaying = jnp.logical_and(z > 0, z < rows - 1)
+    relayed = 2 * (rows - 1) - (rows - 1) * z
+
+    def wd_start():
+        leave, land = d_plane
+        io.keep(d_own, lambda: d_cell(c), land)
+        io.push(leave, lambda: (d_own(), d_cell(c), land + 1, (k, z, near)))
+        io.push(leave + 1, lambda: (d_own(), d_cell(c), land + 2, (k, z, far)))
+
+    def wd_far():
+        leave, land = d_plane
+        arrived(d_cell(near), land + 1)
+        io.push(leave + 2, lambda: (d_cell(near), d_cell(near), land + 3, (k, z, far)))
+
+    def wd_sib(number):
+        zz = lax.rem(z + number, rows)
+        leave, land = d_sibs
+        io.push(leave + number, lambda: (d_cells(lax.rem(z + number, rows), k),) * 2 + (land + lax.rem(z + number, rows), sibling))
+
+    def wd_line():
+        land = d_plane[1]
+        arrived(d_cell(c), land)
+        arrived(d_cell(far), land + 2)
+        arrived(d_cell(opposite), land + 3)
+        leave, land = d_line
+        for number, step in enumerate((2, -2, 1, -1)):
+            io.push(
+                leave + number,
+                lambda step=step: (d_cells(z, k), d_cells(z, k), land + z, (k, lax.rem(z + step + rows, rows), c)),
+                lambda step=step: jnp.logical_and(z + step >= 0, z + step < rows),
+            )
+        wd_sib(0)
+
+    def wd_relay():
+        leave, land = d_line
+
+        @pl.when(relaying)
+        def _():
+            arrived(d_cells(relayed, k), land + relayed)
+
+        io.push(
+            leave + 4,
+            lambda: (d_cells(relayed, k), d_cells(relayed, k), land + relayed, (k, rows - 1 - relayed, c)),
+            lambda: relaying,
+        )
+
+    def wd_done(number):
+        zz = lax.rem(z + number, rows)
+
+        @pl.when(jnp.logical_not(jnp.logical_and(relaying, zz == relayed)))
+        def _():
+            arrived(d_cells(zz, k), d_line[1] + zz)
+
+        wd_sib(number)
+
+    def wd_all_done():
+        for number in range(rows):
+            zz = lax.rem(z + number, rows)
+            arrived(d_cells(zz, 1 - k), d_sibs[1] + zz)
+
     feat = tok.shape[1]
+    count = xt.shape[1]
     x_slot = io.land(4)
     x_send = io.leave(4)
-    xf_slot = io.land(4)
-    xf_send = io.leave(4)
-
-    def x_part(cc, core):
-        return xt.at[pl.ds(aligned(cc * feat + core * (feat // 2), 64), feat // 2), :]
+    n_slot, n_send = io.land(), io.leave()
 
     def is_local(b, core):
         return jnp.logical_and(2 * b + k == c, core == k)
 
+    def spread_features(source, target, leave, land):
+        for b in range(2):
+            for core in range(2):
+
+                def src(b=b, core=core):
+                    return source.at[b, :, pl.ds(core * count, count)]
+
+                def dst():
+                    return target.at[pl.ds(aligned(c * feat, 128), feat), :]
+
+                io.keep(src, dst, land + c, lambda b=b, core=core: is_local(b, core))
+                io.push(
+                    leave + 2 * b + core,
+                    lambda src=src, dst=dst, b=b, core=core: (src(), dst(), land + c, (0 * k + core, z, 2 * b + k)),
+                    lambda b=b, core=core: jnp.logical_not(is_local(b, core)),
+                )
+
     z_start("q")
-    for b in range(2):
-        for core in range(2):
-
-            def src(b=b, core=core):
-                return tok.at[b, pl.ds(core * (feat // 2), feat // 2), :]
-
-            def dst(core=core):
-                return x_part(c, core)
-
-            io.keep(src, dst, x_slot + c, lambda b=b, core=core: is_local(b, core))
-            io.push(
-                x_send + 2 * b + core,
-                lambda src=src, dst=dst, b=b, core=core: (src(), dst(), x_slot + c, (0 * k + core, z, 2 * b + k)),
-                lambda b=b, core=core: jnp.logical_not(is_local(b, core)),
-            )
+    spread_features(tok, xt, x_send, x_slot)
     z_start("p")
 
     t_slot = io.land()
@@ -810,78 +871,65 @@
                 lambda b=b, core=core: (starts, starts_got, s_slot, (0 * k + core, z, 2 * b + k)),
                 lambda b=b, core=core: jnp.logical_and(c == z, jnp.logical_not(is_local(b, core))),
             )
-    for name in ("o", "u", "d"):
+    for name in ("o", "u"):
         z_start(name)
 
     c_slot = io.land(4)
     c_send = io.leave(4)
-    count = ct.shape[1]
-
-    def cot_start():
-        for b in range(2):
-            for core in range(2):
-
-                def src(b=b, core=core):
-                    return cot.at[b, :, pl.ds(core * count, count)]
-
-                def dst():
-                    return ct.at[pl.ds(aligned(c * feat, 128), feat), :]
-
-                io.keep(src, dst, c_slot + c, lambda b=b, core=core: is_local(b, core))
-                io.push(
-                    c_send + 2 * b + core,
-                    lambda src=src, dst=dst, b=b, core=core: (src(), dst(), c_slot + c, (0 * k + core, z, 2 * b + k)),
-                    lambda b=b, core=core: jnp.logical_not(is_local(b, core)),
-                )
-
-    z_done("q")
-    near_start("q")
-    for cc in range(4):
-        arrived(x_part(cc, k), x_slot + cc)
-        io.push(xf_send + cc, lambda cc=cc: (x_part(cc, k), x_part(cc, k), xf_slot + cc, sibling))
-    z_done("p")
-    near_start("p")
+    z_done("q", 0)
+    near_start("q", 0)
+    z_done("p", 0)
+    near_start("p", 0)
+    wd_start()
     arrived(params_col, g_col)
     arrived(params_row, g_row)
     arrived(cb_all, g_cb)
     arrived(pb_all, g_pb)
     arrived(starts_got, s_slot)
+    near_done("q", 0)
+    far_start("q", 0)
     for cc in range(4):
-        arrived(x_part(cc, 1 - k), xf_slot + cc)
-    near_done("q")
-    far_start("q")
+        arrived(xt.at[pl.ds(cc * feat, feat), :], x_slot + cc)
 
     columns = [tall(params_col[cc]) for cc in range(4)]
     gain = jnp.concatenate([col[:, 0:1] for col in columns], axis=0)
     bias = jnp.concatenate([col[:, 1:2] for col in columns], axis=0)
     width = xt.shape[0]
-    seq = xt.shape[1]
+    seq = normed_t.shape[1]
     piece = PIECE
     blocks = seq // 256
-
-    @pl.loop(0, blocks)
+    other = pl.ds(aligned((1 - k) * count, count), count)
+    own = pl.ds(aligned(k * count, count), count)
+
+    @pl.loop(0, count // 256)
     def _(t):
-        here = pl.ds(aligned(t * 256, 256), 256)
-        x = xt[:, here].astype(F32)
+        x = xt[:, pl.ds(aligned(t * 256, 256), 256)].astype(F32)
         mean = jnp.sum(x, axis=0, keepdims=True) * (1.0 / width)
         square = jnp.sum(x * x, axis=0, keepdims=True) * (1.0 / width)
         inverse = lax.rsqrt(square - mean * mean + norm_epsilon)
+        here = pl.ds(aligned(k * count + t * 256, 256), 256)
         normed_t[:, here] = ((x - mean) * inverse * gain + bias).astype(BF16)
 
-    near_done("p")
-    far_start("p")
+    io.push(n_send, lambda: (normed_t.at[:, own], normed_t.at[:, own], n_slot, sibling))
+    near_done("p", 0)
+    far_start("p", 0)
+    wd_far()
+    for name in ("q", "p"):
+        z_done(name, 1)
+        near_start(name, 1)
     z_done("o")
     near_start("o")
-    z_done("u")
-    near_start("u")
-    cot_start()
-    far_done("q")
+    arrived(kcat.at[:, pl.ds(0, 512)], t_slot)
     scale = 0.125
     none = jnp.zeros((256, 64), F32)
 
-    @pl.loop(0, half * blocks)
-    def _(n):
-        i, t = lax.div(n, blocks), lax.rem(n, blocks)
+    def project(i, number):
+        t = lax.rem(k * (blocks // 2) + number, blocks)
+
+        @pl.when(jnp.logical_and(i == 0, number == blocks // 2))
+        def _():
+            arrived(normed_t.at[:, other], n_slot)
+
         here = pl.ds(aligned(t * 256, 256), 256)
         got = tn(normed_t[:, here], wq_half[i])
         for hb in range(2):
@@ -896,19 +944,8 @@
             keys[h, here, :] = jnp.concatenate([key, none], axis=1).astype(BF16)
             vals[h, here, :] = value.astype(BF16)
 
-    near_done("o")
-    far_start("o")
-    z_done("d")
-    near_start("d")
-    far_done("p")
-    arrived(kcat.at[:, pl.ds(0, 512)], t_slot)
-    for h in range(heads):
-        part = wp_half[h // 2, :, (h % 2) * 64 : (h % 2) * 64 + 64]
-        wp_head[h] = jnp.concatenate([jnp.zeros_like(part), part], axis=1)
-
-    @pl.loop(0, heads * blocks)
-    def _(n):
-        h, t = lax.div(n, blocks), lax.rem(n, blocks)
+    def rotate(i, n):
+        h, t = 2 * i + lax.div(n, blocks), lax.rem(n, blocks)
         here = pl.ds(aligned(t * 256, 256), 256)
         angle = nt(qcat[h, here, 512:640], wp_head[h])
         cosine = kcat[here, 0:256].astype(F32)
@@ -916,9 +953,6 @@
         first, second = angle[:, 0:256], angle[:, 256:512]
         qcat[h, here, 0:256] = (first * sine + second * cosine).astype(BF16)
         qcat[h, here, 256:512] = (second * sine - first * cosine).astype(BF16)
-
-    near_done("u")
-    far_start("u")
 
     slot_len = seq // 2
     block = 256
@@ -949,10 +983,6 @@
         probs[h, pl.ds(aligned(low_row, block), block), :] = low
         heads_out[h, here, :] = nn(low, vals[h, 0:keys_seen, :]).astype(BF16)
 
-    def far_d():
-        near_done("d")
-        far_start("d")
-
     def sib_o():
         far_done("o")
         sib_start("o")
@@ -966,10 +996,27 @@
             if (number % 4) // 2 == slot:
                 pl.when(4 * h + 2 * slot + t == number)(action)
 
-    ahead = {6: far_d, 7: sib_o, 12: sib_u}
-
-    @pl.loop(0, heads)
-    def _(h):
+    def far_of(name):
+        def run():
+            near_done(name)
+            far_start(name)
+
+        return run
+
+    def projected():
+        z_done("u")
+        near_start("u")
+        wd_line()
+
+    def rotated():
+        for name in ("q", "p"):
+            near_done(name, 1)
+            far_start(name, 1)
+        spread_features(cot, ct, c_send, c_slot)
+
+    ahead = {1: far_of("o"), 4: far_of("u"), 9: wd_relay, 11: sib_o, 15: sib_u}
+
+    def one_head(h):
         kcat[:, 512:640] = keys[h]
 
         @pl.loop(0, slot_len // block)
@@ -982,11 +1029,22 @@
             attend(h, t * block, seq, 1)
             ticks(h, 1, t, ahead)
 
+    @pl.loop(0, half)
+    def _(i):
+        far_done("q", i)
+        pl.loop(0, blocks)(lambda number: project(i, number))
+        pl.when(i == 0)(projected)
+        far_done("p", i)
+        for hb in range(2):
+            part = wp_half[i, :, hb * 64 : hb * 64 + 64]
+            wp_head[2 * i + hb] = jnp.concatenate([jnp.zeros_like(part), part], axis=1)
+        pl.loop(0, 2 * blocks)(lambda n: rotate(i, n))
+        pl.when(i == 0)(rotated)
+        pl.loop(0, 2)(lambda hb: one_head(2 * i + hb))
+
     own_att[...] = jnp.concatenate([heads_out[h] for h in range(heads)], axis=1)
     a_slot, a_send = io.land(2), io.leave()
     span = own_att.shape[1]
-    other = pl.ds(aligned((1 - k) * count, count), count)
-    own = pl.ds(aligned(k * count, count), count)
     att_part = att.at[:, pl.ds(aligned(k * span, 128), span)]
     io.push(a_send, lambda: (own_att.at[other, :], att_part, a_slot, sibling))
     io.keep(lambda: own_att.at[own, :], lambda: att_part, a_slot + 1)
@@ -997,8 +1055,8 @@
     arrived(own_att.at[own, :], a_slot + 1)
     arrived(own_att.at[own, :], a_slot)
 
-    far_done("d")
-    sib_start("d")
+    for number in range(1, rows):
+        wd_done(number)
 
     def line(index):
         return jnp.concatenate([params_col[cc, index : index + 1, :] for cc in range(cols)], axis=1)
@@ -1006,7 +1064,7 @@
     def out_weight():
         return jnp.concatenate([wo_all[cc] for cc in range(cols)], axis=1)
 
-    x = jnp.transpose(xt[:, own].astype(F32))
+    x = jnp.transpose(xt[...].astype(F32))
     middle = x + nn(att[...], out_weight())
     mid[...] = middle
     mean = jnp.sum(middle, axis=1, keepdims=True) * (1.0 / width)
@@ -1022,8 +1080,8 @@
     acc_two[...] = jnp.zeros_like(acc_two)
     small[...] = jnp.zeros_like(small)
     hidden = wu_all.shape[2]
-
-    part_rows = wd_all.shape[1] // rows // 2
+    wd_all_done()
+
     u0_slot = (io.leave(half), io.land(half))
     o0_slot = (io.leave(), io.land())
     d0_slot = (io.leave(rows), io.land(rows))
@@ -1280,8 +1338,7 @@
 
         @pl.when(step == 1)
         def _():
-            for name in ("u", "d"):
-                sib_done(name)
+            sib_done("u")
 
         here = pl.ds(aligned(r * hidden, hidden), hidden)
         bias = jnp.concatenate([params_row[r, j : j + 1, :] for j in range(hidden // 128)], axis=1)
@@ -1406,11 +1463,12 @@
     io.push(f_send, lambda: (one_low, one_got, f_slot, sibling))
     qp_two(2)
     qp_z(1)
+    d_one()
     arrived(one_got, f_slot)
     columns = [tall(params_col[cc]) for cc in range(cols)]
     gain = jnp.concatenate([col[:, 0:1] for col in columns], axis=0)
     one = one_t[:, own] + one_got[...].astype(F32)
-    x = xt[:, own].astype(F32)
+    x = xt[...].astype(F32)
     mean = jnp.sum(x, axis=0, keepdims=True) * (1.0 / width)
     square = jnp.sum(x * x, axis=0, keepdims=True) * (1.0 / width)
     inverse = lax.rsqrt(square - mean * mean + norm_epsilon)
@@ -1445,9 +1503,9 @@
             p_send + step - 1, lambda step=step: (all_small.at[1], got_plane.at[c], p_slot, (k, z, lax.rem(c + step, 4)))
         )
     io.keep(lambda: all_small.at[1], lambda: got_plane.at[c], p_slot)
+    qp_two(3)
+    d_two()
     back_start(grad_x, grads, grad_slot)
-    qp_two(3)
-    d_one()
     qp_z(2)
     arrived(got_plane, p_slot)
     all_small[2] = (got_plane[0] + got_plane[1]) + (got_plane[2] + got_plane[3])
@@ -1458,7 +1516,6 @@
     io.keep(lambda: all_small.at[2], lambda: got_z.at[z], v_slot)
     u_last()
     o_last()
-    d_two()
     qp_z(3)
     d_last()
     arrived(got_z, v_slot)
@@ -1566,7 +1623,7 @@
             vmem((half, width, q_cols)),
             vmem((half, width, p_cols)),
             vmem((heads, width, 128)),
-            vmem((width, seq)),
+            vmem((width, count)),
             vmem((width, count)),
             vmem((width, seq)),
             vmem((heads, seq, width + 128)),
@@ -1632,8 +1689,8 @@
             vmem((16, width), F32),
             vmem((cols, 16, width), F32),
             vmem((rows, 16, width), F32),
-            pltpu.SemaphoreType.DMA((126,)),
-            pltpu.SemaphoreType.DMA((117,)),
+            pltpu.SemaphoreType.DMA((140,)),
+            pltpu.SemaphoreType.DMA((132,)),
         ],
         compiler_params=pltpu.CompilerParams(collective_id=0, has_side_effects=True, vmem_limit_bytes=limit),
     )(

time: 121 us -> 112 us (0.926)
  the two profiles are of different devices: /device:TPU:9 before, /device:TPU:0 now
where the time goes in v4:
time: 112 us
  Pallas kernels  110 us (98%)
  other arithmetic  1.35 us (1%)
    pallas_call x1, Pallas kernels, fast_shards(): pl.pallas_call(layer_kernel, name='layer', out_shape=(shape((micro, 2, fe...  107 us
    pallas_call x1, Pallas kernels, fast_shards(): pl.pallas_call(final_kernel, name='final', out_shape=(shape(tokens.shape,...  3.22 us

profile of v4, /device:TPU:0, one launch (start us, length us, event | category | flops | bytes accessed | tf_op | source)
XLA Modules:
  0.0 112.2 jit_solution(908351249010218936)
XLA Ops:
  0.6 1.3 %add_bitcast_fusion.packed = f32[16,128]{1,0:T(8,128)} fusion(bf16[512]{0:T(512)(128)(2,1)} %param.30, bf16[128]{0:T(256)(128)(2,1)} %param.32, bf16[128]{0:T(256)(128)(2,1)} %param.28, bf16[128]{0:T(256)(128)(2,1)} %param.27, bf16[128]{0:T(256)(128)(2,1)} %param.21, bf16[128]{0:T(256)(128)(2,1)} %param.20), kind=kLoop, calls=%fused_computation | loop fusion | flops 22528 | bytes 10496 | tf_op jit(solution)/shard_map/reshape | solution.py:1591
  2.0 106.8 %layer.1 = (bf16[2,2,128,512]{3,2,1,0:T(8,128)(2,1)}, bf16[2,2,128,512]{3,2,1,0:T(8,128)(2,1)}, f32[2,256,128]{2,1,0:T(8,128)}, f32[128,128]{1,0:T(8,128)}, f32[...) custom-call(bf16[2,128,1024]{2,1,0:T(8,128)(2,1)} %tok.1, bf16[2,128,1024]{2,1,0:T(8,128)(2,1)} %cot.1, ...), custom_call_target="tpu_custom_call" | custom-call | tf_op jit(solution)/shard_map/layer/pallas_call | solution.py:1605
  108.8 3.2 %final.1 = (f32[2,128,1024]{2,1,0:T(8,128)}, f32[2,128,1024]{2,1,0:T(8,128)}, f32[1,16]{1,0:T(1,128)}, f32[1,16]{1,0:T(1,128)}, f32[192,128]{1,0:T(8,128)}, /*in...) custom-call(bf16[2,2,128,512]{3,2,1,0:T(8,128)(2,1)} %get-tuple-elem, ...), custom_call_target="tpu_custom_call" | custom-call | tf_op jit(solution)/shard_map/final/pallas_call | solution.py:1703

commit v5 on v4

--- a/solution.py
+++ b/solution.py
@@ -993,7 +993,7 @@
 
     def ticks(h, slot, t, actions):
         for number, action in actions.items():
-            if (number % 4) // 2 == slot:
+            if (number % 4) // 2 == slot and (not isinstance(t, int) or number % 2 == t):
                 pl.when(4 * h + 2 * slot + t == number)(action)
 
     def far_of(name):
@@ -1004,14 +1004,9 @@
         return run
 
     def projected():
-        z_done("u")
-        near_start("u")
         wd_line()
 
     def rotated():
-        for name in ("q", "p"):
-            near_done(name, 1)
-            far_start(name, 1)
         spread_features(cot, ct, c_send, c_slot)
 
     ahead = {1: far_of("o"), 4: far_of("u"), 9: wd_relay, 11: sib_o, 15: sib_u}
@@ -1019,15 +1014,20 @@
     def one_head(h):
         kcat[:, 512:640] = keys[h]
 
-        @pl.loop(0, slot_len // block)
-        def _(t):
+        for t in range(slot_len // block):
             attend(h, t * block, slot_len, 0)
+        for t in range(slot_len // block):
             ticks(h, 0, t, ahead)
-
-        @pl.loop(0, slot_len // block)
-        def _(t):
+        for t in range(slot_len // block):
             attend(h, t * block, seq, 1)
+        for t in range(slot_len // block):
             ticks(h, 1, t, ahead)
+
+    for name in ("q", "p"):
+        near_done(name, 1)
+        far_start(name, 1)
+    z_done("u")
+    near_start("u")
 
     @pl.loop(0, half)
     def _(i):
@@ -1438,14 +1438,13 @@
         turned_v[...] = jnp.zeros_like(turned_v)
         turned_p[h] = jnp.zeros(turned_p.shape[1:], F32)
 
-        @pl.loop(0, slot_len // block)
-        def _(t):
+        for t in range(slot_len // block):
             attend_back(h, t * block, slot_len, 0)
+        for t in range(slot_len // block):
             ticks(h, 0, t, behind)
-
-        @pl.loop(0, slot_len // block)
-        def _(t):
+        for t in range(slot_len // block):
             attend_back(h, t * block, seq, 1)
+        for t in range(slot_len // block):
             ticks(h, 1, t, behind)
 
         turned[h, 64:128, :] = turned_k[...].astype(BF16)
@@ -1614,7 +1613,7 @@
             shape((16, width), F32),
         ),
         in_specs=[anywhere, anywhere, vm, vm, vm, vm] + [anywhere] * 6,
-        out_specs=(vm,) * 7,
+        out_specs=(anywhere, anywhere) + (vm,) * 5,
         scratch_shapes=[
             vmem((count, width)),
             vmem((cols, width, 128)),

time: 112 us -> 108 us (0.964)
  Pallas kernels: 110 us -> 105 us
    pallas_call x1, Pallas kernels: 107 us -> 102 us  [fast_shards(): pl.pallas_call(layer_kernel, name='layer', out_shape=(shape((micro, 2, fe...]
where the time goes in v5:
time: 108 us; the launch traced here: 107 us
  Pallas kernels  105 us (97%)
  other arithmetic  1.35 us (1%)
    pallas_call x1, Pallas kernels, fast_shards(): pl.pallas_call(layer_kernel, name='layer', out_shape=(shape((micro, 2, fe...  102 us
    pallas_call x1, Pallas kernels, fast_shards(): pl.pallas_call(final_kernel, name='final', out_shape=(shape(tokens.shape,...  3.22 us

profile of v5, /device:TPU:0, one launch (start us, length us, event | category | flops | bytes accessed | tf_op | source)
XLA Modules:
  0.0 107.5 jit_solution(7699794528109352510)
XLA Ops:
  0.6 1.3 %add_bitcast_fusion.packed = f32[16,128]{1,0:T(8,128)} fusion(bf16[512]{0:T(512)(128)(2,1)} %param.30, bf16[128]{0:T(256)(128)(2,1)} %param.32, bf16[128]{0:T(256)(128)(2,1)} %param.28, bf16[128]{0:T(256)(128)(2,1)} %param.27, bf16[128]{0:T(256)(128)(2,1)} %param.21, bf16[128]{0:T(256)(128)(2,1)} %param.20), kind=kLoop, calls=%fused_computation | loop fusion | flops 22528 | bytes 10496 | tf_op jit(solution)/shard_map/reshape | solution.py:1590
  2.0 102.1 %layer.1 = (bf16[2,2,128,512]{3,2,1,0:T(8,128)(2,1)}, bf16[2,2,128,512]{3,2,1,0:T(8,128)(2,1)}, f32[2,256,128]{2,1,0:T(8,128)}, f32[128,128]{1,0:T(8,128)}, f32[...) custom-call(bf16[2,128,1024]{2,1,0:T(8,128)(2,1)} %tok.1, bf16[2,128,1024]{2,1,0:T(8,128)(2,1)} %cot.1, ...), custom_call_target="tpu_custom_call" | custom-call | tf_op jit(solution)/shard_map/layer/pallas_call | solution.py:1604
  104.1 3.2 %final.1 = (f32[2,128,1024]{2,1,0:T(8,128)}, f32[2,128,1024]{2,1,0:T(8,128)}, f32[1,16]{1,0:T(1,128)}, f32[1,16]{1,0:T(1,128)}, f32[192,128]{1,0:T(8,128)}, /*in...) custom-call(bf16[2,2,128,512]{3,2,1,0:T(8,128)(2,1)} %get-tuple-elem, ...), custom_call_target="tpu_custom_call" | custom-call | tf_op jit(solution)/shard_map/final/pallas_call | solution.py:1702

commit v6 on v5

--- a/solution.py
+++ b/solution.py
@@ -634,7 +634,7 @@
 def layer_kernel(
     tok, cot, starts, packed, cbias, pbias, table, wq, wp, wo, wu, wd,
     outs, grads, f_qp, f_o, f_u, f_d, f_small,
-    att, wo_all, wu_all, wd_all, wq_half, wp_half, wp_head, xt, ct, normed_t, qcat, keys, vals, probs_a, probs_b, heads_out,
+    att, wo_all, wu_all, wd_all, wq_half, wp_half, wp_head, xt, ct, normed_t, qcat, keys, vals, probs_a, probs_b, heads_out, inverse_sum,
     params_col, params_row, cb_all, pb_all, kcat, own_att, starts_got,
     mid, norm, hat, inv, gout, acc_out, acc_two, tall_norm, out_t, grad_mid_t, grad_att, g_up, g_down, g_out, small,
     grad_o, head_grad, turned, turned_k, turned_v, turned_p, one_t, one_low, one_got, grad_x, sums,
@@ -975,13 +975,14 @@
         if slot == 1:
             first = jnp.exp(scores[:, :slot_len] - top)
             total = total + jnp.sum(first, axis=1, keepdims=True)
-            whole = jnp.concatenate([first, last], axis=1)
+            low = jnp.concatenate([first.astype(BF16), last.astype(BF16)], axis=1)
         else:
-            whole = last
-        low = (whole * (1.0 / total)).astype(BF16)
+            low = last.astype(BF16)
+        inverse = 1.0 / total
         probs = (probs_a, probs_b)[slot]
         probs[h, pl.ds(aligned(low_row, block), block), :] = low
-        heads_out[h, here, :] = nn(low, vals[h, 0:keys_seen, :]).astype(BF16)
+        inverse_sum[h, here, :] = inverse
+        heads_out[h, here, :] = (nn(low, vals[h, 0:keys_seen, :]) * inverse).astype(BF16)
 
     def sib_o():
         far_done("o")
@@ -1401,7 +1402,7 @@
     def attend_back(h, low_row, keys_seen, slot):
         at = pl.ds(aligned(low_row, block), block)
         here = pl.ds(aligned(slot * slot_len + low_row, block), block)
-        grad = head_grad[h, here, :]
+        grad = (head_grad[h, here, :].astype(F32) * inverse_sum[h, here, :]).astype(BF16)
         low = (probs_a, probs_b)[slot][h, at, :]
         inner = jnp.sum(grad.astype(F32) * heads_out[h, here, :].astype(F32), axis=1, keepdims=True)
         grad_prob = nt(grad, vals[h, 0:keys_seen, :])
@@ -1427,8 +1428,8 @@
         return run
 
     behind = {
-        0: both(o_one, lambda: u_two(0)), 6: lambda: u_two(1), 7: o_two, 9: lambda: u_z(0), 10: lambda: qp_two(0),
-        11: lambda: u_z(1), 12: o_z, 13: lambda: qp_two(1), 14: lambda: qp_z(0),
+        0: both(o_one, lambda: u_two(0)), 6: lambda: u_two(1), 8: both(o_two, lambda: u_z(0)), 10: lambda: qp_two(0),
+        11: lambda: u_z(1), 13: both(o_z, lambda: qp_two(1)), 15: lambda: qp_z(0),
     }
 
     @pl.loop(0, heads)
@@ -1631,6 +1632,7 @@
             vmem((heads, count, count)),
             vmem((heads, count, seq)),
             vmem((heads, seq, 64)),
+            vmem((heads, seq, 1), F32),
             vmem((cols, 8, 128), F32),
             vmem((rows, 8, 128), F32),
             vmem((rows,) + content_bias.shape, F32),

time: 108 us -> 107 us (level)
    pallas_call x1, Pallas kernels: 102 us -> 101 us  [fast_shards(): pl.pallas_call(layer_kernel, name='layer', out_shape=(shape((micro, 2, fe...]
where the time goes in v6:
time: 107 us; the launch traced here: 106 us
  Pallas kernels  104 us (97%)
  other arithmetic  1.35 us (1%)
    pallas_call x1, Pallas kernels, fast_shards(): pl.pallas_call(layer_kernel, name='layer', out_shape=(shape((micro, 2, fe...  101 us
    pallas_call x1, Pallas kernels, fast_shards(): pl.pallas_call(final_kernel, name='final', out_shape=(shape(tokens.shape,...  3.22 us

profile of v6, /device:TPU:0, one launch (start us, length us, event | category | flops | bytes accessed | tf_op | source)
XLA Modules:
  0.0 106.2 jit_solution(10584117235950833274)
XLA Ops:
  0.6 1.3 %add_bitcast_fusion.packed = f32[16,128]{1,0:T(8,128)} fusion(bf16[512]{0:T(512)(128)(2,1)} %param.30, bf16[128]{0:T(256)(128)(2,1)} %param.32, bf16[128]{0:T(256)(128)(2,1)} %param.28, bf16[128]{0:T(256)(128)(2,1)} %param.27, bf16[128]{0:T(256)(128)(2,1)} %param.21, bf16[128]{0:T(256)(128)(2,1)} %param.20), kind=kLoop, calls=%fused_computation | loop fusion | flops 22528 | bytes 10496 | tf_op jit(solution)/shard_map/reshape | solution.py:1591
  2.0 100.8 %layer.1 = (bf16[2,2,128,512]{3,2,1,0:T(8,128)(2,1)}, bf16[2,2,128,512]{3,2,1,0:T(8,128)(2,1)}, f32[2,256,128]{2,1,0:T(8,128)}, f32[128,128]{1,0:T(8,128)}, f32[...) custom-call(bf16[2,128,1024]{2,1,0:T(8,128)(2,1)} %tok.1, bf16[2,128,1024]{2,1,0:T(8,128)(2,1)} %cot.1, ...), custom_call_target="tpu_custom_call" | custom-call | tf_op jit(solution)/shard_map/layer/pallas_call | solution.py:1605
  102.8 3.2 %final.1 = (f32[2,128,1024]{2,1,0:T(8,128)}, f32[2,128,1024]{2,1,0:T(8,128)}, f32[1,16]{1,0:T(1,128)}, f32[1,16]{1,0:T(1,128)}, f32[192,128]{1,0:T(8,128)}, /*in...) custom-call(bf16[2,2,128,512]{3,2,1,0:T(8,128)(2,1)} %get-tuple-elem, ...), custom_call_target="tpu_custom_call" | custom-call | tf_op jit(solution)/shard_map/final/pallas_call | solution.py:1704
